TPU v7x, 256 devices: a whole 4x4x8 slice. The times are simulated.
256 devices in a mesh: freq: 32 (over z_hi, x, core), beam: 8 (over y, z_lo).
Axes of the slice: x: 4, y: 4, z: 8 (z_hi: 4, z_lo: 2; z = z_hi * 2 + z_lo), core: 2. Of those that a mesh axis runs over, the one named last changes fastest.
Arguments:
- voltages: bfloat16 [2, 16, 1024, 16, 256], P(None, 'beam', 'freq'), parts along dimension 1, may hold values from -6 to 6
- sub_delays: int32 [8192, 512], P('freq'), may hold values from 0 to 31, as said below
- merge_tables: int32 [5, 3, 8192], P(None, None, 'freq'), may hold values from 0 to 255, as said below
Outputs:
- peak_values: float32 [16, 8, 8192], P('beam', None, 'freq'), parts along dimension 0
There are 8 independent parts, one for each index of `beam`. A program takes and returns all parts, laid end to end along the dimension named above; an argument that names none is the same for every part. Nothing has to cross between parts.
Inputs may be any that keep to these rules, and one draw needn't show every extreme that they name: `sub_delays`: every row has some channel with delay 32 - 1. `merge_tables`: for each level and each aligned block of 256 trials, rows 0 and 1 each hold a permutation of 0 to 255; row 2 holds delays of 0 to 63, and each such block has a delay of 63.
All inputs are finite; a program needn't handle non-finite values.
Results may differ from a plain program's by a relative error of at most 0.0003.
Values may be sent and summed in bfloat16 or wider, within the bound.
No kernel may reach another device: no remote copies, remote signals or barrier semaphores. Data moves between devices by JAX's collectives and lax.ppermute only.
A program may use at most 128 MiB of HBM per device.

v0:
```python
import functools
import math

import jax
import jax.numpy as jnp
import numpy as np
from jax import lax
from jax.experimental import pallas as pl
from jax.experimental.pallas import tpu as pltpu
from jax.sharding import PartitionSpec as P

TAPS = 4
WIDTHS = 8
SHIFTS = 32
INNER = 4

epsilon = 1e-06
f32 = jnp.float32
bf16 = jnp.bfloat16


def filter_matrix(upchan):
    length = TAPS * upchan
    n = np.arange(length, dtype=np.float64)
    window = np.sinc((n - (length - 1) / 2) / upchan) * (0.5 - 0.5 * np.cos(2 * np.pi * (n + 0.5) / length))
    window = (window / np.sqrt(2 * np.sum(window * window))).reshape(TAPS, upchan)
    phase = np.arange(upchan)
    angle = 2 * np.pi * (phase[:, None] * phase[None, :]) / upchan
    cosine, sine = np.cos(angle), np.sin(angle)
    transform = np.block([[cosine, sine], [-sine, cosine]])
    full = np.concatenate([transform * np.tile(window[tap], 2)[None, :] for tap in range(TAPS)], axis=1)
    pieces, rest = [], full
    for _ in range(3):
        piece = rest.astype(jnp.bfloat16)
        pieces.append(piece)
        rest = rest - piece.astype(np.float64)
    return np.concatenate(pieces, axis=0)


def shifted(x, amount):
    lane = lax.broadcasted_iota(jnp.int32, x.shape, 1)
    return jnp.where(lane >= amount, pltpu.roll(x, amount, 1), 0.0)


def filter_kernel(matrix_ref, volts_ref, out_ref):
    _, beams, count, upchan, samples = volts_ref.shape
    matrix = matrix_ref[...]
    rows = 2 * upchan
    for beam in range(beams):
        for q in range(count):
            x = volts_ref[:, beam, q].astype(f32).reshape(rows, samples)
            taps = [x] + [shifted(x, tap) for tap in range(1, TAPS)]
            stacked = jnp.concatenate(taps, axis=0).astype(bf16)
            y = jnp.dot(matrix, stacked, preferred_element_type=f32)
            y = y[:rows] + (y[rows : 2 * rows] + y[2 * rows :])
            power = y[:upchan] * y[:upchan] + y[upchan:] * y[upchan:]
            out_ref[q // 2, beam, q % 2] = power.astype(bf16)


def filter_power(voltages):
    parts, beams, coarse, upchan, samples = voltages.shape
    step = 8
    matrix = jnp.asarray(filter_matrix(upchan))
    return pl.pallas_call(
        filter_kernel,
        grid=(coarse // step,),
        out_shape=jax.ShapeDtypeStruct((coarse // 2, beams, 2, upchan, samples), bf16),
        in_specs=[
            pl.BlockSpec(matrix.shape, lambda i: (0, 0)),
            pl.BlockSpec((parts, beams, step, upchan, samples), lambda i: (0, 0, i, 0, 0)),
        ],
        out_specs=pl.BlockSpec((step // 2, beams, 2, upchan, samples), lambda i: (i, 0, 0, 0, 0)),
        name="filter_power",
    )(matrix, voltages)


def put_split(split_ref, slot, x):
    samples = x.shape[1]
    high = x.astype(bf16)
    split_ref[slot, :, :samples] = high
    split_ref[slot, :, samples:] = (x - high.astype(f32)).astype(bf16)


def table_columns(table, level):
    trials = table.shape[1]
    row = lax.broadcasted_iota(jnp.int32, (trials, trials), 0)
    lane = lax.broadcasted_iota(jnp.int32, (trials, trials), 1)
    eye = jnp.where(row == lane, 1.0, 0.0).astype(bf16)
    columns = lax.dot_general(eye, table.astype(bf16), (((1,), (1,)), ((), ())), preferred_element_type=f32)
    return columns[:, 3 * level : 3 * level + 3].astype(jnp.int32)


def take_rows(split, source):
    trials = split.shape[0]
    samples = split.shape[1] // 2
    lane = lax.broadcasted_iota(jnp.int32, (trials, trials), 1)
    onehot = jnp.where(lane == source, 1.0, 0.0).astype(bf16)
    y = jnp.dot(onehot, split, preferred_element_type=f32)
    return y[:, :samples] + y[:, samples:]


def delay_rows(x, delay):
    trials, samples = x.shape
    half = samples // 2
    lane = lax.broadcasted_iota(jnp.int32, (trials, half), 1)
    index = (lane - delay) & (half - 1)
    inside = lane >= delay
    first = jnp.take_along_axis(x[:, :half], index, axis=1)
    second = jnp.take_along_axis(x[:, half:], index, axis=1)
    return jnp.concatenate([jnp.where(inside, first, 0.0), jnp.where(inside, second, first)], axis=1)


def merge_unit(split_ref, table, level):
    columns = table_columns(table, level)
    lower = take_rows(split_ref[0], columns[:, 0:1])
    upper = take_rows(split_ref[1], columns[:, 1:2])
    return lower + delay_rows(upper, columns[:, 2:3])


def dedisperse_kernel(bits_ref, arrived_ref, delays_ref, tables_ref, kept_ref, sent_ref, stack_ref, split_ref, table_ref):
    sources, _, upchan, samples = arrived_ref.shape
    trials = delays_ref.shape[1]
    channels = sources * upchan
    core = bits_ref[0]
    for which in range(2):
        unit = core if which == 0 else 1 - core
        x = arrived_ref[:, pl.ds(unit, 1)].reshape(channels, samples).astype(f32)
        for inner in range(INNER):
            moved = x if inner == 0 else shifted(x, inner)
            stack_ref[inner * channels : (inner + 1) * channels] = moved.astype(bf16)
        delays = delays_ref[which]
        total = jnp.zeros((trials, samples), f32)
        for outer in reversed(range(SHIFTS // INNER)):
            onehot = jnp.concatenate(
                [
                    jnp.where(delays == jnp.asarray(outer * INNER + inner, bf16), jnp.asarray(1, bf16), jnp.asarray(0, bf16))
                    for inner in range(INNER)
                ],
                axis=1,
            )
            if outer != SHIFTS // INNER - 1:
                total = shifted(total, INNER)
            total = total + jnp.dot(onehot, stack_ref[...], preferred_element_type=f32)
        put_split(split_ref, unit, total)
        table_ref[unit] = tables_ref[which]
    emit(bits_ref[1], split_ref, table_ref, 0, kept_ref, sent_ref)


def emit(keep, split_ref, table_ref, level, kept_ref, sent_ref):
    trials = split_ref.shape[1]
    for out_ref, unit in ((sent_ref, 1 - keep), (kept_ref, keep)):
        table = table_ref[unit]
        out_ref[:trials] = merge_unit(split_ref, table, level)
        out_ref[trials:] = table


def merge_kernel(level, bits_ref, kept_in_ref, received_ref, kept_ref, sent_ref, split_ref, table_ref):
    load_units(bits_ref[level], kept_in_ref, received_ref, split_ref, table_ref)
    emit(bits_ref[level + 1], split_ref, table_ref, level, kept_ref, sent_ref)


def load_units(own, kept_in_ref, received_ref, split_ref, table_ref):
    trials = split_ref.shape[1]
    for in_ref, unit in ((kept_in_ref, own), (received_ref, 1 - own)):
        put_split(split_ref, unit, in_ref[:trials])
        table_ref[unit] = in_ref[trials:]


def peaks_kernel(level, bits_ref, kept_in_ref, received_ref, out_ref, split_ref, table_ref):
    load_units(bits_ref[level], kept_in_ref, received_ref, split_ref, table_ref)
    for slot in range(2):
        unit = bits_ref[0] if slot == 0 else 1 - bits_ref[0]
        merged = merge_unit(split_ref, table_ref[unit], level)
        series = merged.T
        samples = series.shape[0]
        mean = jnp.sum(series, axis=0, keepdims=True) * (1.0 / samples)
        centred = series - mean
        variance = jnp.sum(centred * centred, axis=0, keepdims=True) * (1.0 / samples)
        boxcar = centred * lax.rsqrt(variance + epsilon)
        peaks = [jnp.max(boxcar, axis=0, keepdims=True)]
        width = 1
        for _ in range(1, WIDTHS):
            row = lax.broadcasted_iota(jnp.int32, boxcar.shape, 0)
            boxcar = boxcar + jnp.where(row >= width, pltpu.roll(boxcar, width, 0), 0.0)
            width *= 2
            peaks.append(jnp.max(boxcar, axis=0, keepdims=True) * (1.0 / math.sqrt(width)))
        out_ref[slot] = jnp.concatenate(peaks, axis=0)


VMEM = pl.BlockSpec(memory_space=pltpu.VMEM)
SMEM = pl.BlockSpec(memory_space=pltpu.SMEM)


def unit_scratch(trials, samples, table_rows):
    return [pltpu.VMEM((2, trials, 2 * samples), bf16), pltpu.VMEM((2, table_rows, samples), f32)]


def swap(x, bit):
    return lax.ppermute(x, "freq", [(i, i ^ (1 << bit)) for i in range(lax.axis_size("freq"))])


def local(voltages, sub_delays, merge_tables):
    freq_count = lax.axis_size("freq")
    levels = freq_count.bit_length() - 1
    trials, channels = sub_delays.shape
    samples = voltages.shape[4]
    upchan = voltages.shape[3]
    position = lax.axis_index("freq")
    bits = (position >> jnp.arange(8, dtype=jnp.int32)) & 1

    power = filter_power(voltages)
    power = power.reshape(freq_count, 2, upchan, samples)
    arrived = lax.all_to_all(power, "freq", split_axis=0, concat_axis=0, tiled=True)

    delays = sub_delays.astype(bf16)
    delays = jnp.stack([delays, swap(delays, 0)])
    tables = merge_tables.reshape(3 * levels, trials).astype(f32)
    tables = jnp.pad(tables, ((0, -3 * levels % 8), (0, 0)))
    tables = jnp.stack([tables, swap(tables, 0)])
    table_rows = tables.shape[1]

    message = jax.ShapeDtypeStruct((trials + table_rows, samples), f32)
    scratch = unit_scratch(trials, samples, table_rows)
    kept, sent = pl.pallas_call(
        dedisperse_kernel,
        out_shape=(message, message),
        in_specs=[SMEM, VMEM, VMEM, VMEM],
        out_specs=(VMEM, VMEM),
        scratch_shapes=[pltpu.VMEM((INNER * channels, samples), bf16)] + scratch,
        name="dedisperse",
    )(bits, arrived, delays, tables)
    for level in range(1, levels):
        received = swap(sent, level)
        if level < levels - 1:
            kept, sent = pl.pallas_call(
                functools.partial(merge_kernel, level),
                out_shape=(message, message),
                in_specs=[SMEM, VMEM, VMEM],
                out_specs=(VMEM, VMEM),
                scratch_shapes=scratch,
                name="merge",
            )(bits, kept, received)
    peaks = pl.pallas_call(
        functools.partial(peaks_kernel, levels - 1),
        out_shape=jax.ShapeDtypeStruct((2, WIDTHS, trials), f32),
        in_specs=[SMEM, VMEM, VMEM],
        out_specs=VMEM,
        scratch_shapes=scratch,
        name="peaks",
    )(bits, kept, received)
    half = freq_count // 2
    first = lax.ppermute(peaks[0], "freq", [(d, (d & 1) * half + (d >> 1)) for d in range(freq_count)])
    second = lax.ppermute(peaks[1], "freq", [(d, (1 - (d & 1)) * half + (d >> 1)) for d in range(freq_count)])
    top = bits[levels - 1] == 1
    return jnp.stack([jnp.where(top, second, first), jnp.where(top, first, second)])


def solution(mesh):
    return jax.shard_map(
        local,
        mesh=mesh,
        in_specs=(P(None, "beam", "freq", None, None), P("freq", None), P(None, None, "freq")),
        out_specs=P("beam", None, "freq"),
        check_vma=False,
    )
```

profile of v0, /device:TPU:12, one launch (start us, length us, event | category | flops | bytes accessed | tf_op | source)
XLA Modules:
  0.0 120.9 jit_solution(13652581135492723750)
XLA Ops:
  0.0 4.1 %filter_power.1 = bf16[16,2,2,16,256]{4,3,2,1,0:T(8,128)(2,1)} custom-call(bf16[96,128]{1,0:T(8,128)(2,1)} %constant.16.clone.matrix_ref, bf16[2,2,32,16,256]{4,3,2,1,0:T(8,128)(2,1)} %volts_ref.1), custom_call_target="tpu_custom_call" | custom-call | tf_op jit(solution)/shard_map/filter_power/pallas_call | solution.py:64
  4.1 11.7 %all-to-all-start = ((bf16[32,2,16,256]{3,2,1,0:T(8,128)(2,1)}), bf16[32,2,16,256]{3,2,1,0:T(8,128)(2,1)S(1)}, u32[]{:S(2)}, u32[]{:S(2)}) async-start(bf16[32,2,16,256]{3,2,1,0:T(8,128)(2,1)} %bitcast.16), calls=%async_computation | async-start | bytes 1048576 | tf_op jit(solution)/shard_map/all_to_all | solution.py:213
  15.9 0.2 collective-permute-start.1
  16.1 0.5 collective-permute-start
  16.7 0.5 shift-right-arithmetic_and_fusion.bits_ref
  17.2 0.6 pad_maximum_fusion.1.tables_ref
  17.8 0.9 pad_maximum_fusion.delays_ref
  18.7 14.4 %all-to-all-done.arrived_ref = bf16[32,2,16,256]{3,2,1,0:T(8,128)(2,1)S(1)} async-done(((bf16[32,2,16,256]{3,2,1,0:T(8,128)(2,1)}), bf16[32,2,16,256]{3,2,1,0:T(8,128)(2,1)S(1)}, u32[]{:S(2)}, u32[]{:S(2)}) %all-to-all-start) | async-done | bytes 524320 | tf_op jit(solution)/shard_map/all_to_all | solution.py:213
  33.1 0.8 copy-done.1
  33.9 7.4 %dedisperse.1 = (f32[272,256]{1,0:T(8,128)}, f32[272,256]{1,0:T(8,128)}) custom-call(s32[8]{0:T(128)} %shift-right-arithmetic_and_fusion.bits_ref, bf16[32,2,16,256]{3,2,1,0:T(8,128)(2,1)} %copy-done.1, bf16[2,256,512]{2,1,0:T(8,128)(2,1)} %pad_maximum_fusion.delays_ref, f32[2,16,256]{2,1,0:T(8,128)} %pad_maximum_fusion.1.tables_ref), custom_call_target="tpu_custom_call" | custom-call | tf_op jit(solution)/shard_map/dedisperse/pallas_call | solution.py:224
  41.3 1.2 collective-permute-start.2
  42.5 7.0 %collective-permute-done.2.received_ref = f32[272,256]{1,0:T(8,128)S(1)} collective-permute-done((f32[272,256]{1,0:T(8,128)}, f32[272,256]{1,0:T(8,128)S(1)}, u32[]{:S(2)}, u32[]{:S(2)}) %collective-permute-start.2) | collective-permute-done | bytes 278560 | tf_op jit(solution)/shard_map/ppermute | solution.py:199
  49.5 0.7 copy-done.2
  50.2 2.9 %merge.3 = (f32[272,256]{1,0:T(8,128)}, f32[272,256]{1,0:T(8,128)}) custom-call(s32[8]{0:T(128)} %shift-right-arithmetic_and_fusion.bits_ref, f32[272,256]{1,0:T(8,128)} %get-tuple-element.13.kept_in_ref, f32[272,256]{1,0:T(8,128)} %copy-done.2), custom_call_target="tpu_custom_call" | custom-call | tf_op jit(solution)/shard_map/merge/pallas_call | solution.py:235
  53.2 1.5 %collective-permute-start.3 = (f32[272,256]{1,0:T(8,128)}, f32[272,256]{1,0:T(8,128)S(1)}, u32[]{:S(2)}, u32[]{:S(2)}) collective-permute-start(f32[272,256]{1,0:T(8,128)} %get-tuple-element.16), channel_id=1, source_target_pairs={{0,32},{8,40},{16,48},{24,56},{32,0},{40,8},{48,16},{56,24},{64,96... | collective-permute-start | bytes 835592 | tf_op jit(solution)/shard_map/ppermute | solution.py:199
  54.7 7.4 %collective-permute-done.3.received_ref = f32[272,256]{1,0:T(8,128)S(1)} collective-permute-done((f32[272,256]{1,0:T(8,128)}, f32[272,256]{1,0:T(8,128)S(1)}, u32[]{:S(2)}, u32[]{:S(2)}) %collective-permute-start.3) | collective-permute-done | bytes 278560 | tf_op jit(solution)/shard_map/ppermute | solution.py:199
  62.1 0.7 copy-done.3
  62.8 2.9 %merge.4 = (f32[272,256]{1,0:T(8,128)}, f32[272,256]{1,0:T(8,128)}) custom-call(s32[8]{0:T(128)} %shift-right-arithmetic_and_fusion.bits_ref, f32[272,256]{1,0:T(8,128)} %get-tuple-element.15.kept_in_ref, f32[272,256]{1,0:T(8,128)} %copy-done.3), custom_call_target="tpu_custom_call" | custom-call | tf_op jit(solution)/shard_map/merge/pallas_call | solution.py:235
  65.7 1.8 %collective-permute-start.4 = (f32[272,256]{1,0:T(8,128)}, f32[272,256]{1,0:T(8,128)S(1)}, u32[]{:S(2)}, u32[]{:S(2)}) collective-permute-start(f32[272,256]{1,0:T(8,128)} %get-tuple-element.18), channel_id=1, source_target_pairs={{0,64},{8,72},{16,80},{24,88},{32,96},{40,104},{48,112},{56,120},{... | collective-permute-start | bytes 835592 | tf_op jit(solution)/shard_map/ppermute | solution.py:199
  67.5 12.2 %collective-permute-done.4.received_ref = f32[272,256]{1,0:T(8,128)S(1)} collective-permute-done((f32[272,256]{1,0:T(8,128)}, f32[272,256]{1,0:T(8,128)S(1)}, u32[]{:S(2)}, u32[]{:S(2)}) %collective-permute-start.4) | collective-permute-done | bytes 278560 | tf_op jit(solution)/shard_map/ppermute | solution.py:199
  79.7 0.7 copy-done.4
  80.5 2.9 %merge.5 = (f32[272,256]{1,0:T(8,128)}, f32[272,256]{1,0:T(8,128)}) custom-call(s32[8]{0:T(128)} %shift-right-arithmetic_and_fusion.bits_ref, f32[272,256]{1,0:T(8,128)} %get-tuple-element.17.kept_in_ref, f32[272,256]{1,0:T(8,128)} %copy-done.4), custom_call_target="tpu_custom_call" | custom-call | tf_op jit(solution)/shard_map/merge/pallas_call | solution.py:235
  83.4 2.7 %collective-permute-start.5 = (f32[272,256]{1,0:T(8,128)}, f32[272,256]{1,0:T(8,128)S(1)}, u32[]{:S(2)}, u32[]{:S(2)}) collective-permute-start(f32[272,256]{1,0:T(8,128)} %get-tuple-element.20), channel_id=1, source_target_pairs={{0,128},{8,136},{16,144},{24,152},{32,160},{40,168},{48,176},{56,1... | collective-permute-start | bytes 835592 | tf_op jit(solution)/shard_map/ppermute | solution.py:199
  86.1 15.2 %collective-permute-done.5.received_ref = f32[272,256]{1,0:T(8,128)S(1)} collective-permute-done((f32[272,256]{1,0:T(8,128)}, f32[272,256]{1,0:T(8,128)S(1)}, u32[]{:S(2)}, u32[]{:S(2)}) %collective-permute-start.5) | collective-permute-done | bytes 278560 | tf_op jit(solution)/shard_map/ppermute | solution.py:199
  101.2 0.7 copy-done.5
  102.0 3.4 %peaks.1 = f32[2,8,256]{2,1,0:T(8,128)} custom-call(s32[8]{0:T(128)} %shift-right-arithmetic_and_fusion.bits_ref, f32[272,256]{1,0:T(8,128)} %get-tuple-element.19.kept_in_ref, f32[272,256]{1,0:T(8,128)} %copy-done.5), custom_call_target="tpu_custom_call" | custom-call | tf_op jit(solution)/shard_map/peaks/pallas_call | solution.py:243
  105.3 0.7 slice_bitcast_fusion.1
  106.0 5.5 %collective-permute-start.6 = (f32[8,256]{1,0:T(8,128)S(1)}, f32[8,256]{1,0:T(8,128)S(1)}, u32[]{:S(2)}, u32[]{:S(2)}) collective-permute-start(f32[8,256]{1,0:T(8,128)S(1)} %get-tuple-element.23), channel_id=1, source_target_pairs={{0,128},{8,0},{16,136},{24,8},{32,144},{40,16},{48,152},{56,24},{6... | collective-permute-start | bytes 24584 | tf_op jit(solution)/shard_map/ppermute | solution.py:253
  111.5 2.2 %collective-permute-start.7 = (f32[8,256]{1,0:T(8,128)S(1)}, f32[8,256]{1,0:T(8,128)S(1)}, u32[]{:S(2)}, u32[]{:S(2)}) collective-permute-start(f32[8,256]{1,0:T(8,128)S(1)} %get-tuple-element.24), channel_id=1, source_target_pairs={{0,0},{8,128},{16,8},{24,136},{32,16},{40,144},{48,24},{56,152},{6... | collective-permute-start | bytes 24584 | tf_op jit(solution)/shard_map/ppermute | solution.py:252
  113.8 0.6 slice.9
  115.0 5.3 %collective-permute-done.7 = f32[8,256]{1,0:T(8,128)S(1)} collective-permute-done((f32[8,256]{1,0:T(8,128)S(1)}, f32[8,256]{1,0:T(8,128)S(1)}, u32[]{:S(2)}, u32[]{:S(2)}) %collective-permute-start.7) | collective-permute-done | bytes 8224 | tf_op jit(solution)/shard_map/ppermute | solution.py:252
  120.3 0.6 pad_maximum_fusion.2
  (20 shorter events, 0.1 us)
Async XLA Ops:
  4.1 11.7 %copy-start.6 = (s32[5,3,256]{2,1,0:T(4,128)S(1)}, s32[5,3,256]{2,1,0:T(4,128)}, u32[]{:S(2)}) copy-start(s32[5,3,256]{2,1,0:T(4,128)} %param.6) | copy-start | bytes 46084
  4.1 12.0 %copy-start = (s32[256,512]{1,0:T(8,128)S(1)}, s32[256,512]{1,0:T(8,128)}, u32[]{:S(2)}) copy-start(s32[256,512]{1,0:T(8,128)} %param.5) | copy-start | bytes 1572868
  4.1 29.0 %all-to-all-start = ((bf16[32,2,16,256]{3,2,1,0:T(8,128)(2,1)}), bf16[32,2,16,256]{3,2,1,0:T(8,128)(2,1)S(1)}, u32[]{:S(2)}, u32[]{:S(2)}) async-start(bf16[32,2,16,256]{3,2,1,0:T(8,128)(2,1)} %bitcast.16), calls=%async_computation | async-start | bytes 1048576 | tf_op jit(solution)/shard_map/all_to_all | solution.py:213
  15.9 1.3 %collective-permute-start.1 = (f32[16,256]{1,0:T(8,128)S(1)}, f32[16,256]{1,0:T(8,128)S(1)}, u32[]{:S(2)}, u32[]{:S(2)}) collective-permute-start(f32[16,256]{1,0:T(8,128)S(1)} %get-tuple-element.26), channel_id=1, source_target_pairs={{0,8},{8,0},{16,24},{24,16},{32,40},{40,32},{48,56},{56,48},{64,72... | collective-permute-start | bytes 49160 | tf_op jit(solution)/shard_map/ppermute | solution.py:199
  16.1 1.6 %collective-permute-start = (bf16[256,512]{1,0:T(8,128)(2,1)S(1)}, bf16[256,512]{1,0:T(8,128)(2,1)S(1)}, u32[]{:S(2)}, u32[]{:S(2)}) collective-permute-start(bf16[256,512]{1,0:T(8,128)(2,1)S(1)} %convert_element_type.11), channel_id=1, source_target_pairs={{0,8},{8,0},{16,24},{24,16},{32,40},{40,32},{48,56},{56,48},{64,72... | collective-permute-start | bytes 786440 | tf_op jit(solution)/shard_map/ppermute | solution.py:199
  33.1 0.8 copy-start.1
  41.3 8.2 %collective-permute-start.2 = (f32[272,256]{1,0:T(8,128)}, f32[272,256]{1,0:T(8,128)S(1)}, u32[]{:S(2)}, u32[]{:S(2)}) collective-permute-start(f32[272,256]{1,0:T(8,128)} %get-tuple-element.14), channel_id=1, source_target_pairs={{0,16},{8,24},{16,0},{24,8},{32,48},{40,56},{48,32},{56,40},{64,80... | collective-permute-start | bytes 835592 | tf_op jit(solution)/shard_map/ppermute | solution.py:199
  49.5 0.7 copy-start.2
  53.2 8.9 %collective-permute-start.3 = (f32[272,256]{1,0:T(8,128)}, f32[272,256]{1,0:T(8,128)S(1)}, u32[]{:S(2)}, u32[]{:S(2)}) collective-permute-start(f32[272,256]{1,0:T(8,128)} %get-tuple-element.16), channel_id=1, source_target_pairs={{0,32},{8,40},{16,48},{24,56},{32,0},{40,8},{48,16},{56,24},{64,96... | collective-permute-start | bytes 835592 | tf_op jit(solution)/shard_map/ppermute | solution.py:199
  62.0 0.7 copy-start.3
  65.7 14.1 %collective-permute-start.4 = (f32[272,256]{1,0:T(8,128)}, f32[272,256]{1,0:T(8,128)S(1)}, u32[]{:S(2)}, u32[]{:S(2)}) collective-permute-start(f32[272,256]{1,0:T(8,128)} %get-tuple-element.18), channel_id=1, source_target_pairs={{0,64},{8,72},{16,80},{24,88},{32,96},{40,104},{48,112},{56,120},{... | collective-permute-start | bytes 835592 | tf_op jit(solution)/shard_map/ppermute | solution.py:199
  79.7 0.7 copy-start.4
  83.4 17.8 %collective-permute-start.5 = (f32[272,256]{1,0:T(8,128)}, f32[272,256]{1,0:T(8,128)S(1)}, u32[]{:S(2)}, u32[]{:S(2)}) collective-permute-start(f32[272,256]{1,0:T(8,128)} %get-tuple-element.20), channel_id=1, source_target_pairs={{0,128},{8,136},{16,144},{24,152},{32,160},{40,168},{48,176},{56,1... | collective-permute-start | bytes 835592 | tf_op jit(solution)/shard_map/ppermute | solution.py:199
  101.2 0.7 copy-start.5
  106.0 7.7 %copy-start.7 = (s32[8]{0:T(128)S(1)}, s32[8]{0:T(128)}, u32[]{:S(2)}) copy-start(s32[8]{0:T(128)} %shift-right-arithmetic_and_fusion.bits_ref) | copy-start | bytes 100
  106.0 9.0 %collective-permute-start.6 = (f32[8,256]{1,0:T(8,128)S(1)}, f32[8,256]{1,0:T(8,128)S(1)}, u32[]{:S(2)}, u32[]{:S(2)}) collective-permute-start(f32[8,256]{1,0:T(8,128)S(1)} %get-tuple-element.23), channel_id=1, source_target_pairs={{0,128},{8,0},{16,136},{24,8},{32,144},{40,16},{48,152},{56,24},{6... | collective-permute-start | bytes 24584 | tf_op jit(solution)/shard_map/ppermute | solution.py:253
  111.5 8.8 %collective-permute-start.7 = (f32[8,256]{1,0:T(8,128)S(1)}, f32[8,256]{1,0:T(8,128)S(1)}, u32[]{:S(2)}, u32[]{:S(2)}) collective-permute-start(f32[8,256]{1,0:T(8,128)S(1)} %get-tuple-element.24), channel_id=1, source_target_pairs={{0,0},{8,128},{16,8},{24,136},{32,16},{40,144},{48,24},{56,152},{6... | collective-permute-start | bytes 24584 | tf_op jit(solution)/shard_map/ppermute | solution.py:252
where the time goes:
time: 121 us
  waiting for transfers between devices  61.6 us (51%)
  starting transfers between devices  27.3 us (23%)
  Pallas kernels  23.7 us (20%)
  local copies, waits for them, and re-layouts  4.96 us (4%)
  other arithmetic  2.65 us (2%)
    ppermute x6, waiting for transfers between devices, swap(): lax.ppermute(x, 'freq', [(i, i ^ 1 << bit) for i in range(lax.axis_size('...  41.8 us
    all_to_all x1, waiting for transfers between devices, local(): lax.all_to_all(power, 'freq', split_axis=0, concat_axis=0, tiled=True)  14.4 us
    all_to_all x1, starting transfers between devices, local(): lax.all_to_all(power, 'freq', split_axis=0, concat_axis=0, tiled=True)  11.7 us
    pallas_call x3, Pallas kernels, local(): pl.pallas_call(functools.partial(merge_kernel, level), out_shape=(message...  8.8 us
    ppermute x6, starting transfers between devices, swap(): lax.ppermute(x, 'freq', [(i, i ^ 1 << bit) for i in range(lax.axis_size('...  7.88 us
    pallas_call x1, Pallas kernels, local(): pl.pallas_call(dedisperse_kernel, out_shape=(message, message), in_specs=...  7.42 us
    ppermute x1, starting transfers between devices, local(): lax.ppermute(peaks[1], 'freq', [(d, (1 - (d & 1)) * half + (d >> 1)) for...  5.48 us
    ppermute x1, waiting for transfers between devices, local(): lax.ppermute(peaks[0], 'freq', [(d, (d & 1) * half + (d >> 1)) for d in r...  5.33 us
  transfers between devices with their start and end apart: 9, of which 6 were waited for; matrix products, arithmetic and copies ran while one was open for 2% of the time, Pallas kernels for 0%

commit v1 on v0

--- a/solution.py
+++ b/solution.py
@@ -70,24 +70,25 @@
             pl.BlockSpec((parts, beams, step, upchan, samples), lambda i: (0, 0, i, 0, 0)),
         ],
         out_specs=pl.BlockSpec((step // 2, beams, 2, upchan, samples), lambda i: (i, 0, 0, 0, 0)),
+        compiler_params=pltpu.CompilerParams(vmem_limit_bytes=8 << 20),
         name="filter_power",
     )(matrix, voltages)
 
 
-def put_split(split_ref, slot, x):
-    samples = x.shape[1]
+def split_of(x):
     high = x.astype(bf16)
-    split_ref[slot, :, :samples] = high
-    split_ref[slot, :, samples:] = (x - high.astype(f32)).astype(bf16)
-
-
-def table_columns(table, level):
-    trials = table.shape[1]
-    row = lax.broadcasted_iota(jnp.int32, (trials, trials), 0)
-    lane = lax.broadcasted_iota(jnp.int32, (trials, trials), 1)
-    eye = jnp.where(row == lane, 1.0, 0.0).astype(bf16)
+    return jnp.concatenate([high, (x - high.astype(f32)).astype(bf16)], axis=1)
+
+
+def eye_mask(size):
+    row = lax.broadcasted_iota(jnp.int32, (size, size), 0)
+    return row == lax.broadcasted_iota(jnp.int32, (size, size), 1)
+
+
+def columns_of(table):
+    eye = jnp.where(eye_mask(table.shape[1]), 1.0, 0.0).astype(bf16)
     columns = lax.dot_general(eye, table.astype(bf16), (((1,), (1,)), ((), ())), preferred_element_type=f32)
-    return columns[:, 3 * level : 3 * level + 3].astype(jnp.int32)
+    return columns.astype(jnp.int32)
 
 
 def take_rows(split, source):
@@ -111,13 +112,37 @@
 
 
 def merge_unit(split_ref, table, level):
-    columns = table_columns(table, level)
-    lower = take_rows(split_ref[0], columns[:, 0:1])
-    upper = take_rows(split_ref[1], columns[:, 1:2])
-    return lower + delay_rows(upper, columns[:, 2:3])
-
-
-def dedisperse_kernel(bits_ref, arrived_ref, delays_ref, tables_ref, kept_ref, sent_ref, stack_ref, split_ref, table_ref):
+    columns = columns_of(table)
+    lower = take_rows(split_ref[0], columns[:, 3 * level : 3 * level + 1])
+    upper = take_rows(split_ref[1], columns[:, 3 * level + 1 : 3 * level + 2])
+    return lower + delay_rows(upper, columns[:, 3 * level + 2 : 3 * level + 3])
+
+
+STEPS = 65534.0
+
+
+def put_message(out_ref, x, table):
+    trials = x.shape[0]
+    peak = jnp.maximum(jnp.max(x, axis=1, keepdims=True), 1e-30)
+    code = jnp.floor(jnp.log2(peak) * 256.0) + 2.0
+    scale = jnp.exp2(code * (-1.0 / 256.0)) * STEPS
+    out_ref[:trials] = ((x * scale + 0.5).astype(jnp.int32) - int(STEPS) // 2).astype(jnp.int16)
+    code_row = jnp.sum(jnp.where(eye_mask(trials), code, 0.0), axis=0, keepdims=True).astype(jnp.int32)
+    row = lax.broadcasted_iota(jnp.int32, table.shape, 0)
+    rows = jnp.where(row == 0, code_row >> 8, jnp.where(row == 1, code_row & 255, table.astype(jnp.int32)))
+    out_ref[trials:] = rows.astype(jnp.int16)
+
+
+def take_message(in_ref, trials):
+    table = in_ref[trials:].astype(jnp.int32).astype(f32)
+    columns = columns_of(table)
+    code = (columns[:, 0:1] * 256 + columns[:, 1:2]).astype(f32)
+    scale = jnp.exp2(code * (1.0 / 256.0)) * (1.0 / STEPS)
+    x = (in_ref[:trials].astype(jnp.int32) + int(STEPS) // 2).astype(f32) * scale
+    return x, table
+
+
+def dedisperse_kernel(bits_ref, arrived_ref, delays_ref, tables_ref, sent_ref, split_ref, table_ref, stack_ref):
     sources, _, upchan, samples = arrived_ref.shape
     trials = delays_ref.shape[1]
     channels = sources * upchan
@@ -141,35 +166,38 @@
             if outer != SHIFTS // INNER - 1:
                 total = shifted(total, INNER)
             total = total + jnp.dot(onehot, stack_ref[...], preferred_element_type=f32)
-        put_split(split_ref, unit, total)
+        split_ref[unit] = split_of(total)
         table_ref[unit] = tables_ref[which]
-    emit(bits_ref[1], split_ref, table_ref, 0, kept_ref, sent_ref)
-
-
-def emit(keep, split_ref, table_ref, level, kept_ref, sent_ref):
-    trials = split_ref.shape[1]
-    for out_ref, unit in ((sent_ref, 1 - keep), (kept_ref, keep)):
-        table = table_ref[unit]
-        out_ref[:trials] = merge_unit(split_ref, table, level)
-        out_ref[trials:] = table
-
-
-def merge_kernel(level, bits_ref, kept_in_ref, received_ref, kept_ref, sent_ref, split_ref, table_ref):
-    load_units(bits_ref[level], kept_in_ref, received_ref, split_ref, table_ref)
-    emit(bits_ref[level + 1], split_ref, table_ref, level, kept_ref, sent_ref)
-
-
-def load_units(own, kept_in_ref, received_ref, split_ref, table_ref):
-    trials = split_ref.shape[1]
-    for in_ref, unit in ((kept_in_ref, own), (received_ref, 1 - own)):
-        put_split(split_ref, unit, in_ref[:trials])
-        table_ref[unit] = in_ref[trials:]
-
-
-def peaks_kernel(level, bits_ref, kept_in_ref, received_ref, out_ref, split_ref, table_ref):
-    load_units(bits_ref[level], kept_in_ref, received_ref, split_ref, table_ref)
-    for slot in range(2):
-        unit = bits_ref[0] if slot == 0 else 1 - bits_ref[0]
+    put_sent(0, bits_ref, split_ref, table_ref, sent_ref)
+
+
+def put_sent(level, bits_ref, split_ref, table_ref, sent_ref):
+    table = table_ref[1 - bits_ref[level + 1]]
+    put_message(sent_ref, merge_unit(split_ref, table, level), table)
+
+
+def kept_kernel(level, bits_ref, split_in_ref, table_in_ref, split_ref, table_ref):
+    table = table_in_ref[bits_ref[level + 1]]
+    split_ref[...] = split_of(merge_unit(split_in_ref, table, level))
+    table_ref[...] = table
+
+
+def load_units(own, kept_split_ref, kept_table_ref, received_ref, split_ref, table_ref):
+    split_ref[own] = kept_split_ref[...]
+    table_ref[own] = kept_table_ref[...]
+    x, table = take_message(received_ref, kept_split_ref.shape[0])
+    split_ref[1 - own] = split_of(x)
+    table_ref[1 - own] = table
+
+
+def sent_kernel(level, bits_ref, kept_split_ref, kept_table_ref, received_ref, sent_ref, split_ref, table_ref):
+    load_units(bits_ref[level], kept_split_ref, kept_table_ref, received_ref, split_ref, table_ref)
+    put_sent(level, bits_ref, split_ref, table_ref, sent_ref)
+
+
+def peaks_kernel(level, bits_ref, kept_split_ref, kept_table_ref, received_ref, first_ref, second_ref, split_ref, table_ref):
+    load_units(bits_ref[level], kept_split_ref, kept_table_ref, received_ref, split_ref, table_ref)
+    for out_ref, unit in ((first_ref, bits_ref[0]), (second_ref, 1 - bits_ref[0])):
         merged = merge_unit(split_ref, table_ref[unit], level)
         series = merged.T
         samples = series.shape[0]
@@ -184,15 +212,28 @@
             boxcar = boxcar + jnp.where(row >= width, pltpu.roll(boxcar, width, 0), 0.0)
             width *= 2
             peaks.append(jnp.max(boxcar, axis=0, keepdims=True) * (1.0 / math.sqrt(width)))
-        out_ref[slot] = jnp.concatenate(peaks, axis=0)
+        out_ref[...] = jnp.concatenate(peaks, axis=0)
+
+
+def join_kernel(level, bits_ref, first_ref, second_ref, out_ref):
+    out_ref[bits_ref[level]] = first_ref[...]
+    out_ref[1 - bits_ref[level]] = second_ref[...]
 
 
 VMEM = pl.BlockSpec(memory_space=pltpu.VMEM)
 SMEM = pl.BlockSpec(memory_space=pltpu.SMEM)
 
 
-def unit_scratch(trials, samples, table_rows):
-    return [pltpu.VMEM((2, trials, 2 * samples), bf16), pltpu.VMEM((2, table_rows, samples), f32)]
+def call(kernel, name, outs, operands, scratch=(), mebibytes=8):
+    return pl.pallas_call(
+        kernel,
+        out_shape=tuple(jax.ShapeDtypeStruct(shape, dtype) for shape, dtype in outs),
+        in_specs=[SMEM] + [VMEM] * (len(operands) - 1),
+        out_specs=tuple(VMEM for _ in outs),
+        scratch_shapes=list(scratch),
+        compiler_params=pltpu.CompilerParams(vmem_limit_bytes=mebibytes << 20),
+        name=name,
+    )(*operands)
 
 
 def swap(x, bit):
@@ -215,44 +256,35 @@
     delays = sub_delays.astype(bf16)
     delays = jnp.stack([delays, swap(delays, 0)])
     tables = merge_tables.reshape(3 * levels, trials).astype(f32)
-    tables = jnp.pad(tables, ((0, -3 * levels % 8), (0, 0)))
+    tables = jnp.pad(tables, ((0, -3 * levels % 16), (0, 0)))
     tables = jnp.stack([tables, swap(tables, 0)])
-    table_rows = tables.shape[1]
-
-    message = jax.ShapeDtypeStruct((trials + table_rows, samples), f32)
-    scratch = unit_scratch(trials, samples, table_rows)
-    kept, sent = pl.pallas_call(
-        dedisperse_kernel,
-        out_shape=(message, message),
-        in_specs=[SMEM, VMEM, VMEM, VMEM],
-        out_specs=(VMEM, VMEM),
-        scratch_shapes=[pltpu.VMEM((INNER * channels, samples), bf16)] + scratch,
-        name="dedisperse",
-    )(bits, arrived, delays, tables)
-    for level in range(1, levels):
-        received = swap(sent, level)
-        if level < levels - 1:
-            kept, sent = pl.pallas_call(
-                functools.partial(merge_kernel, level),
-                out_shape=(message, message),
-                in_specs=[SMEM, VMEM, VMEM],
-                out_specs=(VMEM, VMEM),
-                scratch_shapes=scratch,
-                name="merge",
-            )(bits, kept, received)
-    peaks = pl.pallas_call(
-        functools.partial(peaks_kernel, levels - 1),
-        out_shape=jax.ShapeDtypeStruct((2, WIDTHS, trials), f32),
-        in_specs=[SMEM, VMEM, VMEM],
-        out_specs=VMEM,
-        scratch_shapes=scratch,
-        name="peaks",
-    )(bits, kept, received)
+    rows = tables.shape[1]
+
+    message = ((trials + rows, samples), jnp.int16)
+    splits, both_tables = ((2, trials, 2 * samples), bf16), ((2, rows, samples), f32)
+    split, table = ((trials, 2 * samples), bf16), ((rows, samples), f32)
+    stack = pltpu.VMEM((INNER * channels, samples), bf16)
+    sent, *both = call(
+        dedisperse_kernel, "dedisperse", (message, splits, both_tables), (bits, arrived, delays, tables), [stack], 24
+    )
+    for level in range(levels - 1):
+        received = swap(sent, level + 1)
+        kept = call(functools.partial(kept_kernel, level), "kept", (split, table), (bits, *both))
+        if level < levels - 2:
+            sent, *both = call(
+                functools.partial(sent_kernel, level + 1), "sent", (message, splits, both_tables), (bits, *kept, received)
+            )
+    peak = ((WIDTHS, trials), f32)
+    scratch = [pltpu.VMEM(*splits), pltpu.VMEM(*both_tables)]
+    first, second = call(
+        functools.partial(peaks_kernel, levels - 1), "peaks", (peak, peak), (bits, *kept, received), scratch
+    )
     half = freq_count // 2
-    first = lax.ppermute(peaks[0], "freq", [(d, (d & 1) * half + (d >> 1)) for d in range(freq_count)])
-    second = lax.ppermute(peaks[1], "freq", [(d, (1 - (d & 1)) * half + (d >> 1)) for d in range(freq_count)])
-    top = bits[levels - 1] == 1
-    return jnp.stack([jnp.where(top, second, first), jnp.where(top, first, second)])
+    first = lax.ppermute(first, "freq", [(d, (d & 1) * half + (d >> 1)) for d in range(freq_count)])
+    second = lax.ppermute(second, "freq", [(d, (1 - (d & 1)) * half + (d >> 1)) for d in range(freq_count)])
+    return call(
+        functools.partial(join_kernel, levels - 1), "join", (((2, WIDTHS, trials), f32),), (bits, first, second)
+    )[0]
 
 
 def solution(mesh):

time: 121 us -> 90 us (0.74)
  the two profiles are of different devices: /device:TPU:12 before, /device:TPU:1 now
where the time goes in v1:
time: 90 us; the launch traced here: 88.4 us
  waiting for transfers between devices  44.5 us (49%)
  Pallas kernels  21 us (23%)
  starting transfers between devices  20.6 us (23%)
  local copies, waits for them, and re-layouts  1.99 us (2%)
    ppermute x6, waiting for transfers between devices, swap(): lax.ppermute(x, 'freq', [(i, i ^ 1 << bit) for i in range(lax.axis_size('...  26 us
    pallas_call x10, Pallas kernels, call(): pl.pallas_call(kernel, out_shape=tuple((jax.ShapeDtypeStruct(shape, dtype...  18.3 us
    all_to_all x1, waiting for transfers between devices, local(): lax.all_to_all(power, 'freq', split_axis=0, concat_axis=0, tiled=True)  16.1 us
    all_to_all x1, starting transfers between devices, local(): lax.all_to_all(power, 'freq', split_axis=0, concat_axis=0, tiled=True)  12.7 us
    ppermute x1, starting transfers between devices, local(): lax.ppermute(first, 'freq', [(d, (d & 1) * half + (d >> 1)) for d in rang...  5.49 us
    pallas_call x1, Pallas kernels, filter_power(): pl.pallas_call(filter_kernel, grid=(coarse // step,), out_shape=jax.Shape...  2.71 us
    ppermute x6, starting transfers between devices, swap(): lax.ppermute(x, 'freq', [(i, i ^ 1 << bit) for i in range(lax.axis_size('...  2.31 us
    unnamed x8, local copies, waits for them, and re-layouts  1.97 us
  transfers between devices with their start and end apart: 9, of which 9 were waited for; matrix products, arithmetic and copies ran while one was open for 0% of the time, Pallas kernels for 5%

profile of v1, /device:TPU:1, one launch (start us, length us, event | category | flops | bytes accessed | tf_op | source)
XLA Modules:
  0.0 88.4 jit_solution(3732018184238679876)
XLA Ops:
  0.0 1.2 %copy-done = bf16[2,2,32,16,256]{4,3,2,1,0:T(8,128)(2,1)S(1)} copy-done((bf16[2,2,32,16,256]{4,3,2,1,0:T(8,128)(2,1)S(1)}, bf16[2,2,32,16,256]{4,3,2,1,0:T(8,128)(2,1)}, u32[]{:S(2)}) %copy-start) | copy-done | bytes 1048600
  1.2 0.7 copy-done.1
  2.0 2.7 %filter_power.1 = bf16[16,2,2,16,256]{4,3,2,1,0:T(8,128)(2,1)} custom-call(bf16[96,128]{1,0:T(8,128)(2,1)S(1)} %copy-done.1, bf16[2,2,32,16,256]{4,3,2,1,0:T(8,128)(2,1)S(1)} %copy-done), custom_call_target="tpu_custom_call" | custom-call | tf_op jit(solution)/shard_map/filter_power/pallas_call | solution.py:64
  4.7 12.7 %all-to-all-start = ((bf16[32,2,16,256]{3,2,1,0:T(8,128)(2,1)}), bf16[32,2,16,256]{3,2,1,0:T(8,128)(2,1)S(1)}, u32[]{:S(2)}, u32[]{:S(2)}) async-start(bf16[32,2,16,256]{3,2,1,0:T(8,128)(2,1)} %bitcast), calls=%async_computation | async-start | bytes 1048576 | tf_op jit(solution)/shard_map/all_to_all | solution.py:254
  17.4 0.3 collective-permute-start.1
  17.8 0.4 collective-permute-start
  18.2 0.5 collective-permute-done.1
  18.7 0.7 collective-permute-done
  19.4 0.1 pad_maximum_fusion.delays_ref
  19.5 16.1 %all-to-all-done.arrived_ref = bf16[32,2,16,256]{3,2,1,0:T(8,128)(2,1)S(1)} async-done(((bf16[32,2,16,256]{3,2,1,0:T(8,128)(2,1)}), bf16[32,2,16,256]{3,2,1,0:T(8,128)(2,1)S(1)}, u32[]{:S(2)}, u32[]{:S(2)}) %all-to-all-start) | async-done | bytes 524320 | tf_op jit(solution)/shard_map/all_to_all | solution.py:254
  35.6 5.7 %dedisperse.1 = (s16[272,256]{1,0:T(8,128)(2,1)S(1)}, bf16[2,256,512]{2,1,0:T(8,128)(2,1)S(1)}, f32[2,16,256]{2,1,0:T(8,128)S(1)}) custom-call(s32[8]{0:T(128)S(1)} %shift-right-arithmetic_and_fusion.bits_ref, bf16[32,2,16,256]{3,2,1,0:T(8,128)(2,1)S(1)} %all-to-all-done.arrived_ref, bf16[2,256,512]{2,1,0:T(8,128)(2,1)S(1)} %pad_maximum_fusion.delays_ref, ...), custom_call_target="tpu_custom_call" | custom-call | tf_op jit(solution)/shard_map/dedisperse/pallas_call | solution.py:228
  41.3 0.1 collective-permute-start.2
  41.4 1.2 %kept.4 = (bf16[256,512]{1,0:T(8,128)(2,1)S(1)}, f32[16,256]{1,0:T(8,128)S(1)}) custom-call(s32[8]{0:T(128)S(1)} %shift-right-arithmetic_and_fusion.bits_ref, bf16[2,256,512]{2,1,0:T(8,128)(2,1)S(1)} %get-tuple-element.27.split_in_ref, f32[2,16,256]{2,1,0:T(8,128)S(1)} %get-tuple-element.28.table_in_ref), custom_call_target="tpu_custom_call" | custom-call | tf_op jit(solution)/shard_map/kept/pallas_call | solution.py:228
  42.5 3.9 %collective-permute-done.2.received_ref = s16[272,256]{1,0:T(8,128)(2,1)S(1)} collective-permute-done((s16[272,256]{1,0:T(8,128)(2,1)S(1)}, s16[272,256]{1,0:T(8,128)(2,1)S(1)}, u32[]{:S(2)}, u32[]{:S(2)}) %collective-permute-start.2) | collective-permute-done | bytes 139296 | tf_op jit(solution)/shard_map/ppermute | solution.py:240
  46.4 1.5 %sent.3 = (s16[272,256]{1,0:T(8,128)(2,1)S(1)}, bf16[2,256,512]{2,1,0:T(8,128)(2,1)S(1)}, f32[2,16,256]{2,1,0:T(8,128)S(1)}) custom-call(s32[8]{0:T(128)S(1)} %shift-right-arithmetic_and_fusion.bits_ref, bf16[256,512]{1,0:T(8,128)(2,1)S(1)} %get-tuple-element.29.kept_split_ref, f32[16,256]{1,0:T(8,128)S(1)} %get-tuple-element.30.kept_table_ref, ...), custom_call_target="tpu_custom_call" | custom-call | tf_op jit(solution)/shard_map/sent/pallas_call | solution.py:228
  47.9 0.2 collective-permute-start.3
  48.1 1.2 %kept.5 = (bf16[256,512]{1,0:T(8,128)(2,1)S(1)}, f32[16,256]{1,0:T(8,128)S(1)}) custom-call(s32[8]{0:T(128)S(1)} %shift-right-arithmetic_and_fusion.bits_ref, bf16[2,256,512]{2,1,0:T(8,128)(2,1)S(1)} %get-tuple-element.32.split_in_ref, f32[2,16,256]{2,1,0:T(8,128)S(1)} %get-tuple-element.33.table_in_ref), custom_call_target="tpu_custom_call" | custom-call | tf_op jit(solution)/shard_map/kept/pallas_call | solution.py:228
  49.3 5.0 %collective-permute-done.3.received_ref = s16[272,256]{1,0:T(8,128)(2,1)S(1)} collective-permute-done((s16[272,256]{1,0:T(8,128)(2,1)S(1)}, s16[272,256]{1,0:T(8,128)(2,1)S(1)}, u32[]{:S(2)}, u32[]{:S(2)}) %collective-permute-start.3) | collective-permute-done | bytes 139296 | tf_op jit(solution)/shard_map/ppermute | solution.py:240
  54.4 1.5 %sent.4 = (s16[272,256]{1,0:T(8,128)(2,1)S(1)}, bf16[2,256,512]{2,1,0:T(8,128)(2,1)S(1)}, f32[2,16,256]{2,1,0:T(8,128)S(1)}) custom-call(s32[8]{0:T(128)S(1)} %shift-right-arithmetic_and_fusion.bits_ref, bf16[256,512]{1,0:T(8,128)(2,1)S(1)} %get-tuple-element.34.kept_split_ref, f32[16,256]{1,0:T(8,128)S(1)} %get-tuple-element.35.kept_table_ref, ...), custom_call_target="tpu_custom_call" | custom-call | tf_op jit(solution)/shard_map/sent/pallas_call | solution.py:228
  55.8 0.6 collective-permute-start.4
  56.5 1.2 %kept.6 = (bf16[256,512]{1,0:T(8,128)(2,1)S(1)}, f32[16,256]{1,0:T(8,128)S(1)}) custom-call(s32[8]{0:T(128)S(1)} %shift-right-arithmetic_and_fusion.bits_ref, bf16[2,256,512]{2,1,0:T(8,128)(2,1)S(1)} %get-tuple-element.37.split_in_ref, f32[2,16,256]{2,1,0:T(8,128)S(1)} %get-tuple-element.38.table_in_ref), custom_call_target="tpu_custom_call" | custom-call | tf_op jit(solution)/shard_map/kept/pallas_call | solution.py:228
  57.6 7.5 %collective-permute-done.4.received_ref = s16[272,256]{1,0:T(8,128)(2,1)S(1)} collective-permute-done((s16[272,256]{1,0:T(8,128)(2,1)S(1)}, s16[272,256]{1,0:T(8,128)(2,1)S(1)}, u32[]{:S(2)}, u32[]{:S(2)}) %collective-permute-start.4) | collective-permute-done | bytes 139296 | tf_op jit(solution)/shard_map/ppermute | solution.py:240
  65.1 1.5 %sent.5 = (s16[272,256]{1,0:T(8,128)(2,1)S(1)}, bf16[2,256,512]{2,1,0:T(8,128)(2,1)S(1)}, f32[2,16,256]{2,1,0:T(8,128)S(1)}) custom-call(s32[8]{0:T(128)S(1)} %shift-right-arithmetic_and_fusion.bits_ref, bf16[256,512]{1,0:T(8,128)(2,1)S(1)} %get-tuple-element.39.kept_split_ref, f32[16,256]{1,0:T(8,128)S(1)} %get-tuple-element.40.kept_table_ref, ...), custom_call_target="tpu_custom_call" | custom-call | tf_op jit(solution)/shard_map/sent/pallas_call | solution.py:228
  66.6 0.7 collective-permute-start.5
  67.3 1.2 %kept.7 = (bf16[256,512]{1,0:T(8,128)(2,1)S(1)}, f32[16,256]{1,0:T(8,128)S(1)}) custom-call(s32[8]{0:T(128)S(1)} %shift-right-arithmetic_and_fusion.bits_ref, bf16[2,256,512]{2,1,0:T(8,128)(2,1)S(1)} %get-tuple-element.42.split_in_ref, f32[2,16,256]{2,1,0:T(8,128)S(1)} %get-tuple-element.43.table_in_ref), custom_call_target="tpu_custom_call" | custom-call | tf_op jit(solution)/shard_map/kept/pallas_call | solution.py:228
  68.4 8.3 %collective-permute-done.5.received_ref = s16[272,256]{1,0:T(8,128)(2,1)S(1)} collective-permute-done((s16[272,256]{1,0:T(8,128)(2,1)S(1)}, s16[272,256]{1,0:T(8,128)(2,1)S(1)}, u32[]{:S(2)}, u32[]{:S(2)}) %collective-permute-start.5) | collective-permute-done | bytes 139296 | tf_op jit(solution)/shard_map/ppermute | solution.py:240
  76.8 2.4 %peaks.1 = (f32[8,256]{1,0:T(8,128)S(1)}, f32[8,256]{1,0:T(8,128)S(1)}) custom-call(s32[8]{0:T(128)S(1)} %shift-right-arithmetic_and_fusion.bits_ref, bf16[256,512]{1,0:T(8,128)(2,1)S(1)} %get-tuple-element.44.kept_split_ref, f32[16,256]{1,0:T(8,128)S(1)} %get-tuple-element.45.kept_table_ref, s16[272,256]{1,0:T(8,128)(2,1)S(1)} %collective-permute-done.5.received_ref), custom_call_target="tpu_custom_call" | custom-call | tf_op jit(solution)/shard_map/peaks/pallas_call | solution.py:228
  79.1 5.5 %collective-permute-start.6 = (f32[8,256]{1,0:T(8,128)S(1)}, f32[8,256]{1,0:T(8,128)S(1)}, u32[]{:S(2)}, u32[]{:S(2)}) collective-permute-start(f32[8,256]{1,0:T(8,128)S(1)} %get-tuple-element.47), channel_id=1, source_target_pairs={{0,0},{8,128},{16,8},{24,136},{32,16},{40,144},{48,24},{56,152},{6... | collective-permute-start | bytes 24584 | tf_op jit(solution)/shard_map/ppermute | solution.py:283
  84.6 0.1 collective-permute-start.7
  84.7 0.7 collective-permute-done.6.first_ref
  85.4 1.8 %collective-permute-done.7.second_ref = f32[8,256]{1,0:T(8,128)S(1)} collective-permute-done((f32[8,256]{1,0:T(8,128)S(1)}, f32[8,256]{1,0:T(8,128)S(1)}, u32[]{:S(2)}, u32[]{:S(2)}) %collective-permute-start.7) | collective-permute-done | bytes 8224 | tf_op jit(solution)/shard_map/ppermute | solution.py:284
  87.2 1.1 %join.1 = f32[2,8,256]{2,1,0:T(8,128)} custom-call(s32[8]{0:T(128)S(1)} %shift-right-arithmetic_and_fusion.bits_ref, f32[8,256]{1,0:T(8,128)S(1)} %collective-permute-done.6.first_ref, f32[8,256]{1,0:T(8,128)S(1)} %collective-permute-done.7.second_ref), custom_call_target="tpu_custom_call" | custom-call | tf_op jit(solution)/shard_map/join/pallas_call | solution.py:228
  (13 shorter events, 0.1 us)
Async XLA Ops:
  0.0 1.2 %copy-start = (bf16[2,2,32,16,256]{4,3,2,1,0:T(8,128)(2,1)S(1)}, bf16[2,2,32,16,256]{4,3,2,1,0:T(8,128)(2,1)}, u32[]{:S(2)}) copy-start(bf16[2,2,32,16,256]{4,3,2,1,0:T(8,128)(2,1)} %volts_ref.1) | copy-start | bytes 3145732
  1.2 0.7 copy-start.1
  4.7 12.7 %copy-start.3 = (s32[5,3,256]{2,1,0:T(4,128)S(1)}, s32[5,3,256]{2,1,0:T(4,128)}, u32[]{:S(2)}) copy-start(s32[5,3,256]{2,1,0:T(4,128)} %param.6) | copy-start | bytes 46084
  4.7 13.1 %copy-start.2 = (s32[256,512]{1,0:T(8,128)S(1)}, s32[256,512]{1,0:T(8,128)}, u32[]{:S(2)}) copy-start(s32[256,512]{1,0:T(8,128)} %param.5) | copy-start | bytes 1572868
  4.7 30.9 %all-to-all-start = ((bf16[32,2,16,256]{3,2,1,0:T(8,128)(2,1)}), bf16[32,2,16,256]{3,2,1,0:T(8,128)(2,1)S(1)}, u32[]{:S(2)}, u32[]{:S(2)}) async-start(bf16[32,2,16,256]{3,2,1,0:T(8,128)(2,1)} %bitcast), calls=%async_computation | async-start | bytes 1048576 | tf_op jit(solution)/shard_map/all_to_all | solution.py:254
  17.4 1.3 %collective-permute-start.1 = (f32[16,256]{1,0:T(8,128)S(1)}, f32[16,256]{1,0:T(8,128)S(1)}, u32[]{:S(2)}, u32[]{:S(2)}) collective-permute-start(f32[16,256]{1,0:T(8,128)S(1)} %get-tuple-element.50), channel_id=1, source_target_pairs={{0,8},{8,0},{16,24},{24,16},{32,40},{40,32},{48,56},{56,48},{64,72... | collective-permute-start | bytes 49160 | tf_op jit(solution)/shard_map/ppermute | solution.py:240
  17.8 1.6 %collective-permute-start = (bf16[256,512]{1,0:T(8,128)(2,1)S(1)}, bf16[256,512]{1,0:T(8,128)(2,1)S(1)}, u32[]{:S(2)}, u32[]{:S(2)}) collective-permute-start(bf16[256,512]{1,0:T(8,128)(2,1)S(1)} %convert_element_type.11), channel_id=1, source_target_pairs={{0,8},{8,0},{16,24},{24,16},{32,40},{40,32},{48,56},{56,48},{64,72... | collective-permute-start | bytes 786440 | tf_op jit(solution)/shard_map/ppermute | solution.py:240
  41.3 5.2 %collective-permute-start.2 = (s16[272,256]{1,0:T(8,128)(2,1)S(1)}, s16[272,256]{1,0:T(8,128)(2,1)S(1)}, u32[]{:S(2)}, u32[]{:S(2)}) collective-permute-start(s16[272,256]{1,0:T(8,128)(2,1)S(1)} %get-tuple-element.31), channel_id=1, source_target_pairs={{0,16},{8,24},{16,0},{24,8},{32,48},{40,56},{48,32},{56,40},{64,80... | collective-permute-start | bytes 417800 | tf_op jit(solution)/shard_map/ppermute | solution.py:240
  47.9 6.5 %collective-permute-start.3 = (s16[272,256]{1,0:T(8,128)(2,1)S(1)}, s16[272,256]{1,0:T(8,128)(2,1)S(1)}, u32[]{:S(2)}, u32[]{:S(2)}) collective-permute-start(s16[272,256]{1,0:T(8,128)(2,1)S(1)} %get-tuple-element.36), channel_id=1, source_target_pairs={{0,32},{8,40},{16,48},{24,56},{32,0},{40,8},{48,16},{56,24},{64,96... | collective-permute-start | bytes 417800 | tf_op jit(solution)/shard_map/ppermute | solution.py:240
  55.8 9.3 %collective-permute-start.4 = (s16[272,256]{1,0:T(8,128)(2,1)S(1)}, s16[272,256]{1,0:T(8,128)(2,1)S(1)}, u32[]{:S(2)}, u32[]{:S(2)}) collective-permute-start(s16[272,256]{1,0:T(8,128)(2,1)S(1)} %get-tuple-element.41), channel_id=1, source_target_pairs={{0,64},{8,72},{16,80},{24,88},{32,96},{40,104},{48,112},{56,120},{... | collective-permute-start | bytes 417800 | tf_op jit(solution)/shard_map/ppermute | solution.py:240
  66.6 10.2 %collective-permute-start.5 = (s16[272,256]{1,0:T(8,128)(2,1)S(1)}, s16[272,256]{1,0:T(8,128)(2,1)S(1)}, u32[]{:S(2)}, u32[]{:S(2)}) collective-permute-start(s16[272,256]{1,0:T(8,128)(2,1)S(1)} %get-tuple-element.46), channel_id=1, source_target_pairs={{0,128},{8,136},{16,144},{24,152},{32,160},{40,168},{48,176},{56,1... | collective-permute-start | bytes 417800 | tf_op jit(solution)/shard_map/ppermute | solution.py:240
  79.1 6.3 %collective-permute-start.6 = (f32[8,256]{1,0:T(8,128)S(1)}, f32[8,256]{1,0:T(8,128)S(1)}, u32[]{:S(2)}, u32[]{:S(2)}) collective-permute-start(f32[8,256]{1,0:T(8,128)S(1)} %get-tuple-element.47), channel_id=1, source_target_pairs={{0,0},{8,128},{16,8},{24,136},{32,16},{40,144},{48,24},{56,152},{6... | collective-permute-start | bytes 24584 | tf_op jit(solution)/shard_map/ppermute | solution.py:283
  84.6 2.6 %collective-permute-start.7 = (f32[8,256]{1,0:T(8,128)S(1)}, f32[8,256]{1,0:T(8,128)S(1)}, u32[]{:S(2)}, u32[]{:S(2)}) collective-permute-start(f32[8,256]{1,0:T(8,128)S(1)} %get-tuple-element.48), channel_id=1, source_target_pairs={{0,128},{8,0},{16,136},{24,8},{32,144},{40,16},{48,152},{56,24},{6... | collective-permute-start | bytes 24584 | tf_op jit(solution)/shard_map/ppermute | solution.py:284

commit v2 on v1

--- a/solution.py
+++ b/solution.py
@@ -13,6 +13,9 @@
 WIDTHS = 8
 SHIFTS = 32
 INNER = 4
+
+BEAM_BIT = 2
+SWAP_BITS = (0, 1, 3, 4)
 
 epsilon = 1e-06
 f32 = jnp.float32
@@ -54,23 +57,22 @@
             y = jnp.dot(matrix, stacked, preferred_element_type=f32)
             y = y[:rows] + (y[rows : 2 * rows] + y[2 * rows :])
             power = y[:upchan] * y[:upchan] + y[upchan:] * y[upchan:]
-            out_ref[q // 2, beam, q % 2] = power.astype(bf16)
+            out_ref[q // 2 + beam * (count // 2), q % 2] = power.astype(bf16)
 
 
 def filter_power(voltages):
     parts, beams, coarse, upchan, samples = voltages.shape
-    step = 8
+    step = 2 << BEAM_BIT
     matrix = jnp.asarray(filter_matrix(upchan))
     return pl.pallas_call(
         filter_kernel,
         grid=(coarse // step,),
-        out_shape=jax.ShapeDtypeStruct((coarse // 2, beams, 2, upchan, samples), bf16),
+        out_shape=jax.ShapeDtypeStruct((coarse // 2 * beams, 2, upchan, samples), bf16),
         in_specs=[
             pl.BlockSpec(matrix.shape, lambda i: (0, 0)),
             pl.BlockSpec((parts, beams, step, upchan, samples), lambda i: (0, 0, i, 0, 0)),
         ],
-        out_specs=pl.BlockSpec((step // 2, beams, 2, upchan, samples), lambda i: (i, 0, 0, 0, 0)),
-        compiler_params=pltpu.CompilerParams(vmem_limit_bytes=8 << 20),
+        out_specs=pl.BlockSpec((step // 2 * beams, 2, upchan, samples), lambda i: (i, 0, 0, 0)),
         name="filter_power",
     )(matrix, voltages)
 
@@ -146,9 +148,9 @@
     sources, _, upchan, samples = arrived_ref.shape
     trials = delays_ref.shape[1]
     channels = sources * upchan
-    core = bits_ref[0]
+    first = bits_ref[BEAM_BIT]
     for which in range(2):
-        unit = core if which == 0 else 1 - core
+        unit = first if which == 0 else 1 - first
         x = arrived_ref[:, pl.ds(unit, 1)].reshape(channels, samples).astype(f32)
         for inner in range(INNER):
             moved = x if inner == 0 else shifted(x, inner)
@@ -172,12 +174,12 @@
 
 
 def put_sent(level, bits_ref, split_ref, table_ref, sent_ref):
-    table = table_ref[1 - bits_ref[level + 1]]
+    table = table_ref[1 - bits_ref[SWAP_BITS[level]]]
     put_message(sent_ref, merge_unit(split_ref, table, level), table)
 
 
 def kept_kernel(level, bits_ref, split_in_ref, table_in_ref, split_ref, table_ref):
-    table = table_in_ref[bits_ref[level + 1]]
+    table = table_in_ref[bits_ref[SWAP_BITS[level]]]
     split_ref[...] = split_of(merge_unit(split_in_ref, table, level))
     table_ref[...] = table
 
@@ -191,13 +193,13 @@
 
 
 def sent_kernel(level, bits_ref, kept_split_ref, kept_table_ref, received_ref, sent_ref, split_ref, table_ref):
-    load_units(bits_ref[level], kept_split_ref, kept_table_ref, received_ref, split_ref, table_ref)
+    load_units(bits_ref[SWAP_BITS[level - 1]], kept_split_ref, kept_table_ref, received_ref, split_ref, table_ref)
     put_sent(level, bits_ref, split_ref, table_ref, sent_ref)
 
 
 def peaks_kernel(level, bits_ref, kept_split_ref, kept_table_ref, received_ref, first_ref, second_ref, split_ref, table_ref):
-    load_units(bits_ref[level], kept_split_ref, kept_table_ref, received_ref, split_ref, table_ref)
-    for out_ref, unit in ((first_ref, bits_ref[0]), (second_ref, 1 - bits_ref[0])):
+    load_units(bits_ref[SWAP_BITS[level - 1]], kept_split_ref, kept_table_ref, received_ref, split_ref, table_ref)
+    for out_ref, unit in ((first_ref, bits_ref[BEAM_BIT]), (second_ref, 1 - bits_ref[BEAM_BIT])):
         merged = merge_unit(split_ref, table_ref[unit], level)
         series = merged.T
         samples = series.shape[0]
@@ -236,8 +238,35 @@
     )(*operands)
 
 
+def move(x, target):
+    return lax.ppermute(x, "freq", [(i, target(i)) for i in range(lax.axis_size("freq"))])
+
+
 def swap(x, bit):
-    return lax.ppermute(x, "freq", [(i, i ^ (1 << bit)) for i in range(lax.axis_size("freq"))])
+    return move(x, lambda i: i ^ (1 << bit))
+
+
+def bit(number, index):
+    return number >> index & 1
+
+
+def gather_units(x):
+    def target(flip):
+        def device(g):
+            low = g >> 1 & (1 << BEAM_BIT) - 1
+            return low | (bit(g, 0) ^ flip) << BEAM_BIT | g >> (BEAM_BIT + 1) << (BEAM_BIT + 1)
+
+        return device
+
+    return jnp.stack([move(x, target(0)), move(x, target(1))])
+
+
+def home(flip, top):
+    def device(d):
+        low = d & (1 << BEAM_BIT) - 1
+        return low | d >> (BEAM_BIT + 1) << BEAM_BIT | (bit(d, BEAM_BIT) ^ flip) << top
+
+    return device
 
 
 def local(voltages, sub_delays, merge_tables):
@@ -254,10 +283,10 @@
     arrived = lax.all_to_all(power, "freq", split_axis=0, concat_axis=0, tiled=True)
 
     delays = sub_delays.astype(bf16)
-    delays = jnp.stack([delays, swap(delays, 0)])
+    delays = gather_units(delays)
     tables = merge_tables.reshape(3 * levels, trials).astype(f32)
     tables = jnp.pad(tables, ((0, -3 * levels % 16), (0, 0)))
-    tables = jnp.stack([tables, swap(tables, 0)])
+    tables = gather_units(tables)
     rows = tables.shape[1]
 
     message = ((trials + rows, samples), jnp.int16)
@@ -268,7 +297,7 @@
         dedisperse_kernel, "dedisperse", (message, splits, both_tables), (bits, arrived, delays, tables), [stack], 24
     )
     for level in range(levels - 1):
-        received = swap(sent, level + 1)
+        received = swap(sent, SWAP_BITS[level])
         kept = call(functools.partial(kept_kernel, level), "kept", (split, table), (bits, *both))
         if level < levels - 2:
             sent, *both = call(
@@ -279,9 +308,7 @@
     first, second = call(
         functools.partial(peaks_kernel, levels - 1), "peaks", (peak, peak), (bits, *kept, received), scratch
     )
-    half = freq_count // 2
-    first = lax.ppermute(first, "freq", [(d, (d & 1) * half + (d >> 1)) for d in range(freq_count)])
-    second = lax.ppermute(second, "freq", [(d, (1 - (d & 1)) * half + (d >> 1)) for d in range(freq_count)])
+    first, second = move(first, home(0, levels - 1)), move(second, home(1, levels - 1))
     return call(
         functools.partial(join_kernel, levels - 1), "join", (((2, WIDTHS, trials), f32),), (bits, first, second)
     )[0]

time: 90 us -> 90 us (level)
  the two profiles are of different devices: /device:TPU:1 before, /device:TPU:80 now
where the time goes in v2:
time: 90 us; the launch traced here: 89.7 us
  starting transfers between devices  37.6 us (42%)
  waiting for transfers between devices  29.3 us (33%)
  Pallas kernels  22.5 us (25%)
    ppermute x10, starting transfers between devices, move(): lax.ppermute(x, 'freq', [(i, target(i)) for i in range(lax.axis_size('fre...  26.7 us
    ppermute x10, waiting for transfers between devices, move(): lax.ppermute(x, 'freq', [(i, target(i)) for i in range(lax.axis_size('fre...  23.4 us
    pallas_call x10, Pallas kernels, call(): pl.pallas_call(kernel, out_shape=tuple((jax.ShapeDtypeStruct(shape, dtype...  18.4 us
    all_to_all x1, starting transfers between devices, local(): lax.all_to_all(power, 'freq', split_axis=0, concat_axis=0, tiled=True)  10.9 us
    all_to_all x1, waiting for transfers between devices, local(): lax.all_to_all(power, 'freq', split_axis=0, concat_axis=0, tiled=True)  5.94 us
    pallas_call x1, Pallas kernels, filter_power(): pl.pallas_call(filter_kernel, grid=(coarse // step,), out_shape=jax.Shape...  4.1 us
  transfers between devices with their start and end apart: 11, of which 7 were waited for; matrix products, arithmetic and copies ran while one was open for 0% of the time, Pallas kernels for 5%

profile of v2, /device:TPU:80, one launch (start us, length us, event | category | flops | bytes accessed | tf_op | source)
XLA Modules:
  0.0 89.7 jit_solution(17153677015903641128)
XLA Ops:
  0.0 4.1 %filter_power.1 = bf16[32,2,16,256]{3,2,1,0:T(8,128)(2,1)} custom-call(bf16[96,128]{1,0:T(8,128)(2,1)} %constant.13.clone.matrix_ref, bf16[2,2,32,16,256]{4,3,2,1,0:T(8,128)(2,1)} %volts_ref.1), custom_call_target="tpu_custom_call" | custom-call | tf_op jit(solution)/shard_map/filter_power/pallas_call | solution.py:67
  4.1 10.9 %all-to-all-start = ((bf16[32,2,16,256]{3,2,1,0:T(8,128)(2,1)}), bf16[32,2,16,256]{3,2,1,0:T(8,128)(2,1)S(1)}, u32[]{:S(2)}, u32[]{:S(2)}) async-start(bf16[32,2,16,256]{3,2,1,0:T(8,128)(2,1)} %filter_power.1), calls=%async_computation | async-start | bytes 1048576 | tf_op jit(solution)/shard_map/all_to_all | solution.py:283
  15.0 0.0 copy-start.1
  15.0 3.1 %collective-permute-start.1 = (bf16[256,512]{1,0:T(8,128)(2,1)S(1)}, bf16[256,512]{1,0:T(8,128)(2,1)S(1)}, u32[]{:S(2)}, u32[]{:S(2)}) collective-permute-start(bf16[256,512]{1,0:T(8,128)(2,1)S(1)} %convert_element_type.11), channel_id=1, source_target_pairs={{0,32},{8,0},{16,40},{24,8},{32,48},{40,16},{48,56},{56,24},{64,96... | collective-permute-start | bytes 786440 | tf_op jit(solution)/shard_map/ppermute | solution.py:242
  18.1 0.7 collective-permute-start
  18.8 3.1 %collective-permute-start.3 = (f32[16,256]{1,0:T(8,128)S(1)}, f32[16,256]{1,0:T(8,128)S(1)}, u32[]{:S(2)}, u32[]{:S(2)}) collective-permute-start(f32[16,256]{1,0:T(8,128)S(1)} %pad.4), channel_id=1, source_target_pairs={{0,32},{8,0},{16,40},{24,8},{32,48},{40,16},{48,56},{56,24},{64,96... | collective-permute-start | bytes 49160 | tf_op jit(solution)/shard_map/ppermute | solution.py:242
  21.9 0.7 collective-permute-start.2
  22.6 3.7 %collective-permute-done.3 = f32[16,256]{1,0:T(8,128)S(1)} collective-permute-done((f32[16,256]{1,0:T(8,128)S(1)}, f32[16,256]{1,0:T(8,128)S(1)}, u32[]{:S(2)}, u32[]{:S(2)}) %collective-permute-start.3) | collective-permute-done | bytes 16416 | tf_op jit(solution)/shard_map/ppermute | solution.py:242
  26.3 0.1 pad_maximum_fusion.delays_ref
  26.3 5.9 %all-to-all-done.arrived_ref = bf16[32,2,16,256]{3,2,1,0:T(8,128)(2,1)S(1)} async-done(((bf16[32,2,16,256]{3,2,1,0:T(8,128)(2,1)}), bf16[32,2,16,256]{3,2,1,0:T(8,128)(2,1)S(1)}, u32[]{:S(2)}, u32[]{:S(2)}) %all-to-all-start) | async-done | bytes 524320 | tf_op jit(solution)/shard_map/all_to_all | solution.py:283
  32.3 5.8 %dedisperse.1 = (s16[272,256]{1,0:T(8,128)(2,1)S(1)}, bf16[2,256,512]{2,1,0:T(8,128)(2,1)S(1)}, f32[2,16,256]{2,1,0:T(8,128)S(1)}) custom-call(s32[8]{0:T(128)S(1)} %shift-right-arithmetic_and_fusion.bits_ref, bf16[32,2,16,256]{3,2,1,0:T(8,128)(2,1)S(1)} %all-to-all-done.arrived_ref, bf16[2,256,512]{2,1,0:T(8,128)(2,1)S(1)} %pad_maximum_fusion.delays_ref, ...), custom_call_target="tpu_custom_call" | custom-call | tf_op jit(solution)/shard_map/dedisperse/pallas_call | solution.py:230
  38.1 0.3 collective-permute-start.4
  38.3 1.2 %kept.4 = (bf16[256,512]{1,0:T(8,128)(2,1)S(1)}, f32[16,256]{1,0:T(8,128)S(1)}) custom-call(s32[8]{0:T(128)S(1)} %shift-right-arithmetic_and_fusion.bits_ref, bf16[2,256,512]{2,1,0:T(8,128)(2,1)S(1)} %get-tuple-element.27.split_in_ref, f32[2,16,256]{2,1,0:T(8,128)S(1)} %get-tuple-element.28.table_in_ref), custom_call_target="tpu_custom_call" | custom-call | tf_op jit(solution)/shard_map/kept/pallas_call | solution.py:230
  39.5 0.0 collective-permute-done.4.received_ref
  39.5 1.5 %sent.3 = (s16[272,256]{1,0:T(8,128)(2,1)S(1)}, bf16[2,256,512]{2,1,0:T(8,128)(2,1)S(1)}, f32[2,16,256]{2,1,0:T(8,128)S(1)}) custom-call(s32[8]{0:T(128)S(1)} %shift-right-arithmetic_and_fusion.bits_ref, bf16[256,512]{1,0:T(8,128)(2,1)S(1)} %get-tuple-element.29.kept_split_ref, f32[16,256]{1,0:T(8,128)S(1)} %get-tuple-element.30.kept_table_ref, ...), custom_call_target="tpu_custom_call" | custom-call | tf_op jit(solution)/shard_map/sent/pallas_call | solution.py:230
  41.0 4.5 %collective-permute-start.5 = (s16[272,256]{1,0:T(8,128)(2,1)S(1)}, s16[272,256]{1,0:T(8,128)(2,1)S(1)}, u32[]{:S(2)}, u32[]{:S(2)}) collective-permute-start(s16[272,256]{1,0:T(8,128)(2,1)S(1)} %get-tuple-element.36), channel_id=1, source_target_pairs={{0,16},{8,24},{16,0},{24,8},{32,48},{40,56},{48,32},{56,40},{64,80... | collective-permute-start | bytes 417800 | tf_op jit(solution)/shard_map/ppermute | solution.py:242
  45.5 1.2 %kept.5 = (bf16[256,512]{1,0:T(8,128)(2,1)S(1)}, f32[16,256]{1,0:T(8,128)S(1)}) custom-call(s32[8]{0:T(128)S(1)} %shift-right-arithmetic_and_fusion.bits_ref, bf16[2,256,512]{2,1,0:T(8,128)(2,1)S(1)} %get-tuple-element.32.split_in_ref, f32[2,16,256]{2,1,0:T(8,128)S(1)} %get-tuple-element.33.table_in_ref), custom_call_target="tpu_custom_call" | custom-call | tf_op jit(solution)/shard_map/kept/pallas_call | solution.py:230
  46.6 3.0 %collective-permute-done.5.received_ref = s16[272,256]{1,0:T(8,128)(2,1)S(1)} collective-permute-done((s16[272,256]{1,0:T(8,128)(2,1)S(1)}, s16[272,256]{1,0:T(8,128)(2,1)S(1)}, u32[]{:S(2)}, u32[]{:S(2)}) %collective-permute-start.5) | collective-permute-done | bytes 139296 | tf_op jit(solution)/shard_map/ppermute | solution.py:242
  49.6 1.5 %sent.4 = (s16[272,256]{1,0:T(8,128)(2,1)S(1)}, bf16[2,256,512]{2,1,0:T(8,128)(2,1)S(1)}, f32[2,16,256]{2,1,0:T(8,128)S(1)}) custom-call(s32[8]{0:T(128)S(1)} %shift-right-arithmetic_and_fusion.bits_ref, bf16[256,512]{1,0:T(8,128)(2,1)S(1)} %get-tuple-element.34.kept_split_ref, f32[16,256]{1,0:T(8,128)S(1)} %get-tuple-element.35.kept_table_ref, ...), custom_call_target="tpu_custom_call" | custom-call | tf_op jit(solution)/shard_map/sent/pallas_call | solution.py:230
  51.1 1.0 %collective-permute-start.6 = (s16[272,256]{1,0:T(8,128)(2,1)S(1)}, s16[272,256]{1,0:T(8,128)(2,1)S(1)}, u32[]{:S(2)}, u32[]{:S(2)}) collective-permute-start(s16[272,256]{1,0:T(8,128)(2,1)S(1)} %get-tuple-element.41), channel_id=1, source_target_pairs={{0,64},{8,72},{16,80},{24,88},{32,96},{40,104},{48,112},{56,120},{... | collective-permute-start | bytes 417800 | tf_op jit(solution)/shard_map/ppermute | solution.py:242
  52.1 1.2 %kept.6 = (bf16[256,512]{1,0:T(8,128)(2,1)S(1)}, f32[16,256]{1,0:T(8,128)S(1)}) custom-call(s32[8]{0:T(128)S(1)} %shift-right-arithmetic_and_fusion.bits_ref, bf16[2,256,512]{2,1,0:T(8,128)(2,1)S(1)} %get-tuple-element.37.split_in_ref, f32[2,16,256]{2,1,0:T(8,128)S(1)} %get-tuple-element.38.table_in_ref), custom_call_target="tpu_custom_call" | custom-call | tf_op jit(solution)/shard_map/kept/pallas_call | solution.py:230
  53.3 4.7 %collective-permute-done.6.received_ref = s16[272,256]{1,0:T(8,128)(2,1)S(1)} collective-permute-done((s16[272,256]{1,0:T(8,128)(2,1)S(1)}, s16[272,256]{1,0:T(8,128)(2,1)S(1)}, u32[]{:S(2)}, u32[]{:S(2)}) %collective-permute-start.6) | collective-permute-done | bytes 139296 | tf_op jit(solution)/shard_map/ppermute | solution.py:242
  57.9 1.5 %sent.5 = (s16[272,256]{1,0:T(8,128)(2,1)S(1)}, bf16[2,256,512]{2,1,0:T(8,128)(2,1)S(1)}, f32[2,16,256]{2,1,0:T(8,128)S(1)}) custom-call(s32[8]{0:T(128)S(1)} %shift-right-arithmetic_and_fusion.bits_ref, bf16[256,512]{1,0:T(8,128)(2,1)S(1)} %get-tuple-element.39.kept_split_ref, f32[16,256]{1,0:T(8,128)S(1)} %get-tuple-element.40.kept_table_ref, ...), custom_call_target="tpu_custom_call" | custom-call | tf_op jit(solution)/shard_map/sent/pallas_call | solution.py:230
  59.4 5.3 %collective-permute-start.7 = (s16[272,256]{1,0:T(8,128)(2,1)S(1)}, s16[272,256]{1,0:T(8,128)(2,1)S(1)}, u32[]{:S(2)}, u32[]{:S(2)}) collective-permute-start(s16[272,256]{1,0:T(8,128)(2,1)S(1)} %get-tuple-element.46), channel_id=1, source_target_pairs={{0,128},{8,136},{16,144},{24,152},{32,160},{40,168},{48,176},{56,1... | collective-permute-start | bytes 417800 | tf_op jit(solution)/shard_map/ppermute | solution.py:242
  64.7 1.2 %kept.7 = (bf16[256,512]{1,0:T(8,128)(2,1)S(1)}, f32[16,256]{1,0:T(8,128)S(1)}) custom-call(s32[8]{0:T(128)S(1)} %shift-right-arithmetic_and_fusion.bits_ref, bf16[2,256,512]{2,1,0:T(8,128)(2,1)S(1)} %get-tuple-element.42.split_in_ref, f32[2,16,256]{2,1,0:T(8,128)S(1)} %get-tuple-element.43.table_in_ref), custom_call_target="tpu_custom_call" | custom-call | tf_op jit(solution)/shard_map/kept/pallas_call | solution.py:230
  65.9 4.7 %collective-permute-done.7.received_ref = s16[272,256]{1,0:T(8,128)(2,1)S(1)} collective-permute-done((s16[272,256]{1,0:T(8,128)(2,1)S(1)}, s16[272,256]{1,0:T(8,128)(2,1)S(1)}, u32[]{:S(2)}, u32[]{:S(2)}) %collective-permute-start.7) | collective-permute-done | bytes 139296 | tf_op jit(solution)/shard_map/ppermute | solution.py:242
  70.6 2.4 %peaks.1 = (f32[8,256]{1,0:T(8,128)S(1)}, f32[8,256]{1,0:T(8,128)S(1)}) custom-call(s32[8]{0:T(128)S(1)} %shift-right-arithmetic_and_fusion.bits_ref, bf16[256,512]{1,0:T(8,128)(2,1)S(1)} %get-tuple-element.44.kept_split_ref, f32[16,256]{1,0:T(8,128)S(1)} %get-tuple-element.45.kept_table_ref, s16[272,256]{1,0:T(8,128)(2,1)S(1)} %collective-permute-done.7.received_ref), custom_call_target="tpu_custom_call" | custom-call | tf_op jit(solution)/shard_map/peaks/pallas_call | solution.py:230
  73.0 7.3 %collective-permute-start.8 = (f32[8,256]{1,0:T(8,128)S(1)}, f32[8,256]{1,0:T(8,128)S(1)}, u32[]{:S(2)}, u32[]{:S(2)}) collective-permute-start(f32[8,256]{1,0:T(8,128)S(1)} %get-tuple-element.47), channel_id=1, source_target_pairs={{0,0},{8,8},{16,16},{24,24},{32,128},{40,136},{48,144},{56,152},{6... | collective-permute-start | bytes 24584 | tf_op jit(solution)/shard_map/ppermute | solution.py:242
  80.3 1.0 %collective-permute-start.9 = (f32[8,256]{1,0:T(8,128)S(1)}, f32[8,256]{1,0:T(8,128)S(1)}, u32[]{:S(2)}, u32[]{:S(2)}) collective-permute-start(f32[8,256]{1,0:T(8,128)S(1)} %get-tuple-element.48), channel_id=1, source_target_pairs={{0,128},{8,136},{16,144},{24,152},{32,0},{40,8},{48,16},{56,24},{6... | collective-permute-start | bytes 24584 | tf_op jit(solution)/shard_map/ppermute | solution.py:242
  81.3 0.4 collective-permute-done.8.first_ref
  81.6 6.9 %collective-permute-done.9.second_ref = f32[8,256]{1,0:T(8,128)S(1)} collective-permute-done((f32[8,256]{1,0:T(8,128)S(1)}, f32[8,256]{1,0:T(8,128)S(1)}, u32[]{:S(2)}, u32[]{:S(2)}) %collective-permute-start.9) | collective-permute-done | bytes 8224 | tf_op jit(solution)/shard_map/ppermute | solution.py:242
  88.5 1.1 %join.1 = f32[2,8,256]{2,1,0:T(8,128)} custom-call(s32[8]{0:T(128)S(1)} %shift-right-arithmetic_and_fusion.bits_ref, f32[8,256]{1,0:T(8,128)S(1)} %collective-permute-done.8.first_ref, f32[8,256]{1,0:T(8,128)S(1)} %collective-permute-done.9.second_ref), custom_call_target="tpu_custom_call" | custom-call | tf_op jit(solution)/shard_map/join/pallas_call | solution.py:230
  (12 shorter events, 0.1 us)
Async XLA Ops:
  4.1 10.9 %copy-start = (s32[256,512]{1,0:T(8,128)S(1)}, s32[256,512]{1,0:T(8,128)}, u32[]{:S(2)}) copy-start(s32[256,512]{1,0:T(8,128)} %param.5) | copy-start | bytes 1572868
  4.1 28.2 %all-to-all-start = ((bf16[32,2,16,256]{3,2,1,0:T(8,128)(2,1)}), bf16[32,2,16,256]{3,2,1,0:T(8,128)(2,1)S(1)}, u32[]{:S(2)}, u32[]{:S(2)}) async-start(bf16[32,2,16,256]{3,2,1,0:T(8,128)(2,1)} %filter_power.1), calls=%async_computation | async-start | bytes 1048576 | tf_op jit(solution)/shard_map/all_to_all | solution.py:283
  15.0 3.8 %copy-start.1 = (s32[5,3,256]{2,1,0:T(4,128)S(1)}, s32[5,3,256]{2,1,0:T(4,128)}, u32[]{:S(2)}) copy-start(s32[5,3,256]{2,1,0:T(4,128)} %param.6) | copy-start | bytes 46084
  15.0 11.2 %collective-permute-start.1 = (bf16[256,512]{1,0:T(8,128)(2,1)S(1)}, bf16[256,512]{1,0:T(8,128)(2,1)S(1)}, u32[]{:S(2)}, u32[]{:S(2)}) collective-permute-start(bf16[256,512]{1,0:T(8,128)(2,1)S(1)} %convert_element_type.11), channel_id=1, source_target_pairs={{0,32},{8,0},{16,40},{24,8},{32,48},{40,16},{48,56},{56,24},{64,96... | collective-permute-start | bytes 786440 | tf_op jit(solution)/shard_map/ppermute | solution.py:242
  18.1 8.2 %collective-permute-start = (bf16[256,512]{1,0:T(8,128)(2,1)S(1)}, bf16[256,512]{1,0:T(8,128)(2,1)S(1)}, u32[]{:S(2)}, u32[]{:S(2)}) collective-permute-start(bf16[256,512]{1,0:T(8,128)(2,1)S(1)} %convert_element_type.11), channel_id=1, source_target_pairs={{0,0},{8,32},{16,8},{24,40},{32,16},{40,48},{48,24},{56,56},{64,64... | collective-permute-start | bytes 786440 | tf_op jit(solution)/shard_map/ppermute | solution.py:242
  18.8 7.4 %collective-permute-start.3 = (f32[16,256]{1,0:T(8,128)S(1)}, f32[16,256]{1,0:T(8,128)S(1)}, u32[]{:S(2)}, u32[]{:S(2)}) collective-permute-start(f32[16,256]{1,0:T(8,128)S(1)} %pad.4), channel_id=1, source_target_pairs={{0,32},{8,0},{16,40},{24,8},{32,48},{40,16},{48,56},{56,24},{64,96... | collective-permute-start | bytes 49160 | tf_op jit(solution)/shard_map/ppermute | solution.py:242
  21.9 4.4 %collective-permute-start.2 = (f32[16,256]{1,0:T(8,128)S(1)}, f32[16,256]{1,0:T(8,128)S(1)}, u32[]{:S(2)}, u32[]{:S(2)}) collective-permute-start(f32[16,256]{1,0:T(8,128)S(1)} %pad.4), channel_id=1, source_target_pairs={{0,0},{8,32},{16,8},{24,40},{32,16},{40,48},{48,24},{56,56},{64,64... | collective-permute-start | bytes 49160 | tf_op jit(solution)/shard_map/ppermute | solution.py:242
  38.1 1.4 %collective-permute-start.4 = (s16[272,256]{1,0:T(8,128)(2,1)S(1)}, s16[272,256]{1,0:T(8,128)(2,1)S(1)}, u32[]{:S(2)}, u32[]{:S(2)}) collective-permute-start(s16[272,256]{1,0:T(8,128)(2,1)S(1)} %get-tuple-element.31), channel_id=1, source_target_pairs={{0,8},{8,0},{16,24},{24,16},{32,40},{40,32},{48,56},{56,48},{64,72... | collective-permute-start | bytes 417800 | tf_op jit(solution)/shard_map/ppermute | solution.py:242
  41.0 8.6 %collective-permute-start.5 = (s16[272,256]{1,0:T(8,128)(2,1)S(1)}, s16[272,256]{1,0:T(8,128)(2,1)S(1)}, u32[]{:S(2)}, u32[]{:S(2)}) collective-permute-start(s16[272,256]{1,0:T(8,128)(2,1)S(1)} %get-tuple-element.36), channel_id=1, source_target_pairs={{0,16},{8,24},{16,0},{24,8},{32,48},{40,56},{48,32},{56,40},{64,80... | collective-permute-start | bytes 417800 | tf_op jit(solution)/shard_map/ppermute | solution.py:242
  51.1 6.8 %collective-permute-start.6 = (s16[272,256]{1,0:T(8,128)(2,1)S(1)}, s16[272,256]{1,0:T(8,128)(2,1)S(1)}, u32[]{:S(2)}, u32[]{:S(2)}) collective-permute-start(s16[272,256]{1,0:T(8,128)(2,1)S(1)} %get-tuple-element.41), channel_id=1, source_target_pairs={{0,64},{8,72},{16,80},{24,88},{32,96},{40,104},{48,112},{56,120},{... | collective-permute-start | bytes 417800 | tf_op jit(solution)/shard_map/ppermute | solution.py:242
  59.4 11.2 %collective-permute-start.7 = (s16[272,256]{1,0:T(8,128)(2,1)S(1)}, s16[272,256]{1,0:T(8,128)(2,1)S(1)}, u32[]{:S(2)}, u32[]{:S(2)}) collective-permute-start(s16[272,256]{1,0:T(8,128)(2,1)S(1)} %get-tuple-element.46), channel_id=1, source_target_pairs={{0,128},{8,136},{16,144},{24,152},{32,160},{40,168},{48,176},{56,1... | collective-permute-start | bytes 417800 | tf_op jit(solution)/shard_map/ppermute | solution.py:242
  73.0 8.7 %collective-permute-start.8 = (f32[8,256]{1,0:T(8,128)S(1)}, f32[8,256]{1,0:T(8,128)S(1)}, u32[]{:S(2)}, u32[]{:S(2)}) collective-permute-start(f32[8,256]{1,0:T(8,128)S(1)} %get-tuple-element.47), channel_id=1, source_target_pairs={{0,0},{8,8},{16,16},{24,24},{32,128},{40,136},{48,144},{56,152},{6... | collective-permute-start | bytes 24584 | tf_op jit(solution)/shard_map/ppermute | solution.py:242
  80.3 8.2 %collective-permute-start.9 = (f32[8,256]{1,0:T(8,128)S(1)}, f32[8,256]{1,0:T(8,128)S(1)}, u32[]{:S(2)}, u32[]{:S(2)}) collective-permute-start(f32[8,256]{1,0:T(8,128)S(1)} %get-tuple-element.48), channel_id=1, source_target_pairs={{0,128},{8,136},{16,144},{24,152},{32,0},{40,8},{48,16},{56,24},{6... | collective-permute-start | bytes 24584 | tf_op jit(solution)/shard_map/ppermute | solution.py:242

commit v3 on v2

--- a/solution.py
+++ b/solution.py
@@ -33,7 +33,7 @@
     transform = np.block([[cosine, sine], [-sine, cosine]])
     full = np.concatenate([transform * np.tile(window[tap], 2)[None, :] for tap in range(TAPS)], axis=1)
     pieces, rest = [], full
-    for _ in range(3):
+    for _ in range(2):
         piece = rest.astype(jnp.bfloat16)
         pieces.append(piece)
         rest = rest - piece.astype(np.float64)
@@ -55,26 +55,27 @@
             taps = [x] + [shifted(x, tap) for tap in range(1, TAPS)]
             stacked = jnp.concatenate(taps, axis=0).astype(bf16)
             y = jnp.dot(matrix, stacked, preferred_element_type=f32)
-            y = y[:rows] + (y[rows : 2 * rows] + y[2 * rows :])
+            y = y[:rows] + y[rows:]
             power = y[:upchan] * y[:upchan] + y[upchan:] * y[upchan:]
-            out_ref[q // 2 + beam * (count // 2), q % 2] = power.astype(bf16)
+            out_ref[0, beam, 0, q // 2, q % 2] = power.astype(bf16)
 
 
 def filter_power(voltages):
     parts, beams, coarse, upchan, samples = voltages.shape
-    step = 2 << BEAM_BIT
+    step = 1 << BEAM_BIT
     matrix = jnp.asarray(filter_matrix(upchan))
-    return pl.pallas_call(
+    power = pl.pallas_call(
         filter_kernel,
         grid=(coarse // step,),
-        out_shape=jax.ShapeDtypeStruct((coarse // 2 * beams, 2, upchan, samples), bf16),
+        out_shape=jax.ShapeDtypeStruct((coarse // step // 2, beams, 2, step // 2, 2, upchan, samples), bf16),
         in_specs=[
             pl.BlockSpec(matrix.shape, lambda i: (0, 0)),
             pl.BlockSpec((parts, beams, step, upchan, samples), lambda i: (0, 0, i, 0, 0)),
         ],
-        out_specs=pl.BlockSpec((step // 2 * beams, 2, upchan, samples), lambda i: (i, 0, 0, 0)),
+        out_specs=pl.BlockSpec((1, beams, 1, step // 2, 2, upchan, samples), lambda i: (i // 2, 0, i % 2, 0, 0, 0, 0)),
         name="filter_power",
     )(matrix, voltages)
+    return power.reshape(coarse // 2 * beams, 2, upchan, samples)
 
 
 def split_of(x):
@@ -144,18 +145,17 @@
     return x, table
 
 
-def dedisperse_kernel(bits_ref, arrived_ref, delays_ref, tables_ref, sent_ref, split_ref, table_ref, stack_ref):
+def dedisperse_kernel(bits_ref, arrived_ref, first_ref, second_ref, sent_ref, split_ref, table_ref, stack_ref):
     sources, _, upchan, samples = arrived_ref.shape
-    trials = delays_ref.shape[1]
+    trials = split_ref.shape[1]
     channels = sources * upchan
     first = bits_ref[BEAM_BIT]
-    for which in range(2):
-        unit = first if which == 0 else 1 - first
+    for in_ref, unit in ((first_ref, first), (second_ref, 1 - first)):
         x = arrived_ref[:, pl.ds(unit, 1)].reshape(channels, samples).astype(f32)
         for inner in range(INNER):
             moved = x if inner == 0 else shifted(x, inner)
             stack_ref[inner * channels : (inner + 1) * channels] = moved.astype(bf16)
-        delays = delays_ref[which]
+        delays = in_ref[:trials]
         total = jnp.zeros((trials, samples), f32)
         for outer in reversed(range(SHIFTS // INNER)):
             onehot = jnp.concatenate(
@@ -169,7 +169,8 @@
                 total = shifted(total, INNER)
             total = total + jnp.dot(onehot, stack_ref[...], preferred_element_type=f32)
         split_ref[unit] = split_of(total)
-        table_ref[unit] = tables_ref[which]
+        packed = in_ref[trials:].astype(f32)
+        table_ref[unit] = jnp.concatenate([packed[:, :samples], packed[:, samples:]], axis=0)
     put_sent(0, bits_ref, split_ref, table_ref, sent_ref)
 
 
@@ -258,7 +259,7 @@
 
         return device
 
-    return jnp.stack([move(x, target(0)), move(x, target(1))])
+    return move(x, target(0)), move(x, target(1))
 
 
 def home(flip, top):
@@ -279,22 +280,19 @@
     bits = (position >> jnp.arange(8, dtype=jnp.int32)) & 1
 
     power = filter_power(voltages)
-    power = power.reshape(freq_count, 2, upchan, samples)
     arrived = lax.all_to_all(power, "freq", split_axis=0, concat_axis=0, tiled=True)
 
-    delays = sub_delays.astype(bf16)
-    delays = gather_units(delays)
-    tables = merge_tables.reshape(3 * levels, trials).astype(f32)
-    tables = jnp.pad(tables, ((0, -3 * levels % 16), (0, 0)))
-    tables = gather_units(tables)
-    rows = tables.shape[1]
+    rows = -(-3 * levels // 16) * 16
+    table = jnp.pad(merge_tables.reshape(3 * levels, trials), ((0, rows - 3 * levels), (0, 0)))
+    table = table.reshape(2, rows // 2, trials).transpose(1, 0, 2).reshape(rows // 2, 2 * trials)
+    first, second = gather_units(jnp.concatenate([sub_delays, table], axis=0).astype(bf16))
 
     message = ((trials + rows, samples), jnp.int16)
     splits, both_tables = ((2, trials, 2 * samples), bf16), ((2, rows, samples), f32)
     split, table = ((trials, 2 * samples), bf16), ((rows, samples), f32)
     stack = pltpu.VMEM((INNER * channels, samples), bf16)
     sent, *both = call(
-        dedisperse_kernel, "dedisperse", (message, splits, both_tables), (bits, arrived, delays, tables), [stack], 24
+        dedisperse_kernel, "dedisperse", (message, splits, both_tables), (bits, arrived, first, second), [stack], 24
     )
     for level in range(levels - 1):
         received = swap(sent, SWAP_BITS[level])

time: 90 us -> 91.9 us (1.021)
  the two profiles are of different devices: /device:TPU:80 before, /device:TPU:72 now
where the time goes in v3:
time: 91.9 us; the launch traced here: 91.6 us
  starting transfers between devices  33.5 us (36%)
  waiting for transfers between devices  33.1 us (36%)
  Pallas kernels  24.7 us (27%)
    ppermute x8, waiting for transfers between devices, move(): lax.ppermute(x, 'freq', [(i, target(i)) for i in range(lax.axis_size('fre...  26.8 us
    ppermute x8, starting transfers between devices, move(): lax.ppermute(x, 'freq', [(i, target(i)) for i in range(lax.axis_size('fre...  22.6 us
    pallas_call x10, Pallas kernels, call(): pl.pallas_call(kernel, out_shape=tuple((jax.ShapeDtypeStruct(shape, dtype...  18.4 us
    all_to_all x1, starting transfers between devices, local(): lax.all_to_all(power, 'freq', split_axis=0, concat_axis=0, tiled=True)  10.9 us
    pallas_call x1, Pallas kernels, filter_power(): pl.pallas_call(filter_kernel, grid=(coarse // step,), out_shape=jax.Shape...  6.38 us
    all_to_all x1, waiting for transfers between devices, local(): lax.all_to_all(power, 'freq', split_axis=0, concat_axis=0, tiled=True)  6.26 us
  transfers between devices with their start and end apart: 9, of which 7 were waited for; matrix products, arithmetic and copies ran while one was open for 0% of the time, Pallas kernels for 5%

profile of v3, /device:TPU:72, one launch (start us, length us, event | category | flops | bytes accessed | tf_op | source)
XLA Modules:
  0.0 91.6 jit_solution(4171899710124846374)
XLA Ops:
  0.0 6.4 %filter_power.1 = bf16[4,2,2,2,2,16,256]{6,5,4,3,2,1,0:T(8,128)(2,1)} custom-call(bf16[64,128]{1,0:T(8,128)(2,1)} %constant.13.clone.matrix_ref, bf16[2,2,32,16,256]{4,3,2,1,0:T(8,128)(2,1)} %volts_ref.1), custom_call_target="tpu_custom_call" | custom-call | tf_op jit(solution)/shard_map/filter_power/pallas_call | solution.py:67
  6.4 0.0 copy-start.1
  6.4 10.9 %all-to-all-start = ((bf16[32,2,16,256]{3,2,1,0:T(8,128)(2,1)}), bf16[32,2,16,256]{3,2,1,0:T(8,128)(2,1)S(1)}, u32[]{:S(2)}, u32[]{:S(2)}) async-start(bf16[32,2,16,256]{3,2,1,0:T(8,128)(2,1)} %bitcast.6), calls=%async_computation | async-start | bytes 1048576 | tf_op jit(solution)/shard_map/all_to_all | solution.py:283
  17.3 0.0 copy-done.1
  17.3 0.0 copy-done
  17.4 3.1 %collective-permute-start.1 = (bf16[264,512]{1,0:T(8,128)(2,1)S(1)}, bf16[264,512]{1,0:T(8,128)(2,1)S(1)}, u32[]{:S(2)}, u32[]{:S(2)}) collective-permute-start(bf16[264,512]{1,0:T(8,128)(2,1)S(1)} %pad_maximum_fusion), channel_id=1, source_target_pairs={{0,32},{8,0},{16,40},{24,8},{32,48},{40,16},{48,56},{56,24},{64,96... | collective-permute-start | bytes 811016 | tf_op jit(solution)/shard_map/ppermute | solution.py:243
  20.5 0.7 collective-permute-start
  21.1 7.2 %collective-permute-done.1.second_ref = bf16[264,512]{1,0:T(8,128)(2,1)S(1)} collective-permute-done((bf16[264,512]{1,0:T(8,128)(2,1)S(1)}, bf16[264,512]{1,0:T(8,128)(2,1)S(1)}, u32[]{:S(2)}, u32[]{:S(2)}) %collective-permute-start.1) | collective-permute-done | bytes 270368 | tf_op jit(solution)/shard_map/ppermute | solution.py:243
  28.3 0.0 collective-permute-done.first_ref
  28.3 6.3 %all-to-all-done.arrived_ref = bf16[32,2,16,256]{3,2,1,0:T(8,128)(2,1)S(1)} async-done(((bf16[32,2,16,256]{3,2,1,0:T(8,128)(2,1)}), bf16[32,2,16,256]{3,2,1,0:T(8,128)(2,1)S(1)}, u32[]{:S(2)}, u32[]{:S(2)}) %all-to-all-start) | async-done | bytes 524320 | tf_op jit(solution)/shard_map/all_to_all | solution.py:283
  34.6 5.8 %dedisperse.1 = (s16[272,256]{1,0:T(8,128)(2,1)S(1)}, bf16[2,256,512]{2,1,0:T(8,128)(2,1)S(1)}, f32[2,16,256]{2,1,0:T(8,128)S(1)}) custom-call(s32[8]{0:T(128)S(1)} %shift-right-arithmetic_and_fusion.bits_ref, bf16[32,2,16,256]{3,2,1,0:T(8,128)(2,1)S(1)} %all-to-all-done.arrived_ref, bf16[264,512]{1,0:T(8,128)(2,1)S(1)} %collective-permute-done.first_ref, ...), custom_call_target="tpu_custom_call" | custom-call | tf_op jit(solution)/shard_map/dedisperse/pallas_call | solution.py:231
  40.3 0.3 collective-permute-start.2
  40.6 1.2 %kept.4 = (bf16[256,512]{1,0:T(8,128)(2,1)S(1)}, f32[16,256]{1,0:T(8,128)S(1)}) custom-call(s32[8]{0:T(128)S(1)} %shift-right-arithmetic_and_fusion.bits_ref, bf16[2,256,512]{2,1,0:T(8,128)(2,1)S(1)} %get-tuple-element.27.split_in_ref, f32[2,16,256]{2,1,0:T(8,128)S(1)} %get-tuple-element.28.table_in_ref), custom_call_target="tpu_custom_call" | custom-call | tf_op jit(solution)/shard_map/kept/pallas_call | solution.py:231
  41.8 0.0 collective-permute-done.2.received_ref
  41.8 1.5 %sent.3 = (s16[272,256]{1,0:T(8,128)(2,1)S(1)}, bf16[2,256,512]{2,1,0:T(8,128)(2,1)S(1)}, f32[2,16,256]{2,1,0:T(8,128)S(1)}) custom-call(s32[8]{0:T(128)S(1)} %shift-right-arithmetic_and_fusion.bits_ref, bf16[256,512]{1,0:T(8,128)(2,1)S(1)} %get-tuple-element.29.kept_split_ref, f32[16,256]{1,0:T(8,128)S(1)} %get-tuple-element.30.kept_table_ref, ...), custom_call_target="tpu_custom_call" | custom-call | tf_op jit(solution)/shard_map/sent/pallas_call | solution.py:231
  43.3 4.0 %collective-permute-start.3 = (s16[272,256]{1,0:T(8,128)(2,1)S(1)}, s16[272,256]{1,0:T(8,128)(2,1)S(1)}, u32[]{:S(2)}, u32[]{:S(2)}) collective-permute-start(s16[272,256]{1,0:T(8,128)(2,1)S(1)} %get-tuple-element.36), channel_id=1, source_target_pairs={{0,16},{8,24},{16,0},{24,8},{32,48},{40,56},{48,32},{56,40},{64,80... | collective-permute-start | bytes 417800 | tf_op jit(solution)/shard_map/ppermute | solution.py:243
  47.3 1.2 %kept.5 = (bf16[256,512]{1,0:T(8,128)(2,1)S(1)}, f32[16,256]{1,0:T(8,128)S(1)}) custom-call(s32[8]{0:T(128)S(1)} %shift-right-arithmetic_and_fusion.bits_ref, bf16[2,256,512]{2,1,0:T(8,128)(2,1)S(1)} %get-tuple-element.32.split_in_ref, f32[2,16,256]{2,1,0:T(8,128)S(1)} %get-tuple-element.33.table_in_ref), custom_call_target="tpu_custom_call" | custom-call | tf_op jit(solution)/shard_map/kept/pallas_call | solution.py:231
  48.5 3.0 %collective-permute-done.3.received_ref = s16[272,256]{1,0:T(8,128)(2,1)S(1)} collective-permute-done((s16[272,256]{1,0:T(8,128)(2,1)S(1)}, s16[272,256]{1,0:T(8,128)(2,1)S(1)}, u32[]{:S(2)}, u32[]{:S(2)}) %collective-permute-start.3) | collective-permute-done | bytes 139296 | tf_op jit(solution)/shard_map/ppermute | solution.py:243
  51.5 1.5 %sent.4 = (s16[272,256]{1,0:T(8,128)(2,1)S(1)}, bf16[2,256,512]{2,1,0:T(8,128)(2,1)S(1)}, f32[2,16,256]{2,1,0:T(8,128)S(1)}) custom-call(s32[8]{0:T(128)S(1)} %shift-right-arithmetic_and_fusion.bits_ref, bf16[256,512]{1,0:T(8,128)(2,1)S(1)} %get-tuple-element.34.kept_split_ref, f32[16,256]{1,0:T(8,128)S(1)} %get-tuple-element.35.kept_table_ref, ...), custom_call_target="tpu_custom_call" | custom-call | tf_op jit(solution)/shard_map/sent/pallas_call | solution.py:231
  52.9 0.8 collective-permute-start.4
  53.8 1.2 %kept.6 = (bf16[256,512]{1,0:T(8,128)(2,1)S(1)}, f32[16,256]{1,0:T(8,128)S(1)}) custom-call(s32[8]{0:T(128)S(1)} %shift-right-arithmetic_and_fusion.bits_ref, bf16[2,256,512]{2,1,0:T(8,128)(2,1)S(1)} %get-tuple-element.37.split_in_ref, f32[2,16,256]{2,1,0:T(8,128)S(1)} %get-tuple-element.38.table_in_ref), custom_call_target="tpu_custom_call" | custom-call | tf_op jit(solution)/shard_map/kept/pallas_call | solution.py:231
  54.9 4.7 %collective-permute-done.4.received_ref = s16[272,256]{1,0:T(8,128)(2,1)S(1)} collective-permute-done((s16[272,256]{1,0:T(8,128)(2,1)S(1)}, s16[272,256]{1,0:T(8,128)(2,1)S(1)}, u32[]{:S(2)}, u32[]{:S(2)}) %collective-permute-start.4) | collective-permute-done | bytes 139296 | tf_op jit(solution)/shard_map/ppermute | solution.py:243
  59.6 1.5 %sent.5 = (s16[272,256]{1,0:T(8,128)(2,1)S(1)}, bf16[2,256,512]{2,1,0:T(8,128)(2,1)S(1)}, f32[2,16,256]{2,1,0:T(8,128)S(1)}) custom-call(s32[8]{0:T(128)S(1)} %shift-right-arithmetic_and_fusion.bits_ref, bf16[256,512]{1,0:T(8,128)(2,1)S(1)} %get-tuple-element.39.kept_split_ref, f32[16,256]{1,0:T(8,128)S(1)} %get-tuple-element.40.kept_table_ref, ...), custom_call_target="tpu_custom_call" | custom-call | tf_op jit(solution)/shard_map/sent/pallas_call | solution.py:231
  61.1 5.5 %collective-permute-start.5 = (s16[272,256]{1,0:T(8,128)(2,1)S(1)}, s16[272,256]{1,0:T(8,128)(2,1)S(1)}, u32[]{:S(2)}, u32[]{:S(2)}) collective-permute-start(s16[272,256]{1,0:T(8,128)(2,1)S(1)} %get-tuple-element.46), channel_id=1, source_target_pairs={{0,128},{8,136},{16,144},{24,152},{32,160},{40,168},{48,176},{56,1... | collective-permute-start | bytes 417800 | tf_op jit(solution)/shard_map/ppermute | solution.py:243
  66.6 1.2 %kept.7 = (bf16[256,512]{1,0:T(8,128)(2,1)S(1)}, f32[16,256]{1,0:T(8,128)S(1)}) custom-call(s32[8]{0:T(128)S(1)} %shift-right-arithmetic_and_fusion.bits_ref, bf16[2,256,512]{2,1,0:T(8,128)(2,1)S(1)} %get-tuple-element.42.split_in_ref, f32[2,16,256]{2,1,0:T(8,128)S(1)} %get-tuple-element.43.table_in_ref), custom_call_target="tpu_custom_call" | custom-call | tf_op jit(solution)/shard_map/kept/pallas_call | solution.py:231
  67.7 4.7 %collective-permute-done.5.received_ref = s16[272,256]{1,0:T(8,128)(2,1)S(1)} collective-permute-done((s16[272,256]{1,0:T(8,128)(2,1)S(1)}, s16[272,256]{1,0:T(8,128)(2,1)S(1)}, u32[]{:S(2)}, u32[]{:S(2)}) %collective-permute-start.5) | collective-permute-done | bytes 139296 | tf_op jit(solution)/shard_map/ppermute | solution.py:243
  72.4 2.4 %peaks.1 = (f32[8,256]{1,0:T(8,128)S(1)}, f32[8,256]{1,0:T(8,128)S(1)}) custom-call(s32[8]{0:T(128)S(1)} %shift-right-arithmetic_and_fusion.bits_ref, bf16[256,512]{1,0:T(8,128)(2,1)S(1)} %get-tuple-element.44.kept_split_ref, f32[16,256]{1,0:T(8,128)S(1)} %get-tuple-element.45.kept_table_ref, s16[272,256]{1,0:T(8,128)(2,1)S(1)} %collective-permute-done.5.received_ref), custom_call_target="tpu_custom_call" | custom-call | tf_op jit(solution)/shard_map/peaks/pallas_call | solution.py:231
  74.8 7.4 %collective-permute-start.6 = (f32[8,256]{1,0:T(8,128)S(1)}, f32[8,256]{1,0:T(8,128)S(1)}, u32[]{:S(2)}, u32[]{:S(2)}) collective-permute-start(f32[8,256]{1,0:T(8,128)S(1)} %get-tuple-element.47), channel_id=1, source_target_pairs={{0,0},{8,8},{16,16},{24,24},{32,128},{40,136},{48,144},{56,152},{6... | collective-permute-start | bytes 24584 | tf_op jit(solution)/shard_map/ppermute | solution.py:243
  82.2 0.9 collective-permute-start.7
  83.1 0.4 collective-permute-done.6.first_ref
  83.5 6.9 %collective-permute-done.7.second_ref = f32[8,256]{1,0:T(8,128)S(1)} collective-permute-done((f32[8,256]{1,0:T(8,128)S(1)}, f32[8,256]{1,0:T(8,128)S(1)}, u32[]{:S(2)}, u32[]{:S(2)}) %collective-permute-start.7) | collective-permute-done | bytes 8224 | tf_op jit(solution)/shard_map/ppermute | solution.py:243
  90.4 1.1 %join.1 = f32[2,8,256]{2,1,0:T(8,128)} custom-call(s32[8]{0:T(128)S(1)} %shift-right-arithmetic_and_fusion.bits_ref, f32[8,256]{1,0:T(8,128)S(1)} %collective-permute-done.6.first_ref, f32[8,256]{1,0:T(8,128)S(1)} %collective-permute-done.7.second_ref), custom_call_target="tpu_custom_call" | custom-call | tf_op jit(solution)/shard_map/join/pallas_call | solution.py:231
  (7 shorter events, 0.1 us)
Async XLA Ops:
  6.4 10.9 %copy-start.1 = (s32[5,3,256]{2,1,0:T(4,128)S(1)}, s32[5,3,256]{2,1,0:T(4,128)}, u32[]{:S(2)}) copy-start(s32[5,3,256]{2,1,0:T(4,128)} %param.6) | copy-start | bytes 46084
  6.4 10.9 %copy-start = (s32[256,512]{1,0:T(8,128)S(1)}, s32[256,512]{1,0:T(8,128)}, u32[]{:S(2)}) copy-start(s32[256,512]{1,0:T(8,128)} %param.5) | copy-start | bytes 1572868
  6.4 28.2 %all-to-all-start = ((bf16[32,2,16,256]{3,2,1,0:T(8,128)(2,1)}), bf16[32,2,16,256]{3,2,1,0:T(8,128)(2,1)S(1)}, u32[]{:S(2)}, u32[]{:S(2)}) async-start(bf16[32,2,16,256]{3,2,1,0:T(8,128)(2,1)} %bitcast.6), calls=%async_computation | async-start | bytes 1048576 | tf_op jit(solution)/shard_map/all_to_all | solution.py:283
  17.4 10.9 %collective-permute-start.1 = (bf16[264,512]{1,0:T(8,128)(2,1)S(1)}, bf16[264,512]{1,0:T(8,128)(2,1)S(1)}, u32[]{:S(2)}, u32[]{:S(2)}) collective-permute-start(bf16[264,512]{1,0:T(8,128)(2,1)S(1)} %pad_maximum_fusion), channel_id=1, source_target_pairs={{0,32},{8,0},{16,40},{24,8},{32,48},{40,16},{48,56},{56,24},{64,96... | collective-permute-start | bytes 811016 | tf_op jit(solution)/shard_map/ppermute | solution.py:243
  20.5 7.8 %collective-permute-start = (bf16[264,512]{1,0:T(8,128)(2,1)S(1)}, bf16[264,512]{1,0:T(8,128)(2,1)S(1)}, u32[]{:S(2)}, u32[]{:S(2)}) collective-permute-start(bf16[264,512]{1,0:T(8,128)(2,1)S(1)} %pad_maximum_fusion), channel_id=1, source_target_pairs={{0,0},{8,32},{16,8},{24,40},{32,16},{40,48},{48,24},{56,56},{64,64... | collective-permute-start | bytes 811016 | tf_op jit(solution)/shard_map/ppermute | solution.py:243
  40.3 1.5 %collective-permute-start.2 = (s16[272,256]{1,0:T(8,128)(2,1)S(1)}, s16[272,256]{1,0:T(8,128)(2,1)S(1)}, u32[]{:S(2)}, u32[]{:S(2)}) collective-permute-start(s16[272,256]{1,0:T(8,128)(2,1)S(1)} %get-tuple-element.31), channel_id=1, source_target_pairs={{0,8},{8,0},{16,24},{24,16},{32,40},{40,32},{48,56},{56,48},{64,72... | collective-permute-start | bytes 417800 | tf_op jit(solution)/shard_map/ppermute | solution.py:243
  43.3 8.2 %collective-permute-start.3 = (s16[272,256]{1,0:T(8,128)(2,1)S(1)}, s16[272,256]{1,0:T(8,128)(2,1)S(1)}, u32[]{:S(2)}, u32[]{:S(2)}) collective-permute-start(s16[272,256]{1,0:T(8,128)(2,1)S(1)} %get-tuple-element.36), channel_id=1, source_target_pairs={{0,16},{8,24},{16,0},{24,8},{32,48},{40,56},{48,32},{56,40},{64,80... | collective-permute-start | bytes 417800 | tf_op jit(solution)/shard_map/ppermute | solution.py:243
  52.9 6.7 %collective-permute-start.4 = (s16[272,256]{1,0:T(8,128)(2,1)S(1)}, s16[272,256]{1,0:T(8,128)(2,1)S(1)}, u32[]{:S(2)}, u32[]{:S(2)}) collective-permute-start(s16[272,256]{1,0:T(8,128)(2,1)S(1)} %get-tuple-element.41), channel_id=1, source_target_pairs={{0,64},{8,72},{16,80},{24,88},{32,96},{40,104},{48,112},{56,120},{... | collective-permute-start | bytes 417800 | tf_op jit(solution)/shard_map/ppermute | solution.py:243
  61.1 11.3 %collective-permute-start.5 = (s16[272,256]{1,0:T(8,128)(2,1)S(1)}, s16[272,256]{1,0:T(8,128)(2,1)S(1)}, u32[]{:S(2)}, u32[]{:S(2)}) collective-permute-start(s16[272,256]{1,0:T(8,128)(2,1)S(1)} %get-tuple-element.46), channel_id=1, source_target_pairs={{0,128},{8,136},{16,144},{24,152},{32,160},{40,168},{48,176},{56,1... | collective-permute-start | bytes 417800 | tf_op jit(solution)/shard_map/ppermute | solution.py:243
  74.8 8.7 %collective-permute-start.6 = (f32[8,256]{1,0:T(8,128)S(1)}, f32[8,256]{1,0:T(8,128)S(1)}, u32[]{:S(2)}, u32[]{:S(2)}) collective-permute-start(f32[8,256]{1,0:T(8,128)S(1)} %get-tuple-element.47), channel_id=1, source_target_pairs={{0,0},{8,8},{16,16},{24,24},{32,128},{40,136},{48,144},{56,152},{6... | collective-permute-start | bytes 24584 | tf_op jit(solution)/shard_map/ppermute | solution.py:243
  82.2 8.2 %collective-permute-start.7 = (f32[8,256]{1,0:T(8,128)S(1)}, f32[8,256]{1,0:T(8,128)S(1)}, u32[]{:S(2)}, u32[]{:S(2)}) collective-permute-start(f32[8,256]{1,0:T(8,128)S(1)} %get-tuple-element.48), channel_id=1, source_target_pairs={{0,128},{8,136},{16,144},{24,152},{32,0},{40,8},{48,16},{56,24},{6... | collective-permute-start | bytes 24584 | tf_op jit(solution)/shard_map/ppermute | solution.py:243

commit v4 on v3

--- a/solution.py
+++ b/solution.py
@@ -14,8 +14,8 @@
 SHIFTS = 32
 INNER = 4
 
-BEAM_BIT = 2
-SWAP_BITS = (0, 1, 3, 4)
+BEAM_BIT = 0
+SWAP_BITS = (1, 2, 3, 4)
 
 epsilon = 1e-06
 f32 = jnp.float32
@@ -45,37 +45,58 @@
     return jnp.where(lane >= amount, pltpu.roll(x, amount, 1), 0.0)
 
 
-def filter_kernel(matrix_ref, volts_ref, out_ref):
-    _, beams, count, upchan, samples = volts_ref.shape
+def filter_kernel(matrix_hbm, volts_hbm, out_hbm, matrix_ref, volts_ref, out_ref, in_sems, out_sems):
+    chunks, _, beams, count, upchan, samples = volts_ref.shape
+    matrix_copy = pltpu.make_async_copy(matrix_hbm, matrix_ref, in_sems.at[chunks])
+    matrix_copy.start()
+    loads, stores = [], []
+    for chunk in range(chunks):
+        source = volts_hbm.at[:, :, pl.ds(chunk * count, count)]
+        loads.append(pltpu.make_async_copy(source, volts_ref.at[chunk], in_sems.at[chunk]))
+        target = out_hbm.at[pl.ds(chunk * count // 2 * beams, count // 2 * beams)]
+        stores.append(pltpu.make_async_copy(out_ref.at[chunk], target, out_sems.at[chunk]))
+        loads[chunk].start()
+    matrix_copy.wait()
     matrix = matrix_ref[...]
     rows = 2 * upchan
-    for beam in range(beams):
+    low = (1 << BEAM_BIT) - 1
+    for chunk in range(chunks):
+        loads[chunk].wait()
         for q in range(count):
-            x = volts_ref[:, beam, q].astype(f32).reshape(rows, samples)
-            taps = [x] + [shifted(x, tap) for tap in range(1, TAPS)]
-            stacked = jnp.concatenate(taps, axis=0).astype(bf16)
-            y = jnp.dot(matrix, stacked, preferred_element_type=f32)
-            y = y[:rows] + y[rows:]
-            power = y[:upchan] * y[:upchan] + y[upchan:] * y[upchan:]
-            out_ref[0, beam, 0, q // 2, q % 2] = power.astype(bf16)
+            for beam in range(beams):
+                x = volts_ref[chunk, :, beam, q].astype(f32).reshape(rows, samples)
+                taps = [x] + [shifted(x, tap) for tap in range(1, TAPS)]
+                stacked = jnp.concatenate(taps, axis=0).astype(bf16)
+                y = jnp.dot(matrix, stacked, preferred_element_type=f32)
+                y = y[:rows] + y[rows:]
+                power = y[:upchan] * y[:upchan] + y[upchan:] * y[upchan:]
+                half = q // 2
+                place = half & low | beam << BEAM_BIT | half >> BEAM_BIT << (BEAM_BIT + 1)
+                out_ref[chunk, place, q % 2] = power.astype(bf16)
+        stores[chunk].start()
+    for store in stores:
+        store.wait()
 
 
 def filter_power(voltages):
     parts, beams, coarse, upchan, samples = voltages.shape
-    step = 1 << BEAM_BIT
+    chunks = 4
+    count = coarse // chunks
     matrix = jnp.asarray(filter_matrix(upchan))
-    power = pl.pallas_call(
+    return pl.pallas_call(
         filter_kernel,
-        grid=(coarse // step,),
-        out_shape=jax.ShapeDtypeStruct((coarse // step // 2, beams, 2, step // 2, 2, upchan, samples), bf16),
-        in_specs=[
-            pl.BlockSpec(matrix.shape, lambda i: (0, 0)),
-            pl.BlockSpec((parts, beams, step, upchan, samples), lambda i: (0, 0, i, 0, 0)),
+        out_shape=jax.ShapeDtypeStruct((coarse // 2 * beams, 2, upchan, samples), bf16),
+        in_specs=[pl.BlockSpec(memory_space=pl.ANY), pl.BlockSpec(memory_space=pl.ANY)],
+        out_specs=pl.BlockSpec(memory_space=pl.ANY),
+        scratch_shapes=[
+            pltpu.VMEM(matrix.shape, bf16),
+            pltpu.VMEM((chunks, parts, beams, count, upchan, samples), bf16),
+            pltpu.VMEM((chunks, count // 2 * beams, 2, upchan, samples), bf16),
+            pltpu.SemaphoreType.DMA((chunks + 1,)),
+            pltpu.SemaphoreType.DMA((chunks,)),
         ],
-        out_specs=pl.BlockSpec((1, beams, 1, step // 2, 2, upchan, samples), lambda i: (i // 2, 0, i % 2, 0, 0, 0, 0)),
         name="filter_power",
     )(matrix, voltages)
-    return power.reshape(coarse // 2 * beams, 2, upchan, samples)
 
 
 def split_of(x):
@@ -198,29 +219,35 @@
     put_sent(level, bits_ref, split_ref, table_ref, sent_ref)
 
 
-def peaks_kernel(level, bits_ref, kept_split_ref, kept_table_ref, received_ref, first_ref, second_ref, split_ref, table_ref):
+def unit_peaks(merged):
+    series = merged.T
+    samples = series.shape[0]
+    mean = jnp.sum(series, axis=0, keepdims=True) * (1.0 / samples)
+    centred = series - mean
+    variance = jnp.sum(centred * centred, axis=0, keepdims=True) * (1.0 / samples)
+    boxcar = centred * lax.rsqrt(variance + epsilon)
+    peaks = [jnp.max(boxcar, axis=0, keepdims=True)]
+    width = 1
+    for _ in range(1, WIDTHS):
+        row = lax.broadcasted_iota(jnp.int32, boxcar.shape, 0)
+        boxcar = boxcar + jnp.where(row >= width, pltpu.roll(boxcar, width, 0), 0.0)
+        width *= 2
+        peaks.append(jnp.max(boxcar, axis=0, keepdims=True) * (1.0 / math.sqrt(width)))
+    return jnp.concatenate(peaks, axis=0)
+
+
+def sent_peaks_kernel(level, bits_ref, kept_split_ref, kept_table_ref, received_ref, peaks_ref, split_ref, table_ref):
     load_units(bits_ref[SWAP_BITS[level - 1]], kept_split_ref, kept_table_ref, received_ref, split_ref, table_ref)
-    for out_ref, unit in ((first_ref, bits_ref[BEAM_BIT]), (second_ref, 1 - bits_ref[BEAM_BIT])):
-        merged = merge_unit(split_ref, table_ref[unit], level)
-        series = merged.T
-        samples = series.shape[0]
-        mean = jnp.sum(series, axis=0, keepdims=True) * (1.0 / samples)
-        centred = series - mean
-        variance = jnp.sum(centred * centred, axis=0, keepdims=True) * (1.0 / samples)
-        boxcar = centred * lax.rsqrt(variance + epsilon)
-        peaks = [jnp.max(boxcar, axis=0, keepdims=True)]
-        width = 1
-        for _ in range(1, WIDTHS):
-            row = lax.broadcasted_iota(jnp.int32, boxcar.shape, 0)
-            boxcar = boxcar + jnp.where(row >= width, pltpu.roll(boxcar, width, 0), 0.0)
-            width *= 2
-            peaks.append(jnp.max(boxcar, axis=0, keepdims=True) * (1.0 / math.sqrt(width)))
-        out_ref[...] = jnp.concatenate(peaks, axis=0)
-
-
-def join_kernel(level, bits_ref, first_ref, second_ref, out_ref):
-    out_ref[bits_ref[level]] = first_ref[...]
-    out_ref[1 - bits_ref[level]] = second_ref[...]
+    peaks_ref[...] = unit_peaks(merge_unit(split_ref, table_ref[1 - bits_ref[BEAM_BIT]], level))
+
+
+def kept_peaks_kernel(level, bits_ref, split_ref, table_ref, peaks_ref):
+    peaks_ref[...] = unit_peaks(merge_unit(split_ref, table_ref[bits_ref[BEAM_BIT]], level))
+
+
+def join_kernel(bits_ref, kept_ref, received_ref, out_ref):
+    out_ref[bits_ref[BEAM_BIT]] = kept_ref[...]
+    out_ref[1 - bits_ref[BEAM_BIT]] = received_ref[...]
 
 
 VMEM = pl.BlockSpec(memory_space=pltpu.VMEM)
@@ -240,7 +267,8 @@
 
 
 def move(x, target):
-    return lax.ppermute(x, "freq", [(i, target(i)) for i in range(lax.axis_size("freq"))])
+    pairs = [(i, target(i)) for i in range(lax.axis_size("freq"))]
+    return x if all(i == j for i, j in pairs) else lax.ppermute(x, "freq", pairs)
 
 
 def swap(x, bit):
@@ -262,10 +290,10 @@
     return move(x, target(0)), move(x, target(1))
 
 
-def home(flip, top):
+def home(top):
     def device(d):
         low = d & (1 << BEAM_BIT) - 1
-        return low | d >> (BEAM_BIT + 1) << BEAM_BIT | (bit(d, BEAM_BIT) ^ flip) << top
+        return low | d >> (BEAM_BIT + 1) << BEAM_BIT | bit(d, BEAM_BIT) << top
 
     return device
 
@@ -302,14 +330,13 @@
                 functools.partial(sent_kernel, level + 1), "sent", (message, splits, both_tables), (bits, *kept, received)
             )
     peak = ((WIDTHS, trials), f32)
-    scratch = [pltpu.VMEM(*splits), pltpu.VMEM(*both_tables)]
-    first, second = call(
-        functools.partial(peaks_kernel, levels - 1), "peaks", (peak, peak), (bits, *kept, received), scratch
+    sent, *both = call(
+        functools.partial(sent_peaks_kernel, levels - 1), "sent_peaks", (peak, splits, both_tables), (bits, *kept, received)
     )
-    first, second = move(first, home(0, levels - 1)), move(second, home(1, levels - 1))
-    return call(
-        functools.partial(join_kernel, levels - 1), "join", (((2, WIDTHS, trials), f32),), (bits, first, second)
-    )[0]
+    received = swap(sent, BEAM_BIT)
+    kept = call(functools.partial(kept_peaks_kernel, levels - 1), "kept_peaks", (peak,), (bits, *both))
+    peaks = call(join_kernel, "join", (((2, WIDTHS, trials), f32),), (bits, *kept, received))[0]
+    return move(peaks, home(levels - 1))
 
 
 def solution(mesh):

time: 91.9 us -> 87 us (0.947)
  the two profiles are of different devices: /device:TPU:72 before, /device:TPU:1 now
where the time goes in v4:
time: 87 us; the launch traced here: 86.7 us
  waiting for transfers between devices  43.3 us (50%)
  Pallas kernels  22.2 us (26%)
  starting transfers between devices  20.3 us (23%)
    ppermute x7, waiting for transfers between devices, move(): lax.ppermute(x, 'freq', pairs)  26.9 us
    pallas_call x11, Pallas kernels, call(): pl.pallas_call(kernel, out_shape=tuple((jax.ShapeDtypeStruct(shape, dtype...  18.7 us
    all_to_all x1, waiting for transfers between devices, local(): lax.all_to_all(power, 'freq', split_axis=0, concat_axis=0, tiled=True)  16.4 us
    all_to_all x1, starting transfers between devices, local(): lax.all_to_all(power, 'freq', split_axis=0, concat_axis=0, tiled=True)  12.7 us
    ppermute x7, starting transfers between devices, move(): lax.ppermute(x, 'freq', pairs)  7.57 us
    pallas_call x1, Pallas kernels, filter_power(): pl.pallas_call(filter_kernel, out_shape=jax.ShapeDtypeStruct((coarse // 2...  3.46 us
  transfers between devices with their start and end apart: 8, of which 7 were waited for; matrix products, arithmetic and copies ran while one was open for 0% of the time, Pallas kernels for 7%

profile of v4, /device:TPU:1, one launch (start us, length us, event | category | flops | bytes accessed | tf_op | source)
XLA Modules:
  0.0 86.7 jit_solution(14837534888249095945)
XLA Ops:
  0.0 3.5 %filter_power.1 = bf16[32,2,16,256]{3,2,1,0:T(8,128)(2,1)} custom-call(bf16[64,128]{1,0:T(8,128)(2,1)} %constant.13.clone.matrix_hbm, bf16[2,2,32,16,256]{4,3,2,1,0:T(8,128)(2,1)} %volts_hbm.1), custom_call_target="tpu_custom_call" | custom-call | tf_op jit(solution)/shard_map/filter_power/pallas_call | solution.py:86
  3.5 0.0 copy-start.1
  3.5 0.0 copy-start
  3.5 12.7 %all-to-all-start = ((bf16[32,2,16,256]{3,2,1,0:T(8,128)(2,1)}), bf16[32,2,16,256]{3,2,1,0:T(8,128)(2,1)S(1)}, u32[]{:S(2)}, u32[]{:S(2)}) async-start(bf16[32,2,16,256]{3,2,1,0:T(8,128)(2,1)} %filter_power.1), calls=%async_computation | async-start | bytes 1048576 | tf_op jit(solution)/shard_map/all_to_all | solution.py:311
  16.2 0.0 copy-done.1
  16.4 0.3 collective-permute-start
  16.7 1.3 %collective-permute-done.second_ref = bf16[264,512]{1,0:T(8,128)(2,1)S(1)} collective-permute-done((bf16[264,512]{1,0:T(8,128)(2,1)S(1)}, bf16[264,512]{1,0:T(8,128)(2,1)S(1)}, u32[]{:S(2)}, u32[]{:S(2)}) %collective-permute-start) | collective-permute-done | bytes 270368 | tf_op jit(solution)/shard_map/ppermute | solution.py:271
  18.0 16.4 %all-to-all-done.arrived_ref = bf16[32,2,16,256]{3,2,1,0:T(8,128)(2,1)S(1)} async-done(((bf16[32,2,16,256]{3,2,1,0:T(8,128)(2,1)}), bf16[32,2,16,256]{3,2,1,0:T(8,128)(2,1)S(1)}, u32[]{:S(2)}, u32[]{:S(2)}) %all-to-all-start) | async-done | bytes 524320 | tf_op jit(solution)/shard_map/all_to_all | solution.py:311
  34.4 5.8 %dedisperse.1 = (s16[272,256]{1,0:T(8,128)(2,1)S(1)}, bf16[2,256,512]{2,1,0:T(8,128)(2,1)S(1)}, f32[2,16,256]{2,1,0:T(8,128)S(1)}) custom-call(s32[8]{0:T(128)S(1)} %shift-right-arithmetic_and_fusion.bits_ref, bf16[32,2,16,256]{3,2,1,0:T(8,128)(2,1)S(1)} %all-to-all-done.arrived_ref, bf16[264,512]{1,0:T(8,128)(2,1)S(1)} %pad_maximum_fusion.first_ref, ...), custom_call_target="tpu_custom_call" | custom-call | tf_op jit(solution)/shard_map/dedisperse/pallas_call | solution.py:258
  40.2 0.1 collective-permute-start.1
  40.3 1.2 %kept.4 = (bf16[256,512]{1,0:T(8,128)(2,1)S(1)}, f32[16,256]{1,0:T(8,128)S(1)}) custom-call(s32[8]{0:T(128)S(1)} %shift-right-arithmetic_and_fusion.bits_ref, bf16[2,256,512]{2,1,0:T(8,128)(2,1)S(1)} %get-tuple-element.28.split_in_ref, f32[2,16,256]{2,1,0:T(8,128)S(1)} %get-tuple-element.29.table_in_ref), custom_call_target="tpu_custom_call" | custom-call | tf_op jit(solution)/shard_map/kept/pallas_call | solution.py:258
  41.5 3.9 %collective-permute-done.1.received_ref = s16[272,256]{1,0:T(8,128)(2,1)S(1)} collective-permute-done((s16[272,256]{1,0:T(8,128)(2,1)S(1)}, s16[272,256]{1,0:T(8,128)(2,1)S(1)}, u32[]{:S(2)}, u32[]{:S(2)}) %collective-permute-start.1) | collective-permute-done | bytes 139296 | tf_op jit(solution)/shard_map/ppermute | solution.py:271
  45.3 1.5 %sent.3 = (s16[272,256]{1,0:T(8,128)(2,1)S(1)}, bf16[2,256,512]{2,1,0:T(8,128)(2,1)S(1)}, f32[2,16,256]{2,1,0:T(8,128)S(1)}) custom-call(s32[8]{0:T(128)S(1)} %shift-right-arithmetic_and_fusion.bits_ref, bf16[256,512]{1,0:T(8,128)(2,1)S(1)} %get-tuple-element.30.kept_split_ref, f32[16,256]{1,0:T(8,128)S(1)} %get-tuple-element.31.kept_table_ref, ...), custom_call_target="tpu_custom_call" | custom-call | tf_op jit(solution)/shard_map/sent/pallas_call | solution.py:258
  46.8 0.3 collective-permute-start.2
  47.1 1.2 %kept.5 = (bf16[256,512]{1,0:T(8,128)(2,1)S(1)}, f32[16,256]{1,0:T(8,128)S(1)}) custom-call(s32[8]{0:T(128)S(1)} %shift-right-arithmetic_and_fusion.bits_ref, bf16[2,256,512]{2,1,0:T(8,128)(2,1)S(1)} %get-tuple-element.33.split_in_ref, f32[2,16,256]{2,1,0:T(8,128)S(1)} %get-tuple-element.34.table_in_ref), custom_call_target="tpu_custom_call" | custom-call | tf_op jit(solution)/shard_map/kept/pallas_call | solution.py:258
  48.2 5.0 %collective-permute-done.2.received_ref = s16[272,256]{1,0:T(8,128)(2,1)S(1)} collective-permute-done((s16[272,256]{1,0:T(8,128)(2,1)S(1)}, s16[272,256]{1,0:T(8,128)(2,1)S(1)}, u32[]{:S(2)}, u32[]{:S(2)}) %collective-permute-start.2) | collective-permute-done | bytes 139296 | tf_op jit(solution)/shard_map/ppermute | solution.py:271
  53.3 1.5 %sent.4 = (s16[272,256]{1,0:T(8,128)(2,1)S(1)}, bf16[2,256,512]{2,1,0:T(8,128)(2,1)S(1)}, f32[2,16,256]{2,1,0:T(8,128)S(1)}) custom-call(s32[8]{0:T(128)S(1)} %shift-right-arithmetic_and_fusion.bits_ref, bf16[256,512]{1,0:T(8,128)(2,1)S(1)} %get-tuple-element.35.kept_split_ref, f32[16,256]{1,0:T(8,128)S(1)} %get-tuple-element.36.kept_table_ref, ...), custom_call_target="tpu_custom_call" | custom-call | tf_op jit(solution)/shard_map/sent/pallas_call | solution.py:258
  54.8 0.6 collective-permute-start.3
  55.4 1.2 %kept.6 = (bf16[256,512]{1,0:T(8,128)(2,1)S(1)}, f32[16,256]{1,0:T(8,128)S(1)}) custom-call(s32[8]{0:T(128)S(1)} %shift-right-arithmetic_and_fusion.bits_ref, bf16[2,256,512]{2,1,0:T(8,128)(2,1)S(1)} %get-tuple-element.38.split_in_ref, f32[2,16,256]{2,1,0:T(8,128)S(1)} %get-tuple-element.39.table_in_ref), custom_call_target="tpu_custom_call" | custom-call | tf_op jit(solution)/shard_map/kept/pallas_call | solution.py:258
  56.5 7.6 %collective-permute-done.3.received_ref = s16[272,256]{1,0:T(8,128)(2,1)S(1)} collective-permute-done((s16[272,256]{1,0:T(8,128)(2,1)S(1)}, s16[272,256]{1,0:T(8,128)(2,1)S(1)}, u32[]{:S(2)}, u32[]{:S(2)}) %collective-permute-start.3) | collective-permute-done | bytes 139296 | tf_op jit(solution)/shard_map/ppermute | solution.py:271
  64.1 1.5 %sent.5 = (s16[272,256]{1,0:T(8,128)(2,1)S(1)}, bf16[2,256,512]{2,1,0:T(8,128)(2,1)S(1)}, f32[2,16,256]{2,1,0:T(8,128)S(1)}) custom-call(s32[8]{0:T(128)S(1)} %shift-right-arithmetic_and_fusion.bits_ref, bf16[256,512]{1,0:T(8,128)(2,1)S(1)} %get-tuple-element.40.kept_split_ref, f32[16,256]{1,0:T(8,128)S(1)} %get-tuple-element.41.kept_table_ref, ...), custom_call_target="tpu_custom_call" | custom-call | tf_op jit(solution)/shard_map/sent/pallas_call | solution.py:258
  65.6 0.6 collective-permute-start.4
  66.2 1.2 %kept.7 = (bf16[256,512]{1,0:T(8,128)(2,1)S(1)}, f32[16,256]{1,0:T(8,128)S(1)}) custom-call(s32[8]{0:T(128)S(1)} %shift-right-arithmetic_and_fusion.bits_ref, bf16[2,256,512]{2,1,0:T(8,128)(2,1)S(1)} %get-tuple-element.43.split_in_ref, f32[2,16,256]{2,1,0:T(8,128)S(1)} %get-tuple-element.44.table_in_ref), custom_call_target="tpu_custom_call" | custom-call | tf_op jit(solution)/shard_map/kept/pallas_call | solution.py:258
  67.4 8.3 %collective-permute-done.4.received_ref = s16[272,256]{1,0:T(8,128)(2,1)S(1)} collective-permute-done((s16[272,256]{1,0:T(8,128)(2,1)S(1)}, s16[272,256]{1,0:T(8,128)(2,1)S(1)}, u32[]{:S(2)}, u32[]{:S(2)}) %collective-permute-start.4) | collective-permute-done | bytes 139296 | tf_op jit(solution)/shard_map/ppermute | solution.py:271
  75.7 1.7 %sent_peaks.1 = (f32[8,256]{1,0:T(8,128)S(1)}, bf16[2,256,512]{2,1,0:T(8,128)(2,1)S(1)}, f32[2,16,256]{2,1,0:T(8,128)S(1)}) custom-call(s32[8]{0:T(128)S(1)} %shift-right-arithmetic_and_fusion.bits_ref, bf16[256,512]{1,0:T(8,128)(2,1)S(1)} %get-tuple-element.45.kept_split_ref, f32[16,256]{1,0:T(8,128)S(1)} %get-tuple-element.46.kept_table_ref, ...), custom_call_target="tpu_custom_call" | custom-call | tf_op jit(solution)/shard_map/sent_peaks/pallas_call | solution.py:258
  77.4 1.3 %collective-permute-start.5 = (f32[8,256]{1,0:T(8,128)S(1)}, f32[8,256]{1,0:T(8,128)S(1)}, u32[]{:S(2)}, u32[]{:S(2)}) collective-permute-start(f32[8,256]{1,0:T(8,128)S(1)} %get-tuple-element.50), channel_id=1, source_target_pairs={{0,8},{8,0},{16,24},{24,16},{32,40},{40,32},{48,56},{56,48},{64,72... | collective-permute-start | bytes 24584 | tf_op jit(solution)/shard_map/ppermute | solution.py:271
  78.7 1.5 %kept_peaks.1.kept_ref = f32[8,256]{1,0:T(8,128)S(1)} custom-call(s32[8]{0:T(128)S(1)} %shift-right-arithmetic_and_fusion.bits_ref, bf16[2,256,512]{2,1,0:T(8,128)(2,1)S(1)} %get-tuple-element.48.split_ref, f32[2,16,256]{2,1,0:T(8,128)S(1)} %get-tuple-element.49.table_ref), custom_call_target="tpu_custom_call" | custom-call | tf_op jit(solution)/shard_map/kept_peaks/pallas_call | solution.py:258
  80.3 0.0 collective-permute-done.5.received_ref
  80.3 0.5 join.1
  80.8 4.4 %collective-permute-start.6 = (f32[2,8,256]{2,1,0:T(8,128)S(1)}, f32[2,8,256]{2,1,0:T(8,128)S(1)}, u32[]{:S(2)}, u32[]{:S(2)}) collective-permute-start(f32[2,8,256]{2,1,0:T(8,128)S(1)} %join.1), channel_id=1, source_target_pairs={{0,0},{8,128},{16,8},{24,136},{32,16},{40,144},{48,24},{56,152},{6... | collective-permute-start | bytes 49160 | tf_op jit(solution)/shard_map/ppermute | solution.py:271
  85.2 0.8 collective-permute-done.6
  86.1 0.6 copy.6
  (7 shorter events, 0.1 us)
Async XLA Ops:
  3.5 12.8 %copy-start.1 = (s32[5,3,256]{2,1,0:T(4,128)S(1)}, s32[5,3,256]{2,1,0:T(4,128)}, u32[]{:S(2)}) copy-start(s32[5,3,256]{2,1,0:T(4,128)} %param.6) | copy-start | bytes 46084
  3.5 12.8 %copy-start = (s32[256,512]{1,0:T(8,128)S(1)}, s32[256,512]{1,0:T(8,128)}, u32[]{:S(2)}) copy-start(s32[256,512]{1,0:T(8,128)} %param.5) | copy-start | bytes 1572868
  3.5 30.9 %all-to-all-start = ((bf16[32,2,16,256]{3,2,1,0:T(8,128)(2,1)}), bf16[32,2,16,256]{3,2,1,0:T(8,128)(2,1)S(1)}, u32[]{:S(2)}, u32[]{:S(2)}) async-start(bf16[32,2,16,256]{3,2,1,0:T(8,128)(2,1)} %filter_power.1), calls=%async_computation | async-start | bytes 1048576 | tf_op jit(solution)/shard_map/all_to_all | solution.py:311
  16.4 1.6 %collective-permute-start = (bf16[264,512]{1,0:T(8,128)(2,1)S(1)}, bf16[264,512]{1,0:T(8,128)(2,1)S(1)}, u32[]{:S(2)}, u32[]{:S(2)}) collective-permute-start(bf16[264,512]{1,0:T(8,128)(2,1)S(1)} %pad_maximum_fusion.first_ref), channel_id=1, source_target_pairs={{0,8},{8,0},{16,24},{24,16},{32,40},{40,32},{48,56},{56,48},{64,72... | collective-permute-start | bytes 811016 | tf_op jit(solution)/shard_map/ppermute | solution.py:271
  40.2 5.2 %collective-permute-start.1 = (s16[272,256]{1,0:T(8,128)(2,1)S(1)}, s16[272,256]{1,0:T(8,128)(2,1)S(1)}, u32[]{:S(2)}, u32[]{:S(2)}) collective-permute-start(s16[272,256]{1,0:T(8,128)(2,1)S(1)} %get-tuple-element.32), channel_id=1, source_target_pairs={{0,16},{8,24},{16,0},{24,8},{32,48},{40,56},{48,32},{56,40},{64,80... | collective-permute-start | bytes 417800 | tf_op jit(solution)/shard_map/ppermute | solution.py:271
  46.8 6.5 %collective-permute-start.2 = (s16[272,256]{1,0:T(8,128)(2,1)S(1)}, s16[272,256]{1,0:T(8,128)(2,1)S(1)}, u32[]{:S(2)}, u32[]{:S(2)}) collective-permute-start(s16[272,256]{1,0:T(8,128)(2,1)S(1)} %get-tuple-element.37), channel_id=1, source_target_pairs={{0,32},{8,40},{16,48},{24,56},{32,0},{40,8},{48,16},{56,24},{64,96... | collective-permute-start | bytes 417800 | tf_op jit(solution)/shard_map/ppermute | solution.py:271
  54.8 9.4 %collective-permute-start.3 = (s16[272,256]{1,0:T(8,128)(2,1)S(1)}, s16[272,256]{1,0:T(8,128)(2,1)S(1)}, u32[]{:S(2)}, u32[]{:S(2)}) collective-permute-start(s16[272,256]{1,0:T(8,128)(2,1)S(1)} %get-tuple-element.42), channel_id=1, source_target_pairs={{0,64},{8,72},{16,80},{24,88},{32,96},{40,104},{48,112},{56,120},{... | collective-permute-start | bytes 417800 | tf_op jit(solution)/shard_map/ppermute | solution.py:271
  65.6 10.0 %collective-permute-start.4 = (s16[272,256]{1,0:T(8,128)(2,1)S(1)}, s16[272,256]{1,0:T(8,128)(2,1)S(1)}, u32[]{:S(2)}, u32[]{:S(2)}) collective-permute-start(s16[272,256]{1,0:T(8,128)(2,1)S(1)} %get-tuple-element.47), channel_id=1, source_target_pairs={{0,128},{8,136},{16,144},{24,152},{32,160},{40,168},{48,176},{56,1... | collective-permute-start | bytes 417800 | tf_op jit(solution)/shard_map/ppermute | solution.py:271
  77.4 2.9 %collective-permute-start.5 = (f32[8,256]{1,0:T(8,128)S(1)}, f32[8,256]{1,0:T(8,128)S(1)}, u32[]{:S(2)}, u32[]{:S(2)}) collective-permute-start(f32[8,256]{1,0:T(8,128)S(1)} %get-tuple-element.50), channel_id=1, source_target_pairs={{0,8},{8,0},{16,24},{24,16},{32,40},{40,32},{48,56},{56,48},{64,72... | collective-permute-start | bytes 24584 | tf_op jit(solution)/shard_map/ppermute | solution.py:271
  80.8 5.2 %collective-permute-start.6 = (f32[2,8,256]{2,1,0:T(8,128)S(1)}, f32[2,8,256]{2,1,0:T(8,128)S(1)}, u32[]{:S(2)}, u32[]{:S(2)}) collective-permute-start(f32[2,8,256]{2,1,0:T(8,128)S(1)} %join.1), channel_id=1, source_target_pairs={{0,0},{8,128},{16,8},{24,136},{32,16},{40,144},{48,24},{56,152},{6... | collective-permute-start | bytes 49160 | tf_op jit(solution)/shard_map/ppermute | solution.py:271

commit v5 on v4

--- a/solution.py
+++ b/solution.py
@@ -15,7 +15,25 @@
 INNER = 4
 
 BEAM_BIT = 0
-SWAP_BITS = (1, 2, 3, 4)
+PARTNERS = (2, 6, 8, 24)
+
+
+def bit(number, index):
+    return number >> index & 1
+
+
+KEEPS = (
+    lambda d: bit(d, 1) ^ bit(d, 2),
+    lambda d: 1 - bit(d, 1),
+    lambda d: bit(d, 3) ^ bit(d, 4),
+    lambda d: 1 - bit(d, 3),
+    lambda d: bit(d, 0),
+)
+
+
+def home(d):
+    return sum(keep(d) << level for level, keep in enumerate(KEEPS))
+
 
 epsilon = 1e-06
 f32 = jnp.float32
@@ -144,6 +162,8 @@
 
 STEPS = 65534.0
 
+KEEP = 5
+
 
 def put_message(out_ref, x, table):
     trials = x.shape[0]
@@ -170,7 +190,7 @@
     sources, _, upchan, samples = arrived_ref.shape
     trials = split_ref.shape[1]
     channels = sources * upchan
-    first = bits_ref[BEAM_BIT]
+    first = bits_ref[0]
     for in_ref, unit in ((first_ref, first), (second_ref, 1 - first)):
         x = arrived_ref[:, pl.ds(unit, 1)].reshape(channels, samples).astype(f32)
         for inner in range(INNER):
@@ -196,12 +216,12 @@
 
 
 def put_sent(level, bits_ref, split_ref, table_ref, sent_ref):
-    table = table_ref[1 - bits_ref[SWAP_BITS[level]]]
+    table = table_ref[1 - bits_ref[KEEP + level]]
     put_message(sent_ref, merge_unit(split_ref, table, level), table)
 
 
 def kept_kernel(level, bits_ref, split_in_ref, table_in_ref, split_ref, table_ref):
-    table = table_in_ref[bits_ref[SWAP_BITS[level]]]
+    table = table_in_ref[bits_ref[KEEP + level]]
     split_ref[...] = split_of(merge_unit(split_in_ref, table, level))
     table_ref[...] = table
 
@@ -215,7 +235,7 @@
 
 
 def sent_kernel(level, bits_ref, kept_split_ref, kept_table_ref, received_ref, sent_ref, split_ref, table_ref):
-    load_units(bits_ref[SWAP_BITS[level - 1]], kept_split_ref, kept_table_ref, received_ref, split_ref, table_ref)
+    load_units(bits_ref[level], kept_split_ref, kept_table_ref, received_ref, split_ref, table_ref)
     put_sent(level, bits_ref, split_ref, table_ref, sent_ref)
 
 
@@ -237,17 +257,17 @@
 
 
 def sent_peaks_kernel(level, bits_ref, kept_split_ref, kept_table_ref, received_ref, peaks_ref, split_ref, table_ref):
-    load_units(bits_ref[SWAP_BITS[level - 1]], kept_split_ref, kept_table_ref, received_ref, split_ref, table_ref)
-    peaks_ref[...] = unit_peaks(merge_unit(split_ref, table_ref[1 - bits_ref[BEAM_BIT]], level))
+    load_units(bits_ref[level], kept_split_ref, kept_table_ref, received_ref, split_ref, table_ref)
+    peaks_ref[...] = unit_peaks(merge_unit(split_ref, table_ref[1 - bits_ref[KEEP + level]], level))
 
 
 def kept_peaks_kernel(level, bits_ref, split_ref, table_ref, peaks_ref):
-    peaks_ref[...] = unit_peaks(merge_unit(split_ref, table_ref[bits_ref[BEAM_BIT]], level))
+    peaks_ref[...] = unit_peaks(merge_unit(split_ref, table_ref[bits_ref[KEEP + level]], level))
 
 
 def join_kernel(bits_ref, kept_ref, received_ref, out_ref):
-    out_ref[bits_ref[BEAM_BIT]] = kept_ref[...]
-    out_ref[1 - bits_ref[BEAM_BIT]] = received_ref[...]
+    out_ref[bits_ref[0]] = kept_ref[...]
+    out_ref[1 - bits_ref[0]] = received_ref[...]
 
 
 VMEM = pl.BlockSpec(memory_space=pltpu.VMEM)
@@ -271,12 +291,8 @@
     return x if all(i == j for i, j in pairs) else lax.ppermute(x, "freq", pairs)
 
 
-def swap(x, bit):
-    return move(x, lambda i: i ^ (1 << bit))
-
-
-def bit(number, index):
-    return number >> index & 1
+def swap(x, mask):
+    return move(x, lambda i: i ^ mask)
 
 
 def gather_units(x):
@@ -288,14 +304,6 @@
         return device
 
     return move(x, target(0)), move(x, target(1))
-
-
-def home(top):
-    def device(d):
-        low = d & (1 << BEAM_BIT) - 1
-        return low | d >> (BEAM_BIT + 1) << BEAM_BIT | bit(d, BEAM_BIT) << top
-
-    return device
 
 
 def local(voltages, sub_delays, merge_tables):
@@ -305,7 +313,8 @@
     samples = voltages.shape[4]
     upchan = voltages.shape[3]
     position = lax.axis_index("freq")
-    bits = (position >> jnp.arange(8, dtype=jnp.int32)) & 1
+    bits = [bit(position, index) for index in range(levels)] + [keep(position) for keep in KEEPS]
+    bits = jnp.stack(bits + [0] * (16 - len(bits))).astype(jnp.int32)
 
     power = filter_power(voltages)
     arrived = lax.all_to_all(power, "freq", split_axis=0, concat_axis=0, tiled=True)
@@ -323,7 +332,7 @@
         dedisperse_kernel, "dedisperse", (message, splits, both_tables), (bits, arrived, first, second), [stack], 24
     )
     for level in range(levels - 1):
-        received = swap(sent, SWAP_BITS[level])
+        received = swap(sent, PARTNERS[level])
         kept = call(functools.partial(kept_kernel, level), "kept", (split, table), (bits, *both))
         if level < levels - 2:
             sent, *both = call(
@@ -333,10 +342,10 @@
     sent, *both = call(
         functools.partial(sent_peaks_kernel, levels - 1), "sent_peaks", (peak, splits, both_tables), (bits, *kept, received)
     )
-    received = swap(sent, BEAM_BIT)
+    received = swap(sent, 1 << BEAM_BIT)
     kept = call(functools.partial(kept_peaks_kernel, levels - 1), "kept_peaks", (peak,), (bits, *both))
     peaks = call(join_kernel, "join", (((2, WIDTHS, trials), f32),), (bits, *kept, received))[0]
-    return move(peaks, home(levels - 1))
+    return move(peaks, home)
 
 
 def solution(mesh):

time: 87 us -> 85.1 us (0.978)
  starting transfers between devices: 20.3 us -> 16.9 us
  waiting for transfers between devices: 43.3 us -> 44.4 us
    ppermute x7, starting transfers between devices: 7.57 us -> 4.17 us  [move(): lax.ppermute(x, 'freq', pairs)]
    ppermute x7, waiting for transfers between devices: 26.9 us -> 28.1 us  [move(): lax.ppermute(x, 'freq', pairs)]
where the time goes in v5:
time: 85.1 us; the launch traced here: 84.5 us
  waiting for transfers between devices  44.4 us (52%)
  Pallas kernels  22.1 us (26%)
  starting transfers between devices  16.9 us (20%)
    ppermute x7, waiting for transfers between devices, move(): lax.ppermute(x, 'freq', pairs)  28.1 us
    pallas_call x11, Pallas kernels, call(): pl.pallas_call(kernel, out_shape=tuple((jax.ShapeDtypeStruct(shape, dtype...  18.7 us
    all_to_all x1, waiting for transfers between devices, local(): lax.all_to_all(power, 'freq', split_axis=0, concat_axis=0, tiled=True)  16.4 us
    all_to_all x1, starting transfers between devices, local(): lax.all_to_all(power, 'freq', split_axis=0, concat_axis=0, tiled=True)  12.7 us
    ppermute x7, starting transfers between devices, move(): lax.ppermute(x, 'freq', pairs)  4.17 us
    pallas_call x1, Pallas kernels, filter_power(): pl.pallas_call(filter_kernel, out_shape=jax.ShapeDtypeStruct((coarse // 2...  3.46 us
  transfers between devices with their start and end apart: 8, of which 7 were waited for; matrix products, arithmetic and copies ran while one was open for 0% of the time, Pallas kernels for 7%

profile of v5, /device:TPU:1, one launch (start us, length us, event | category | flops | bytes accessed | tf_op | source)
XLA Modules:
  0.0 84.5 jit_solution(13622544149377296496)
XLA Ops:
  0.0 3.5 %filter_power.1 = bf16[32,2,16,256]{3,2,1,0:T(8,128)(2,1)} custom-call(bf16[64,128]{1,0:T(8,128)(2,1)} %constant.22.clone.matrix_hbm, bf16[2,2,32,16,256]{4,3,2,1,0:T(8,128)(2,1)} %volts_hbm.1), custom_call_target="tpu_custom_call" | custom-call | tf_op jit(solution)/shard_map/filter_power/pallas_call | solution.py:104
  3.5 0.0 copy-start.1
  3.5 0.0 copy-start
  3.5 12.7 %all-to-all-start = ((bf16[32,2,16,256]{3,2,1,0:T(8,128)(2,1)}), bf16[32,2,16,256]{3,2,1,0:T(8,128)(2,1)S(1)}, u32[]{:S(2)}, u32[]{:S(2)}) async-start(bf16[32,2,16,256]{3,2,1,0:T(8,128)(2,1)} %filter_power.1), calls=%async_computation | async-start | bytes 1048576 | tf_op jit(solution)/shard_map/all_to_all | solution.py:320
  16.4 0.3 collective-permute-start
  16.7 0.1 stack.40.bits_ref
  16.8 1.2 %collective-permute-done.second_ref = bf16[264,512]{1,0:T(8,128)(2,1)S(1)} collective-permute-done((bf16[264,512]{1,0:T(8,128)(2,1)S(1)}, bf16[264,512]{1,0:T(8,128)(2,1)S(1)}, u32[]{:S(2)}, u32[]{:S(2)}) %collective-permute-start) | collective-permute-done | bytes 270368 | tf_op jit(solution)/shard_map/ppermute | solution.py:291
  18.0 16.4 %all-to-all-done.arrived_ref = bf16[32,2,16,256]{3,2,1,0:T(8,128)(2,1)S(1)} async-done(((bf16[32,2,16,256]{3,2,1,0:T(8,128)(2,1)}), bf16[32,2,16,256]{3,2,1,0:T(8,128)(2,1)S(1)}, u32[]{:S(2)}, u32[]{:S(2)}) %all-to-all-start) | async-done | bytes 524320 | tf_op jit(solution)/shard_map/all_to_all | solution.py:320
  34.4 5.8 %dedisperse.1 = (s16[272,256]{1,0:T(8,128)(2,1)S(1)}, bf16[2,256,512]{2,1,0:T(8,128)(2,1)S(1)}, f32[2,16,256]{2,1,0:T(8,128)S(1)}) custom-call(s32[16]{0:T(128)S(1)} %stack.40.bits_ref, bf16[32,2,16,256]{3,2,1,0:T(8,128)(2,1)S(1)} %all-to-all-done.arrived_ref, bf16[264,512]{1,0:T(8,128)(2,1)S(1)} %pad_maximum_fusion.first_ref, ...), custom_call_target="tpu_custom_call" | custom-call | tf_op jit(solution)/shard_map/dedisperse/pallas_call | solution.py:278
  40.2 0.1 collective-permute-start.1
  40.3 1.2 %kept.4 = (bf16[256,512]{1,0:T(8,128)(2,1)S(1)}, f32[16,256]{1,0:T(8,128)S(1)}) custom-call(s32[16]{0:T(128)S(1)} %stack.40.bits_ref, bf16[2,256,512]{2,1,0:T(8,128)(2,1)S(1)} %get-tuple-element.28.split_in_ref, f32[2,16,256]{2,1,0:T(8,128)S(1)} %get-tuple-element.29.table_in_ref), custom_call_target="tpu_custom_call" | custom-call | tf_op jit(solution)/shard_map/kept/pallas_call | solution.py:278
  41.4 3.9 %collective-permute-done.1.received_ref = s16[272,256]{1,0:T(8,128)(2,1)S(1)} collective-permute-done((s16[272,256]{1,0:T(8,128)(2,1)S(1)}, s16[272,256]{1,0:T(8,128)(2,1)S(1)}, u32[]{:S(2)}, u32[]{:S(2)}) %collective-permute-start.1) | collective-permute-done | bytes 139296 | tf_op jit(solution)/shard_map/ppermute | solution.py:291
  45.3 1.5 %sent.3 = (s16[272,256]{1,0:T(8,128)(2,1)S(1)}, bf16[2,256,512]{2,1,0:T(8,128)(2,1)S(1)}, f32[2,16,256]{2,1,0:T(8,128)S(1)}) custom-call(s32[16]{0:T(128)S(1)} %stack.40.bits_ref, bf16[256,512]{1,0:T(8,128)(2,1)S(1)} %get-tuple-element.30.kept_split_ref, f32[16,256]{1,0:T(8,128)S(1)} %get-tuple-element.31.kept_table_ref, ...), custom_call_target="tpu_custom_call" | custom-call | tf_op jit(solution)/shard_map/sent/pallas_call | solution.py:278
  46.8 1.3 %collective-permute-start.2 = (s16[272,256]{1,0:T(8,128)(2,1)S(1)}, s16[272,256]{1,0:T(8,128)(2,1)S(1)}, u32[]{:S(2)}, u32[]{:S(2)}) collective-permute-start(s16[272,256]{1,0:T(8,128)(2,1)S(1)} %get-tuple-element.37), channel_id=1, source_target_pairs={{0,48},{8,56},{16,32},{24,40},{32,16},{40,24},{48,0},{56,8},{64,11... | collective-permute-start | bytes 417800 | tf_op jit(solution)/shard_map/ppermute | solution.py:291
  48.1 1.2 %kept.5 = (bf16[256,512]{1,0:T(8,128)(2,1)S(1)}, f32[16,256]{1,0:T(8,128)S(1)}) custom-call(s32[16]{0:T(128)S(1)} %stack.40.bits_ref, bf16[2,256,512]{2,1,0:T(8,128)(2,1)S(1)} %get-tuple-element.33.split_in_ref, f32[2,16,256]{2,1,0:T(8,128)S(1)} %get-tuple-element.34.table_in_ref), custom_call_target="tpu_custom_call" | custom-call | tf_op jit(solution)/shard_map/kept/pallas_call | solution.py:278
  49.2 3.7 %collective-permute-done.2.received_ref = s16[272,256]{1,0:T(8,128)(2,1)S(1)} collective-permute-done((s16[272,256]{1,0:T(8,128)(2,1)S(1)}, s16[272,256]{1,0:T(8,128)(2,1)S(1)}, u32[]{:S(2)}, u32[]{:S(2)}) %collective-permute-start.2) | collective-permute-done | bytes 139296 | tf_op jit(solution)/shard_map/ppermute | solution.py:291
  53.0 1.5 %sent.4 = (s16[272,256]{1,0:T(8,128)(2,1)S(1)}, bf16[2,256,512]{2,1,0:T(8,128)(2,1)S(1)}, f32[2,16,256]{2,1,0:T(8,128)S(1)}) custom-call(s32[16]{0:T(128)S(1)} %stack.40.bits_ref, bf16[256,512]{1,0:T(8,128)(2,1)S(1)} %get-tuple-element.35.kept_split_ref, f32[16,256]{1,0:T(8,128)S(1)} %get-tuple-element.36.kept_table_ref, ...), custom_call_target="tpu_custom_call" | custom-call | tf_op jit(solution)/shard_map/sent/pallas_call | solution.py:278
  54.4 0.6 collective-permute-start.3
  55.1 1.2 %kept.6 = (bf16[256,512]{1,0:T(8,128)(2,1)S(1)}, f32[16,256]{1,0:T(8,128)S(1)}) custom-call(s32[16]{0:T(128)S(1)} %stack.40.bits_ref, bf16[2,256,512]{2,1,0:T(8,128)(2,1)S(1)} %get-tuple-element.38.split_in_ref, f32[2,16,256]{2,1,0:T(8,128)S(1)} %get-tuple-element.39.table_in_ref), custom_call_target="tpu_custom_call" | custom-call | tf_op jit(solution)/shard_map/kept/pallas_call | solution.py:278
  56.3 7.5 %collective-permute-done.3.received_ref = s16[272,256]{1,0:T(8,128)(2,1)S(1)} collective-permute-done((s16[272,256]{1,0:T(8,128)(2,1)S(1)}, s16[272,256]{1,0:T(8,128)(2,1)S(1)}, u32[]{:S(2)}, u32[]{:S(2)}) %collective-permute-start.3) | collective-permute-done | bytes 139296 | tf_op jit(solution)/shard_map/ppermute | solution.py:291
  63.8 1.5 %sent.5 = (s16[272,256]{1,0:T(8,128)(2,1)S(1)}, bf16[2,256,512]{2,1,0:T(8,128)(2,1)S(1)}, f32[2,16,256]{2,1,0:T(8,128)S(1)}) custom-call(s32[16]{0:T(128)S(1)} %stack.40.bits_ref, bf16[256,512]{1,0:T(8,128)(2,1)S(1)} %get-tuple-element.40.kept_split_ref, f32[16,256]{1,0:T(8,128)S(1)} %get-tuple-element.41.kept_table_ref, ...), custom_call_target="tpu_custom_call" | custom-call | tf_op jit(solution)/shard_map/sent/pallas_call | solution.py:278
  65.3 0.1 collective-permute-start.4
  65.4 1.2 %kept.7 = (bf16[256,512]{1,0:T(8,128)(2,1)S(1)}, f32[16,256]{1,0:T(8,128)S(1)}) custom-call(s32[16]{0:T(128)S(1)} %stack.40.bits_ref, bf16[2,256,512]{2,1,0:T(8,128)(2,1)S(1)} %get-tuple-element.43.split_in_ref, f32[2,16,256]{2,1,0:T(8,128)S(1)} %get-tuple-element.44.table_in_ref), custom_call_target="tpu_custom_call" | custom-call | tf_op jit(solution)/shard_map/kept/pallas_call | solution.py:278
  66.6 5.5 %collective-permute-done.4.received_ref = s16[272,256]{1,0:T(8,128)(2,1)S(1)} collective-permute-done((s16[272,256]{1,0:T(8,128)(2,1)S(1)}, s16[272,256]{1,0:T(8,128)(2,1)S(1)}, u32[]{:S(2)}, u32[]{:S(2)}) %collective-permute-start.4) | collective-permute-done | bytes 139296 | tf_op jit(solution)/shard_map/ppermute | solution.py:291
  72.1 1.7 %sent_peaks.1 = (f32[8,256]{1,0:T(8,128)S(1)}, bf16[2,256,512]{2,1,0:T(8,128)(2,1)S(1)}, f32[2,16,256]{2,1,0:T(8,128)S(1)}) custom-call(s32[16]{0:T(128)S(1)} %stack.40.bits_ref, bf16[256,512]{1,0:T(8,128)(2,1)S(1)} %get-tuple-element.45.kept_split_ref, f32[16,256]{1,0:T(8,128)S(1)} %get-tuple-element.46.kept_table_ref, ...), custom_call_target="tpu_custom_call" | custom-call | tf_op jit(solution)/shard_map/sent_peaks/pallas_call | solution.py:278
  73.8 1.7 %collective-permute-start.5 = (f32[8,256]{1,0:T(8,128)S(1)}, f32[8,256]{1,0:T(8,128)S(1)}, u32[]{:S(2)}, u32[]{:S(2)}) collective-permute-start(f32[8,256]{1,0:T(8,128)S(1)} %get-tuple-element.50), channel_id=1, source_target_pairs={{0,8},{8,0},{16,24},{24,16},{32,40},{40,32},{48,56},{56,48},{64,72... | collective-permute-start | bytes 24584 | tf_op jit(solution)/shard_map/ppermute | solution.py:291
  75.5 1.5 %kept_peaks.1.kept_ref = f32[8,256]{1,0:T(8,128)S(1)} custom-call(s32[16]{0:T(128)S(1)} %stack.40.bits_ref, bf16[2,256,512]{2,1,0:T(8,128)(2,1)S(1)} %get-tuple-element.48.split_ref, f32[2,16,256]{2,1,0:T(8,128)S(1)} %get-tuple-element.49.table_ref), custom_call_target="tpu_custom_call" | custom-call | tf_op jit(solution)/shard_map/kept_peaks/pallas_call | solution.py:278
  77.0 0.0 collective-permute-done.5.received_ref
  77.0 0.5 join.1
  77.6 0.1 collective-permute-start.6
  77.7 6.2 %collective-permute-done.6 = f32[2,8,256]{2,1,0:T(8,128)S(1)} collective-permute-done((f32[2,8,256]{2,1,0:T(8,128)S(1)}, f32[2,8,256]{2,1,0:T(8,128)S(1)}, u32[]{:S(2)}, u32[]{:S(2)}) %collective-permute-start.6) | collective-permute-done | bytes 16416 | tf_op jit(solution)/shard_map/ppermute | solution.py:291
  83.8 0.6 copy.6
  (9 shorter events, 0.1 us)
Async XLA Ops:
  3.5 12.8 %copy-start.1 = (s32[5,3,256]{2,1,0:T(4,128)S(1)}, s32[5,3,256]{2,1,0:T(4,128)}, u32[]{:S(2)}) copy-start(s32[5,3,256]{2,1,0:T(4,128)} %param.6) | copy-start | bytes 46084
  3.5 12.8 %copy-start = (s32[256,512]{1,0:T(8,128)S(1)}, s32[256,512]{1,0:T(8,128)}, u32[]{:S(2)}) copy-start(s32[256,512]{1,0:T(8,128)} %param.5) | copy-start | bytes 1572868
  3.5 30.9 %all-to-all-start = ((bf16[32,2,16,256]{3,2,1,0:T(8,128)(2,1)}), bf16[32,2,16,256]{3,2,1,0:T(8,128)(2,1)S(1)}, u32[]{:S(2)}, u32[]{:S(2)}) async-start(bf16[32,2,16,256]{3,2,1,0:T(8,128)(2,1)} %filter_power.1), calls=%async_computation | async-start | bytes 1048576 | tf_op jit(solution)/shard_map/all_to_all | solution.py:320
  16.4 1.6 %collective-permute-start = (bf16[264,512]{1,0:T(8,128)(2,1)S(1)}, bf16[264,512]{1,0:T(8,128)(2,1)S(1)}, u32[]{:S(2)}, u32[]{:S(2)}) collective-permute-start(bf16[264,512]{1,0:T(8,128)(2,1)S(1)} %pad_maximum_fusion.first_ref), channel_id=1, source_target_pairs={{0,8},{8,0},{16,24},{24,16},{32,40},{40,32},{48,56},{56,48},{64,72... | collective-permute-start | bytes 811016 | tf_op jit(solution)/shard_map/ppermute | solution.py:291
  40.2 5.2 %collective-permute-start.1 = (s16[272,256]{1,0:T(8,128)(2,1)S(1)}, s16[272,256]{1,0:T(8,128)(2,1)S(1)}, u32[]{:S(2)}, u32[]{:S(2)}) collective-permute-start(s16[272,256]{1,0:T(8,128)(2,1)S(1)} %get-tuple-element.32), channel_id=1, source_target_pairs={{0,16},{8,24},{16,0},{24,8},{32,48},{40,56},{48,32},{56,40},{64,80... | collective-permute-start | bytes 417800 | tf_op jit(solution)/shard_map/ppermute | solution.py:291
  46.8 6.2 %collective-permute-start.2 = (s16[272,256]{1,0:T(8,128)(2,1)S(1)}, s16[272,256]{1,0:T(8,128)(2,1)S(1)}, u32[]{:S(2)}, u32[]{:S(2)}) collective-permute-start(s16[272,256]{1,0:T(8,128)(2,1)S(1)} %get-tuple-element.37), channel_id=1, source_target_pairs={{0,48},{8,56},{16,32},{24,40},{32,16},{40,24},{48,0},{56,8},{64,11... | collective-permute-start | bytes 417800 | tf_op jit(solution)/shard_map/ppermute | solution.py:291
  54.4 9.4 %collective-permute-start.3 = (s16[272,256]{1,0:T(8,128)(2,1)S(1)}, s16[272,256]{1,0:T(8,128)(2,1)S(1)}, u32[]{:S(2)}, u32[]{:S(2)}) collective-permute-start(s16[272,256]{1,0:T(8,128)(2,1)S(1)} %get-tuple-element.42), channel_id=1, source_target_pairs={{0,64},{8,72},{16,80},{24,88},{32,96},{40,104},{48,112},{56,120},{... | collective-permute-start | bytes 417800 | tf_op jit(solution)/shard_map/ppermute | solution.py:291
  65.3 6.8 %collective-permute-start.4 = (s16[272,256]{1,0:T(8,128)(2,1)S(1)}, s16[272,256]{1,0:T(8,128)(2,1)S(1)}, u32[]{:S(2)}, u32[]{:S(2)}) collective-permute-start(s16[272,256]{1,0:T(8,128)(2,1)S(1)} %get-tuple-element.47), channel_id=1, source_target_pairs={{0,192},{8,200},{16,208},{24,216},{32,224},{40,232},{48,240},{56,2... | collective-permute-start | bytes 417800 | tf_op jit(solution)/shard_map/ppermute | solution.py:291
  73.8 3.2 %collective-permute-start.5 = (f32[8,256]{1,0:T(8,128)S(1)}, f32[8,256]{1,0:T(8,128)S(1)}, u32[]{:S(2)}, u32[]{:S(2)}) collective-permute-start(f32[8,256]{1,0:T(8,128)S(1)} %get-tuple-element.50), channel_id=1, source_target_pairs={{0,8},{8,0},{16,24},{24,16},{32,40},{40,32},{48,56},{56,48},{64,72... | collective-permute-start | bytes 24584 | tf_op jit(solution)/shard_map/ppermute | solution.py:291
  77.6 6.3 %collective-permute-start.6 = (f32[2,8,256]{2,1,0:T(8,128)S(1)}, f32[2,8,256]{2,1,0:T(8,128)S(1)}, u32[]{:S(2)}, u32[]{:S(2)}) collective-permute-start(f32[2,8,256]{2,1,0:T(8,128)S(1)} %join.1), channel_id=1, source_target_pairs={{0,80},{8,208},{16,72},{24,200},{32,88},{40,216},{48,64},{56,192},... | collective-permute-start | bytes 49160 | tf_op jit(solution)/shard_map/ppermute | solution.py:291

commit v6 on v5

--- a/solution.py
+++ b/solution.py
@@ -29,6 +29,10 @@
     lambda d: 1 - bit(d, 3),
     lambda d: bit(d, 0),
 )
+
+
+def here():
+    return lax.axis_index("freq")
 
 
 def home(d):
@@ -162,8 +166,6 @@
 
 STEPS = 65534.0
 
-KEEP = 5
-
 
 def put_message(out_ref, x, table):
     trials = x.shape[0]
@@ -186,11 +188,11 @@
     return x, table
 
 
-def dedisperse_kernel(bits_ref, arrived_ref, first_ref, second_ref, sent_ref, split_ref, table_ref, stack_ref):
+def dedisperse_kernel(arrived_ref, first_ref, second_ref, sent_ref, split_ref, table_ref, stack_ref):
     sources, _, upchan, samples = arrived_ref.shape
     trials = split_ref.shape[1]
     channels = sources * upchan
-    first = bits_ref[0]
+    first = bit(here(), BEAM_BIT)
     for in_ref, unit in ((first_ref, first), (second_ref, 1 - first)):
         x = arrived_ref[:, pl.ds(unit, 1)].reshape(channels, samples).astype(f32)
         for inner in range(INNER):
@@ -212,16 +214,16 @@
         split_ref[unit] = split_of(total)
         packed = in_ref[trials:].astype(f32)
         table_ref[unit] = jnp.concatenate([packed[:, :samples], packed[:, samples:]], axis=0)
-    put_sent(0, bits_ref, split_ref, table_ref, sent_ref)
-
-
-def put_sent(level, bits_ref, split_ref, table_ref, sent_ref):
-    table = table_ref[1 - bits_ref[KEEP + level]]
+    put_sent(0, split_ref, table_ref, sent_ref)
+
+
+def put_sent(level, split_ref, table_ref, sent_ref):
+    table = table_ref[1 - KEEPS[level](here())]
     put_message(sent_ref, merge_unit(split_ref, table, level), table)
 
 
-def kept_kernel(level, bits_ref, split_in_ref, table_in_ref, split_ref, table_ref):
-    table = table_in_ref[bits_ref[KEEP + level]]
+def kept_kernel(level, split_in_ref, table_in_ref, split_ref, table_ref):
+    table = table_in_ref[KEEPS[level](here())]
     split_ref[...] = split_of(merge_unit(split_in_ref, table, level))
     table_ref[...] = table
 
@@ -234,9 +236,9 @@
     table_ref[1 - own] = table
 
 
-def sent_kernel(level, bits_ref, kept_split_ref, kept_table_ref, received_ref, sent_ref, split_ref, table_ref):
-    load_units(bits_ref[level], kept_split_ref, kept_table_ref, received_ref, split_ref, table_ref)
-    put_sent(level, bits_ref, split_ref, table_ref, sent_ref)
+def sent_kernel(level, kept_split_ref, kept_table_ref, received_ref, sent_ref, split_ref, table_ref):
+    load_units(bit(here(), level), kept_split_ref, kept_table_ref, received_ref, split_ref, table_ref)
+    put_sent(level, split_ref, table_ref, sent_ref)
 
 
 def unit_peaks(merged):
@@ -256,29 +258,29 @@
     return jnp.concatenate(peaks, axis=0)
 
 
-def sent_peaks_kernel(level, bits_ref, kept_split_ref, kept_table_ref, received_ref, peaks_ref, split_ref, table_ref):
-    load_units(bits_ref[level], kept_split_ref, kept_table_ref, received_ref, split_ref, table_ref)
-    peaks_ref[...] = unit_peaks(merge_unit(split_ref, table_ref[1 - bits_ref[KEEP + level]], level))
-
-
-def kept_peaks_kernel(level, bits_ref, split_ref, table_ref, peaks_ref):
-    peaks_ref[...] = unit_peaks(merge_unit(split_ref, table_ref[bits_ref[KEEP + level]], level))
-
-
-def join_kernel(bits_ref, kept_ref, received_ref, out_ref):
-    out_ref[bits_ref[0]] = kept_ref[...]
-    out_ref[1 - bits_ref[0]] = received_ref[...]
+def sent_peaks_kernel(level, kept_split_ref, kept_table_ref, received_ref, peaks_ref, split_ref, table_ref):
+    load_units(bit(here(), level), kept_split_ref, kept_table_ref, received_ref, split_ref, table_ref)
+    peaks_ref[...] = unit_peaks(merge_unit(split_ref, table_ref[1 - KEEPS[level](here())], level))
+
+
+def kept_peaks_kernel(level, split_ref, table_ref, peaks_ref):
+    peaks_ref[...] = unit_peaks(merge_unit(split_ref, table_ref[KEEPS[level](here())], level))
+
+
+def join_kernel(kept_ref, received_ref, out_ref):
+    beam = bit(here(), BEAM_BIT)
+    out_ref[beam] = kept_ref[...]
+    out_ref[1 - beam] = received_ref[...]
 
 
 VMEM = pl.BlockSpec(memory_space=pltpu.VMEM)
-SMEM = pl.BlockSpec(memory_space=pltpu.SMEM)
 
 
 def call(kernel, name, outs, operands, scratch=(), mebibytes=8):
     return pl.pallas_call(
         kernel,
         out_shape=tuple(jax.ShapeDtypeStruct(shape, dtype) for shape, dtype in outs),
-        in_specs=[SMEM] + [VMEM] * (len(operands) - 1),
+        in_specs=[VMEM] * len(operands),
         out_specs=tuple(VMEM for _ in outs),
         scratch_shapes=list(scratch),
         compiler_params=pltpu.CompilerParams(vmem_limit_bytes=mebibytes << 20),
@@ -312,10 +314,6 @@
     trials, channels = sub_delays.shape
     samples = voltages.shape[4]
     upchan = voltages.shape[3]
-    position = lax.axis_index("freq")
-    bits = [bit(position, index) for index in range(levels)] + [keep(position) for keep in KEEPS]
-    bits = jnp.stack(bits + [0] * (16 - len(bits))).astype(jnp.int32)
-
     power = filter_power(voltages)
     arrived = lax.all_to_all(power, "freq", split_axis=0, concat_axis=0, tiled=True)
 
@@ -329,22 +327,22 @@
     split, table = ((trials, 2 * samples), bf16), ((rows, samples), f32)
     stack = pltpu.VMEM((INNER * channels, samples), bf16)
     sent, *both = call(
-        dedisperse_kernel, "dedisperse", (message, splits, both_tables), (bits, arrived, first, second), [stack], 24
+        dedisperse_kernel, "dedisperse", (message, splits, both_tables), (arrived, first, second), [stack], 24
     )
     for level in range(levels - 1):
         received = swap(sent, PARTNERS[level])
-        kept = call(functools.partial(kept_kernel, level), "kept", (split, table), (bits, *both))
+        kept = call(functools.partial(kept_kernel, level), "kept", (split, table), tuple(both))
         if level < levels - 2:
             sent, *both = call(
-                functools.partial(sent_kernel, level + 1), "sent", (message, splits, both_tables), (bits, *kept, received)
+                functools.partial(sent_kernel, level + 1), "sent", (message, splits, both_tables), (*kept, received)
             )
     peak = ((WIDTHS, trials), f32)
     sent, *both = call(
-        functools.partial(sent_peaks_kernel, levels - 1), "sent_peaks", (peak, splits, both_tables), (bits, *kept, received)
+        functools.partial(sent_peaks_kernel, levels - 1), "sent_peaks", (peak, splits, both_tables), (*kept, received)
     )
     received = swap(sent, 1 << BEAM_BIT)
-    kept = call(functools.partial(kept_peaks_kernel, levels - 1), "kept_peaks", (peak,), (bits, *both))
-    peaks = call(join_kernel, "join", (((2, WIDTHS, trials), f32),), (bits, *kept, received))[0]
+    kept = call(functools.partial(kept_peaks_kernel, levels - 1), "kept_peaks", (peak,), tuple(both))
+    peaks = call(join_kernel, "join", (((2, WIDTHS, trials), f32),), (*kept, received))[0]
     return move(peaks, home)
 
 

time: 85.1 us -> 81.3 us (0.955)
  Pallas kernels: 22.1 us -> 16.3 us
  waiting for transfers between devices: 44.4 us -> 46.6 us
    pallas_call x11, Pallas kernels: 18.7 us -> 12.8 us  [call(): pl.pallas_call(kernel, out_shape=tuple((jax.ShapeDtypeStruct(shape, dtype...]
    ppermute x7, waiting for transfers between devices: 28.1 us -> 30.2 us  [move(): lax.ppermute(x, 'freq', pairs)]
  transfers between devices with their start and end apart: 8 -> 8, of which waited for: 7 -> 7; matrix products, arithmetic and copies ran while one was open for 0% -> 0% of each run, Pallas kernels for 7% -> 4%
where the time goes in v6:
time: 81.3 us; the launch traced here: 80.6 us
  waiting for transfers between devices  46.6 us (57%)
  starting transfers between devices  16.9 us (21%)
  Pallas kernels  16.3 us (20%)
    ppermute x7, waiting for transfers between devices, move(): lax.ppermute(x, 'freq', pairs)  30.2 us
    all_to_all x1, waiting for transfers between devices, local(): lax.all_to_all(power, 'freq', split_axis=0, concat_axis=0, tiled=True)  16.4 us
    pallas_call x11, Pallas kernels, call(): pl.pallas_call(kernel, out_shape=tuple((jax.ShapeDtypeStruct(shape, dtype...  12.8 us
    all_to_all x1, starting transfers between devices, local(): lax.all_to_all(power, 'freq', split_axis=0, concat_axis=0, tiled=True)  12.7 us
    ppermute x7, starting transfers between devices, move(): lax.ppermute(x, 'freq', pairs)  4.15 us
    pallas_call x1, Pallas kernels, filter_power(): pl.pallas_call(filter_kernel, out_shape=jax.ShapeDtypeStruct((coarse // 2...  3.46 us
  transfers between devices with their start and end apart: 8, of which 7 were waited for; matrix products, arithmetic and copies ran while one was open for 0% of the time, Pallas kernels for 4%

profile of v6, /device:TPU:1, one launch (start us, length us, event | category | flops | bytes accessed | tf_op | source)
XLA Modules:
  0.0 80.6 jit_solution(9106249366990504956)
XLA Ops:
  0.0 3.5 %filter_power.1 = bf16[32,2,16,256]{3,2,1,0:T(8,128)(2,1)} custom-call(bf16[64,128]{1,0:T(8,128)(2,1)} %constant.5.clone.matrix_hbm, bf16[2,2,32,16,256]{4,3,2,1,0:T(8,128)(2,1)} %volts_hbm.1), custom_call_target="tpu_custom_call" | custom-call | tf_op jit(solution)/shard_map/filter_power/pallas_call | solution.py:108
  3.5 0.0 copy-start.1
  3.5 0.0 copy-start
  3.5 12.7 %all-to-all-start = ((bf16[32,2,16,256]{3,2,1,0:T(8,128)(2,1)}), bf16[32,2,16,256]{3,2,1,0:T(8,128)(2,1)S(1)}, u32[]{:S(2)}, u32[]{:S(2)}) async-start(bf16[32,2,16,256]{3,2,1,0:T(8,128)(2,1)} %filter_power.1), calls=%async_computation | async-start | bytes 1048576 | tf_op jit(solution)/shard_map/all_to_all | solution.py:318
  16.2 0.0 copy-done.1
  16.3 0.0 copy-done
  16.4 0.3 collective-permute-start
  16.7 1.3 %collective-permute-done.second_ref = bf16[264,512]{1,0:T(8,128)(2,1)S(1)} collective-permute-done((bf16[264,512]{1,0:T(8,128)(2,1)S(1)}, bf16[264,512]{1,0:T(8,128)(2,1)S(1)}, u32[]{:S(2)}, u32[]{:S(2)}) %collective-permute-start) | collective-permute-done | bytes 270368 | tf_op jit(solution)/shard_map/ppermute | solution.py:293
  18.0 16.4 %all-to-all-done.arrived_ref = bf16[32,2,16,256]{3,2,1,0:T(8,128)(2,1)S(1)} async-done(((bf16[32,2,16,256]{3,2,1,0:T(8,128)(2,1)}), bf16[32,2,16,256]{3,2,1,0:T(8,128)(2,1)S(1)}, u32[]{:S(2)}, u32[]{:S(2)}) %all-to-all-start) | async-done | bytes 524320 | tf_op jit(solution)/shard_map/all_to_all | solution.py:318
  34.4 5.2 %dedisperse.1 = (s16[272,256]{1,0:T(8,128)(2,1)S(1)}, bf16[2,256,512]{2,1,0:T(8,128)(2,1)S(1)}, f32[2,16,256]{2,1,0:T(8,128)S(1)}) custom-call(bf16[32,2,16,256]{3,2,1,0:T(8,128)(2,1)S(1)} %all-to-all-done.arrived_ref, bf16[264,512]{1,0:T(8,128)(2,1)S(1)} %pad_maximum_fusion.first_ref, bf16[264,512]{1,0:T(8,128)(2,1)S(1)} %collective-permute-done.second_ref), custom_call_target="tpu_custom_call" | custom-call | tf_op jit(solution)/shard_map/dedisperse/pallas_call | solution.py:280
  39.6 0.1 collective-permute-start.1
  39.7 0.6 kept.4
  40.3 4.4 %collective-permute-done.1.received_ref = s16[272,256]{1,0:T(8,128)(2,1)S(1)} collective-permute-done((s16[272,256]{1,0:T(8,128)(2,1)S(1)}, s16[272,256]{1,0:T(8,128)(2,1)S(1)}, u32[]{:S(2)}, u32[]{:S(2)}) %collective-permute-start.1) | collective-permute-done | bytes 139296 | tf_op jit(solution)/shard_map/ppermute | solution.py:293
  44.7 0.9 %sent.3 = (s16[272,256]{1,0:T(8,128)(2,1)S(1)}, bf16[2,256,512]{2,1,0:T(8,128)(2,1)S(1)}, f32[2,16,256]{2,1,0:T(8,128)S(1)}) custom-call(bf16[256,512]{1,0:T(8,128)(2,1)S(1)} %get-tuple-element.30.kept_split_ref, f32[16,256]{1,0:T(8,128)S(1)} %get-tuple-element.31.kept_table_ref, s16[272,256]{1,0:T(8,128)(2,1)S(1)} %collective-permute-done.1.received_ref), custom_call_target="tpu_custom_call" | custom-call | tf_op jit(solution)/shard_map/sent/pallas_call | solution.py:280
  45.7 1.2 %collective-permute-start.2 = (s16[272,256]{1,0:T(8,128)(2,1)S(1)}, s16[272,256]{1,0:T(8,128)(2,1)S(1)}, u32[]{:S(2)}, u32[]{:S(2)}) collective-permute-start(s16[272,256]{1,0:T(8,128)(2,1)S(1)} %get-tuple-element.37), channel_id=1, source_target_pairs={{0,48},{8,56},{16,32},{24,40},{32,16},{40,24},{48,0},{56,8},{64,11... | collective-permute-start | bytes 417800 | tf_op jit(solution)/shard_map/ppermute | solution.py:293
  46.9 0.6 kept.5
  47.6 4.3 %collective-permute-done.2.received_ref = s16[272,256]{1,0:T(8,128)(2,1)S(1)} collective-permute-done((s16[272,256]{1,0:T(8,128)(2,1)S(1)}, s16[272,256]{1,0:T(8,128)(2,1)S(1)}, u32[]{:S(2)}, u32[]{:S(2)}) %collective-permute-start.2) | collective-permute-done | bytes 139296 | tf_op jit(solution)/shard_map/ppermute | solution.py:293
  51.8 0.9 %sent.4 = (s16[272,256]{1,0:T(8,128)(2,1)S(1)}, bf16[2,256,512]{2,1,0:T(8,128)(2,1)S(1)}, f32[2,16,256]{2,1,0:T(8,128)S(1)}) custom-call(bf16[256,512]{1,0:T(8,128)(2,1)S(1)} %get-tuple-element.35.kept_split_ref, f32[16,256]{1,0:T(8,128)S(1)} %get-tuple-element.36.kept_table_ref, s16[272,256]{1,0:T(8,128)(2,1)S(1)} %collective-permute-done.2.received_ref), custom_call_target="tpu_custom_call" | custom-call | tf_op jit(solution)/shard_map/sent/pallas_call | solution.py:280
  52.8 0.6 collective-permute-start.3
  53.4 0.6 kept.6
  54.0 8.0 %collective-permute-done.3.received_ref = s16[272,256]{1,0:T(8,128)(2,1)S(1)} collective-permute-done((s16[272,256]{1,0:T(8,128)(2,1)S(1)}, s16[272,256]{1,0:T(8,128)(2,1)S(1)}, u32[]{:S(2)}, u32[]{:S(2)}) %collective-permute-start.3) | collective-permute-done | bytes 139296 | tf_op jit(solution)/shard_map/ppermute | solution.py:293
  62.1 0.9 %sent.5 = (s16[272,256]{1,0:T(8,128)(2,1)S(1)}, bf16[2,256,512]{2,1,0:T(8,128)(2,1)S(1)}, f32[2,16,256]{2,1,0:T(8,128)S(1)}) custom-call(bf16[256,512]{1,0:T(8,128)(2,1)S(1)} %get-tuple-element.40.kept_split_ref, f32[16,256]{1,0:T(8,128)S(1)} %get-tuple-element.41.kept_table_ref, s16[272,256]{1,0:T(8,128)(2,1)S(1)} %collective-permute-done.3.received_ref), custom_call_target="tpu_custom_call" | custom-call | tf_op jit(solution)/shard_map/sent/pallas_call | solution.py:280
  63.0 0.1 collective-permute-start.4
  63.1 0.6 kept.7
  63.7 6.0 %collective-permute-done.4.received_ref = s16[272,256]{1,0:T(8,128)(2,1)S(1)} collective-permute-done((s16[272,256]{1,0:T(8,128)(2,1)S(1)}, s16[272,256]{1,0:T(8,128)(2,1)S(1)}, u32[]{:S(2)}, u32[]{:S(2)}) %collective-permute-start.4) | collective-permute-done | bytes 139296 | tf_op jit(solution)/shard_map/ppermute | solution.py:293
  69.7 1.2 %sent_peaks.1 = (f32[8,256]{1,0:T(8,128)S(1)}, bf16[2,256,512]{2,1,0:T(8,128)(2,1)S(1)}, f32[2,16,256]{2,1,0:T(8,128)S(1)}) custom-call(bf16[256,512]{1,0:T(8,128)(2,1)S(1)} %get-tuple-element.45.kept_split_ref, f32[16,256]{1,0:T(8,128)S(1)} %get-tuple-element.46.kept_table_ref, s16[272,256]{1,0:T(8,128)(2,1)S(1)} %collective-permute-done.4.received_ref), custom_call_target="tpu_custom_call" | custom-call | tf_op jit(solution)/shard_map/sent_peaks/pallas_call | solution.py:280
  71.0 1.7 %collective-permute-start.5 = (f32[8,256]{1,0:T(8,128)S(1)}, f32[8,256]{1,0:T(8,128)S(1)}, u32[]{:S(2)}, u32[]{:S(2)}) collective-permute-start(f32[8,256]{1,0:T(8,128)S(1)} %get-tuple-element.50), channel_id=1, source_target_pairs={{0,8},{8,0},{16,24},{24,16},{32,40},{40,32},{48,56},{56,48},{64,72... | collective-permute-start | bytes 24584 | tf_op jit(solution)/shard_map/ppermute | solution.py:293
  72.7 1.0 %kept_peaks.1.kept_ref = f32[8,256]{1,0:T(8,128)S(1)} custom-call(bf16[2,256,512]{2,1,0:T(8,128)(2,1)S(1)} %get-tuple-element.48.split_ref, f32[2,16,256]{2,1,0:T(8,128)S(1)} %get-tuple-element.49.table_ref), custom_call_target="tpu_custom_call" | custom-call | tf_op jit(solution)/shard_map/kept_peaks/pallas_call | solution.py:280
  73.7 0.0 collective-permute-done.5.received_ref
  73.7 0.1 collective-permute-start.6
  73.8 6.2 %collective-permute-done.6 = f32[2,8,256]{2,1,0:T(8,128)S(1)} collective-permute-done((f32[2,8,256]{2,1,0:T(8,128)S(1)}, f32[2,8,256]{2,1,0:T(8,128)S(1)}, u32[]{:S(2)}, u32[]{:S(2)}) %collective-permute-start.6) | collective-permute-done | bytes 16416 | tf_op jit(solution)/shard_map/ppermute | solution.py:293
  80.0 0.6 copy.6
  (6 shorter events, 0.1 us)
Async XLA Ops:
  3.5 12.8 %copy-start.1 = (s32[5,3,256]{2,1,0:T(4,128)S(1)}, s32[5,3,256]{2,1,0:T(4,128)}, u32[]{:S(2)}) copy-start(s32[5,3,256]{2,1,0:T(4,128)} %param.6) | copy-start | bytes 46084
  3.5 12.8 %copy-start = (s32[256,512]{1,0:T(8,128)S(1)}, s32[256,512]{1,0:T(8,128)}, u32[]{:S(2)}) copy-start(s32[256,512]{1,0:T(8,128)} %param.5) | copy-start | bytes 1572868
  3.5 30.9 %all-to-all-start = ((bf16[32,2,16,256]{3,2,1,0:T(8,128)(2,1)}), bf16[32,2,16,256]{3,2,1,0:T(8,128)(2,1)S(1)}, u32[]{:S(2)}, u32[]{:S(2)}) async-start(bf16[32,2,16,256]{3,2,1,0:T(8,128)(2,1)} %filter_power.1), calls=%async_computation | async-start | bytes 1048576 | tf_op jit(solution)/shard_map/all_to_all | solution.py:318
  16.4 1.6 %collective-permute-start = (bf16[264,512]{1,0:T(8,128)(2,1)S(1)}, bf16[264,512]{1,0:T(8,128)(2,1)S(1)}, u32[]{:S(2)}, u32[]{:S(2)}) collective-permute-start(bf16[264,512]{1,0:T(8,128)(2,1)S(1)} %pad_maximum_fusion.first_ref), channel_id=1, source_target_pairs={{0,8},{8,0},{16,24},{24,16},{32,40},{40,32},{48,56},{56,48},{64,72... | collective-permute-start | bytes 811016 | tf_op jit(solution)/shard_map/ppermute | solution.py:293
  39.6 5.2 %collective-permute-start.1 = (s16[272,256]{1,0:T(8,128)(2,1)S(1)}, s16[272,256]{1,0:T(8,128)(2,1)S(1)}, u32[]{:S(2)}, u32[]{:S(2)}) collective-permute-start(s16[272,256]{1,0:T(8,128)(2,1)S(1)} %get-tuple-element.32), channel_id=1, source_target_pairs={{0,16},{8,24},{16,0},{24,8},{32,48},{40,56},{48,32},{56,40},{64,80... | collective-permute-start | bytes 417800 | tf_op jit(solution)/shard_map/ppermute | solution.py:293
  45.7 6.2 %collective-permute-start.2 = (s16[272,256]{1,0:T(8,128)(2,1)S(1)}, s16[272,256]{1,0:T(8,128)(2,1)S(1)}, u32[]{:S(2)}, u32[]{:S(2)}) collective-permute-start(s16[272,256]{1,0:T(8,128)(2,1)S(1)} %get-tuple-element.37), channel_id=1, source_target_pairs={{0,48},{8,56},{16,32},{24,40},{32,16},{40,24},{48,0},{56,8},{64,11... | collective-permute-start | bytes 417800 | tf_op jit(solution)/shard_map/ppermute | solution.py:293
  52.8 9.3 %collective-permute-start.3 = (s16[272,256]{1,0:T(8,128)(2,1)S(1)}, s16[272,256]{1,0:T(8,128)(2,1)S(1)}, u32[]{:S(2)}, u32[]{:S(2)}) collective-permute-start(s16[272,256]{1,0:T(8,128)(2,1)S(1)} %get-tuple-element.42), channel_id=1, source_target_pairs={{0,64},{8,72},{16,80},{24,88},{32,96},{40,104},{48,112},{56,120},{... | collective-permute-start | bytes 417800 | tf_op jit(solution)/shard_map/ppermute | solution.py:293
  63.0 6.7 %collective-permute-start.4 = (s16[272,256]{1,0:T(8,128)(2,1)S(1)}, s16[272,256]{1,0:T(8,128)(2,1)S(1)}, u32[]{:S(2)}, u32[]{:S(2)}) collective-permute-start(s16[272,256]{1,0:T(8,128)(2,1)S(1)} %get-tuple-element.47), channel_id=1, source_target_pairs={{0,192},{8,200},{16,208},{24,216},{32,224},{40,232},{48,240},{56,2... | collective-permute-start | bytes 417800 | tf_op jit(solution)/shard_map/ppermute | solution.py:293
  71.0 2.8 %collective-permute-start.5 = (f32[8,256]{1,0:T(8,128)S(1)}, f32[8,256]{1,0:T(8,128)S(1)}, u32[]{:S(2)}, u32[]{:S(2)}) collective-permute-start(f32[8,256]{1,0:T(8,128)S(1)} %get-tuple-element.50), channel_id=1, source_target_pairs={{0,8},{8,0},{16,24},{24,16},{32,40},{40,32},{48,56},{56,48},{64,72... | collective-permute-start | bytes 24584 | tf_op jit(solution)/shard_map/ppermute | solution.py:293
  73.7 6.3 %collective-permute-start.6 = (f32[2,8,256]{2,1,0:T(8,128)S(1)}, f32[2,8,256]{2,1,0:T(8,128)S(1)}, u32[]{:S(2)}, u32[]{:S(2)}) collective-permute-start(f32[2,8,256]{2,1,0:T(8,128)S(1)} %join.1), channel_id=1, source_target_pairs={{0,80},{8,208},{16,72},{24,200},{32,88},{40,216},{48,64},{56,192},... | collective-permute-start | bytes 49160 | tf_op jit(solution)/shard_map/ppermute | solution.py:293

commit v7 on v6

--- a/solution.py
+++ b/solution.py
@@ -63,8 +63,10 @@
 
 
 def shifted(x, amount):
-    lane = lax.broadcasted_iota(jnp.int32, x.shape, 1)
-    return jnp.where(lane >= amount, pltpu.roll(x, amount, 1), 0.0)
+    rolled = pltpu.roll(x, amount, 1)
+    head = rolled[:, :128]
+    lane = lax.broadcasted_iota(jnp.int32, head.shape, 1)
+    return jnp.concatenate([jnp.where(lane >= amount, head, 0.0), rolled[:, 128:]], axis=1)
 
 
 def filter_kernel(matrix_hbm, volts_hbm, out_hbm, matrix_ref, volts_ref, out_ref, in_sems, out_sems):
@@ -102,7 +104,7 @@
 
 def filter_power(voltages):
     parts, beams, coarse, upchan, samples = voltages.shape
-    chunks = 4
+    chunks = 2
     count = coarse // chunks
     matrix = jnp.asarray(filter_matrix(upchan))
     return pl.pallas_call(
@@ -188,17 +190,16 @@
     return x, table
 
 
-def dedisperse_kernel(arrived_ref, first_ref, second_ref, sent_ref, split_ref, table_ref, stack_ref):
+def dedisperse_kernel(arrived_ref, tables_ref, sent_ref, split_ref, table_ref, stack_ref):
     sources, _, upchan, samples = arrived_ref.shape
     trials = split_ref.shape[1]
     channels = sources * upchan
-    first = bit(here(), BEAM_BIT)
-    for in_ref, unit in ((first_ref, first), (second_ref, 1 - first)):
-        x = arrived_ref[:, pl.ds(unit, 1)].reshape(channels, samples).astype(f32)
+    for unit in range(2):
+        x = arrived_ref[:, unit].reshape(channels, samples).astype(f32)
         for inner in range(INNER):
             moved = x if inner == 0 else shifted(x, inner)
             stack_ref[inner * channels : (inner + 1) * channels] = moved.astype(bf16)
-        delays = in_ref[:trials]
+        delays = tables_ref[unit, :trials]
         total = jnp.zeros((trials, samples), f32)
         for outer in reversed(range(SHIFTS // INNER)):
             onehot = jnp.concatenate(
@@ -212,7 +213,7 @@
                 total = shifted(total, INNER)
             total = total + jnp.dot(onehot, stack_ref[...], preferred_element_type=f32)
         split_ref[unit] = split_of(total)
-        packed = in_ref[trials:].astype(f32)
+        packed = tables_ref[unit, trials:].astype(f32)
         table_ref[unit] = jnp.concatenate([packed[:, :samples], packed[:, samples:]], axis=0)
     put_sent(0, split_ref, table_ref, sent_ref)
 
@@ -321,13 +322,15 @@
     table = jnp.pad(merge_tables.reshape(3 * levels, trials), ((0, rows - 3 * levels), (0, 0)))
     table = table.reshape(2, rows // 2, trials).transpose(1, 0, 2).reshape(rows // 2, 2 * trials)
     first, second = gather_units(jnp.concatenate([sub_delays, table], axis=0).astype(bf16))
+    swapped = bit(here(), BEAM_BIT) == 1
+    tables = jnp.stack([jnp.where(swapped, second, first), jnp.where(swapped, first, second)])
 
     message = ((trials + rows, samples), jnp.int16)
     splits, both_tables = ((2, trials, 2 * samples), bf16), ((2, rows, samples), f32)
     split, table = ((trials, 2 * samples), bf16), ((rows, samples), f32)
     stack = pltpu.VMEM((INNER * channels, samples), bf16)
     sent, *both = call(
-        dedisperse_kernel, "dedisperse", (message, splits, both_tables), (arrived, first, second), [stack], 24
+        dedisperse_kernel, "dedisperse", (message, splits, both_tables), (arrived, tables), [stack], 24
     )
     for level in range(levels - 1):
         received = swap(sent, PARTNERS[level])

time: 81.3 us -> 81.1 us (level)
  starting transfers between devices: 16.9 us -> 18 us
  waiting for transfers between devices: 46.6 us -> 45.5 us
    ppermute x7, starting transfers between devices: 4.15 us -> 5.32 us  [move(): lax.ppermute(x, 'freq', pairs)]
    ppermute x7, waiting for transfers between devices: 30.2 us -> 29.3 us  [move(): lax.ppermute(x, 'freq', pairs)]
where the time goes in v7:
time: 81.1 us; the launch traced here: 80.4 us
  waiting for transfers between devices  45.5 us (56%)
  starting transfers between devices  18 us (22%)
  Pallas kernels  15.8 us (19%)
    ppermute x7, waiting for transfers between devices, move(): lax.ppermute(x, 'freq', pairs)  29.3 us
    all_to_all x1, waiting for transfers between devices, local(): lax.all_to_all(power, 'freq', split_axis=0, concat_axis=0, tiled=True)  16.2 us
    all_to_all x1, starting transfers between devices, local(): lax.all_to_all(power, 'freq', split_axis=0, concat_axis=0, tiled=True)  12.7 us
    pallas_call x11, Pallas kernels, call(): pl.pallas_call(kernel, out_shape=tuple((jax.ShapeDtypeStruct(shape, dtype...  12.7 us
    ppermute x7, starting transfers between devices, move(): lax.ppermute(x, 'freq', pairs)  5.32 us
    pallas_call x1, Pallas kernels, filter_power(): pl.pallas_call(filter_kernel, out_shape=jax.ShapeDtypeStruct((coarse // 2...  3.07 us
  transfers between devices with their start and end apart: 8, of which 7 were waited for; matrix products, arithmetic and copies ran while one was open for 0% of the time, Pallas kernels for 4%

profile of v7, /device:TPU:1, one launch (start us, length us, event | category | flops | bytes accessed | tf_op | source)
XLA Modules:
  0.0 80.4 jit_solution(13252474505797684634)
XLA Ops:
  0.0 3.1 %filter_power.1 = bf16[32,2,16,256]{3,2,1,0:T(8,128)(2,1)} custom-call(bf16[64,128]{1,0:T(8,128)(2,1)} %constant.14.clone.matrix_hbm, bf16[2,2,32,16,256]{4,3,2,1,0:T(8,128)(2,1)} %volts_hbm.1), custom_call_target="tpu_custom_call" | custom-call | tf_op jit(solution)/shard_map/filter_power/pallas_call | solution.py:110
  3.1 0.0 copy-start.1
  3.1 0.0 copy-start
  3.1 12.7 %all-to-all-start = ((bf16[32,2,16,256]{3,2,1,0:T(8,128)(2,1)}), bf16[32,2,16,256]{3,2,1,0:T(8,128)(2,1)S(1)}, u32[]{:S(2)}, u32[]{:S(2)}) async-start(bf16[32,2,16,256]{3,2,1,0:T(8,128)(2,1)} %filter_power.1), calls=%async_computation | async-start | bytes 1048576 | tf_op jit(solution)/shard_map/all_to_all | solution.py:319
  16.0 0.3 collective-permute-start
  16.3 1.3 %collective-permute-done = bf16[264,512]{1,0:T(8,128)(2,1)S(1)} collective-permute-done((bf16[264,512]{1,0:T(8,128)(2,1)S(1)}, bf16[264,512]{1,0:T(8,128)(2,1)S(1)}, u32[]{:S(2)}, u32[]{:S(2)}) %collective-permute-start) | collective-permute-done | bytes 270368 | tf_op jit(solution)/shard_map/ppermute | solution.py:294
  17.6 0.1 select_bitcast_fusion.1
  17.7 0.1 pad_maximum_fusion.tables_ref
  17.8 16.2 %all-to-all-done.arrived_ref = bf16[32,2,16,256]{3,2,1,0:T(8,128)(2,1)S(1)} async-done(((bf16[32,2,16,256]{3,2,1,0:T(8,128)(2,1)}), bf16[32,2,16,256]{3,2,1,0:T(8,128)(2,1)S(1)}, u32[]{:S(2)}, u32[]{:S(2)}) %all-to-all-start) | async-done | bytes 524320 | tf_op jit(solution)/shard_map/all_to_all | solution.py:319
  34.0 5.1 %dedisperse.1 = (s16[272,256]{1,0:T(8,128)(2,1)S(1)}, bf16[2,256,512]{2,1,0:T(8,128)(2,1)S(1)}, f32[2,16,256]{2,1,0:T(8,128)S(1)}) custom-call(bf16[32,2,16,256]{3,2,1,0:T(8,128)(2,1)S(1)} %all-to-all-done.arrived_ref, bf16[2,264,512]{2,1,0:T(8,128)(2,1)S(1)} %pad_maximum_fusion.tables_ref), custom_call_target="tpu_custom_call" | custom-call | tf_op jit(solution)/shard_map/dedisperse/pallas_call | solution.py:281
  39.1 0.1 collective-permute-start.1
  39.2 0.6 kept.4
  39.8 4.4 %collective-permute-done.1.received_ref = s16[272,256]{1,0:T(8,128)(2,1)S(1)} collective-permute-done((s16[272,256]{1,0:T(8,128)(2,1)S(1)}, s16[272,256]{1,0:T(8,128)(2,1)S(1)}, u32[]{:S(2)}, u32[]{:S(2)}) %collective-permute-start.1) | collective-permute-done | bytes 139296 | tf_op jit(solution)/shard_map/ppermute | solution.py:294
  44.3 0.9 %sent.3 = (s16[272,256]{1,0:T(8,128)(2,1)S(1)}, bf16[2,256,512]{2,1,0:T(8,128)(2,1)S(1)}, f32[2,16,256]{2,1,0:T(8,128)S(1)}) custom-call(bf16[256,512]{1,0:T(8,128)(2,1)S(1)} %get-tuple-element.30.kept_split_ref, f32[16,256]{1,0:T(8,128)S(1)} %get-tuple-element.31.kept_table_ref, s16[272,256]{1,0:T(8,128)(2,1)S(1)} %collective-permute-done.1.received_ref), custom_call_target="tpu_custom_call" | custom-call | tf_op jit(solution)/shard_map/sent/pallas_call | solution.py:281
  45.2 1.3 %collective-permute-start.2 = (s16[272,256]{1,0:T(8,128)(2,1)S(1)}, s16[272,256]{1,0:T(8,128)(2,1)S(1)}, u32[]{:S(2)}, u32[]{:S(2)}) collective-permute-start(s16[272,256]{1,0:T(8,128)(2,1)S(1)} %get-tuple-element.37), channel_id=1, source_target_pairs={{0,48},{8,56},{16,32},{24,40},{32,16},{40,24},{48,0},{56,8},{64,11... | collective-permute-start | bytes 417800 | tf_op jit(solution)/shard_map/ppermute | solution.py:294
  46.5 0.6 kept.5
  47.1 4.2 %collective-permute-done.2.received_ref = s16[272,256]{1,0:T(8,128)(2,1)S(1)} collective-permute-done((s16[272,256]{1,0:T(8,128)(2,1)S(1)}, s16[272,256]{1,0:T(8,128)(2,1)S(1)}, u32[]{:S(2)}, u32[]{:S(2)}) %collective-permute-start.2) | collective-permute-done | bytes 139296 | tf_op jit(solution)/shard_map/ppermute | solution.py:294
  51.4 0.9 %sent.4 = (s16[272,256]{1,0:T(8,128)(2,1)S(1)}, bf16[2,256,512]{2,1,0:T(8,128)(2,1)S(1)}, f32[2,16,256]{2,1,0:T(8,128)S(1)}) custom-call(bf16[256,512]{1,0:T(8,128)(2,1)S(1)} %get-tuple-element.35.kept_split_ref, f32[16,256]{1,0:T(8,128)S(1)} %get-tuple-element.36.kept_table_ref, s16[272,256]{1,0:T(8,128)(2,1)S(1)} %collective-permute-done.2.received_ref), custom_call_target="tpu_custom_call" | custom-call | tf_op jit(solution)/shard_map/sent/pallas_call | solution.py:281
  52.3 0.6 collective-permute-start.3
  52.9 0.6 kept.6
  53.6 8.3 %collective-permute-done.3.received_ref = s16[272,256]{1,0:T(8,128)(2,1)S(1)} collective-permute-done((s16[272,256]{1,0:T(8,128)(2,1)S(1)}, s16[272,256]{1,0:T(8,128)(2,1)S(1)}, u32[]{:S(2)}, u32[]{:S(2)}) %collective-permute-start.3) | collective-permute-done | bytes 139296 | tf_op jit(solution)/shard_map/ppermute | solution.py:294
  61.8 0.9 %sent.5 = (s16[272,256]{1,0:T(8,128)(2,1)S(1)}, bf16[2,256,512]{2,1,0:T(8,128)(2,1)S(1)}, f32[2,16,256]{2,1,0:T(8,128)S(1)}) custom-call(bf16[256,512]{1,0:T(8,128)(2,1)S(1)} %get-tuple-element.40.kept_split_ref, f32[16,256]{1,0:T(8,128)S(1)} %get-tuple-element.41.kept_table_ref, s16[272,256]{1,0:T(8,128)(2,1)S(1)} %collective-permute-done.3.received_ref), custom_call_target="tpu_custom_call" | custom-call | tf_op jit(solution)/shard_map/sent/pallas_call | solution.py:281
  62.8 0.1 collective-permute-start.4
  62.9 0.6 kept.7
  63.5 6.1 %collective-permute-done.4.received_ref = s16[272,256]{1,0:T(8,128)(2,1)S(1)} collective-permute-done((s16[272,256]{1,0:T(8,128)(2,1)S(1)}, s16[272,256]{1,0:T(8,128)(2,1)S(1)}, u32[]{:S(2)}, u32[]{:S(2)}) %collective-permute-start.4) | collective-permute-done | bytes 139296 | tf_op jit(solution)/shard_map/ppermute | solution.py:294
  69.6 1.2 %sent_peaks.1 = (f32[8,256]{1,0:T(8,128)S(1)}, bf16[2,256,512]{2,1,0:T(8,128)(2,1)S(1)}, f32[2,16,256]{2,1,0:T(8,128)S(1)}) custom-call(bf16[256,512]{1,0:T(8,128)(2,1)S(1)} %get-tuple-element.45.kept_split_ref, f32[16,256]{1,0:T(8,128)S(1)} %get-tuple-element.46.kept_table_ref, s16[272,256]{1,0:T(8,128)(2,1)S(1)} %collective-permute-done.4.received_ref), custom_call_target="tpu_custom_call" | custom-call | tf_op jit(solution)/shard_map/sent_peaks/pallas_call | solution.py:281
  70.9 1.6 %collective-permute-start.5 = (f32[8,256]{1,0:T(8,128)S(1)}, f32[8,256]{1,0:T(8,128)S(1)}, u32[]{:S(2)}, u32[]{:S(2)}) collective-permute-start(f32[8,256]{1,0:T(8,128)S(1)} %get-tuple-element.50), channel_id=1, source_target_pairs={{0,8},{8,0},{16,24},{24,16},{32,40},{40,32},{48,56},{56,48},{64,72... | collective-permute-start | bytes 24584 | tf_op jit(solution)/shard_map/ppermute | solution.py:294
  72.5 1.0 %kept_peaks.1.kept_ref = f32[8,256]{1,0:T(8,128)S(1)} custom-call(bf16[2,256,512]{2,1,0:T(8,128)(2,1)S(1)} %get-tuple-element.48.split_ref, f32[2,16,256]{2,1,0:T(8,128)S(1)} %get-tuple-element.49.table_ref), custom_call_target="tpu_custom_call" | custom-call | tf_op jit(solution)/shard_map/kept_peaks/pallas_call | solution.py:281
  73.5 0.0 collective-permute-done.5.received_ref
  73.5 1.3 %collective-permute-start.6 = (f32[2,8,256]{2,1,0:T(8,128)S(1)}, f32[2,8,256]{2,1,0:T(8,128)S(1)}, u32[]{:S(2)}, u32[]{:S(2)}) collective-permute-start(f32[2,8,256]{2,1,0:T(8,128)S(1)} %join.1), channel_id=1, source_target_pairs={{0,80},{8,208},{16,72},{24,200},{32,88},{40,216},{48,64},{56,192},... | collective-permute-start | bytes 49160 | tf_op jit(solution)/shard_map/ppermute | solution.py:294
  74.8 4.9 %collective-permute-done.6 = f32[2,8,256]{2,1,0:T(8,128)S(1)} collective-permute-done((f32[2,8,256]{2,1,0:T(8,128)S(1)}, f32[2,8,256]{2,1,0:T(8,128)S(1)}, u32[]{:S(2)}, u32[]{:S(2)}) %collective-permute-start.6) | collective-permute-done | bytes 16416 | tf_op jit(solution)/shard_map/ppermute | solution.py:294
  79.8 0.6 copy.6
  (8 shorter events, 0.1 us)
Async XLA Ops:
  3.1 12.8 %copy-start.1 = (s32[5,3,256]{2,1,0:T(4,128)S(1)}, s32[5,3,256]{2,1,0:T(4,128)}, u32[]{:S(2)}) copy-start(s32[5,3,256]{2,1,0:T(4,128)} %param.6) | copy-start | bytes 46084
  3.1 12.8 %copy-start = (s32[256,512]{1,0:T(8,128)S(1)}, s32[256,512]{1,0:T(8,128)}, u32[]{:S(2)}) copy-start(s32[256,512]{1,0:T(8,128)} %param.5) | copy-start | bytes 1572868
  3.1 30.9 %all-to-all-start = ((bf16[32,2,16,256]{3,2,1,0:T(8,128)(2,1)}), bf16[32,2,16,256]{3,2,1,0:T(8,128)(2,1)S(1)}, u32[]{:S(2)}, u32[]{:S(2)}) async-start(bf16[32,2,16,256]{3,2,1,0:T(8,128)(2,1)} %filter_power.1), calls=%async_computation | async-start | bytes 1048576 | tf_op jit(solution)/shard_map/all_to_all | solution.py:319
  16.0 1.6 %collective-permute-start = (bf16[264,512]{1,0:T(8,128)(2,1)S(1)}, bf16[264,512]{1,0:T(8,128)(2,1)S(1)}, u32[]{:S(2)}, u32[]{:S(2)}) collective-permute-start(bf16[264,512]{1,0:T(8,128)(2,1)S(1)} %pad_maximum_fusion.1), channel_id=1, source_target_pairs={{0,8},{8,0},{16,24},{24,16},{32,40},{40,32},{48,56},{56,48},{64,72... | collective-permute-start | bytes 811016 | tf_op jit(solution)/shard_map/ppermute | solution.py:294
  39.1 5.2 %collective-permute-start.1 = (s16[272,256]{1,0:T(8,128)(2,1)S(1)}, s16[272,256]{1,0:T(8,128)(2,1)S(1)}, u32[]{:S(2)}, u32[]{:S(2)}) collective-permute-start(s16[272,256]{1,0:T(8,128)(2,1)S(1)} %get-tuple-element.32), channel_id=1, source_target_pairs={{0,16},{8,24},{16,0},{24,8},{32,48},{40,56},{48,32},{56,40},{64,80... | collective-permute-start | bytes 417800 | tf_op jit(solution)/shard_map/ppermute | solution.py:294
  45.2 6.1 %collective-permute-start.2 = (s16[272,256]{1,0:T(8,128)(2,1)S(1)}, s16[272,256]{1,0:T(8,128)(2,1)S(1)}, u32[]{:S(2)}, u32[]{:S(2)}) collective-permute-start(s16[272,256]{1,0:T(8,128)(2,1)S(1)} %get-tuple-element.37), channel_id=1, source_target_pairs={{0,48},{8,56},{16,32},{24,40},{32,16},{40,24},{48,0},{56,8},{64,11... | collective-permute-start | bytes 417800 | tf_op jit(solution)/shard_map/ppermute | solution.py:294
  52.3 9.5 %collective-permute-start.3 = (s16[272,256]{1,0:T(8,128)(2,1)S(1)}, s16[272,256]{1,0:T(8,128)(2,1)S(1)}, u32[]{:S(2)}, u32[]{:S(2)}) collective-permute-start(s16[272,256]{1,0:T(8,128)(2,1)S(1)} %get-tuple-element.42), channel_id=1, source_target_pairs={{0,64},{8,72},{16,80},{24,88},{32,96},{40,104},{48,112},{56,120},{... | collective-permute-start | bytes 417800 | tf_op jit(solution)/shard_map/ppermute | solution.py:294
  62.8 6.9 %collective-permute-start.4 = (s16[272,256]{1,0:T(8,128)(2,1)S(1)}, s16[272,256]{1,0:T(8,128)(2,1)S(1)}, u32[]{:S(2)}, u32[]{:S(2)}) collective-permute-start(s16[272,256]{1,0:T(8,128)(2,1)S(1)} %get-tuple-element.47), channel_id=1, source_target_pairs={{0,192},{8,200},{16,208},{24,216},{32,224},{40,232},{48,240},{56,2... | collective-permute-start | bytes 417800 | tf_op jit(solution)/shard_map/ppermute | solution.py:294
  70.9 2.6 %collective-permute-start.5 = (f32[8,256]{1,0:T(8,128)S(1)}, f32[8,256]{1,0:T(8,128)S(1)}, u32[]{:S(2)}, u32[]{:S(2)}) collective-permute-start(f32[8,256]{1,0:T(8,128)S(1)} %get-tuple-element.50), channel_id=1, source_target_pairs={{0,8},{8,0},{16,24},{24,16},{32,40},{40,32},{48,56},{56,48},{64,72... | collective-permute-start | bytes 24584 | tf_op jit(solution)/shard_map/ppermute | solution.py:294
  73.5 6.3 %collective-permute-start.6 = (f32[2,8,256]{2,1,0:T(8,128)S(1)}, f32[2,8,256]{2,1,0:T(8,128)S(1)}, u32[]{:S(2)}, u32[]{:S(2)}) collective-permute-start(f32[2,8,256]{2,1,0:T(8,128)S(1)} %join.1), channel_id=1, source_target_pairs={{0,80},{8,208},{16,72},{24,200},{32,88},{40,216},{48,64},{56,192},... | collective-permute-start | bytes 49160 | tf_op jit(solution)/shard_map/ppermute | solution.py:294

commit v8 on v7

--- a/solution.py
+++ b/solution.py
@@ -125,7 +125,7 @@
 
 def split_of(x):
     high = x.astype(bf16)
-    return jnp.concatenate([high, (x - high.astype(f32)).astype(bf16)], axis=1)
+    return jnp.concatenate([high, (x - high.astype(f32)).astype(bf16)], axis=0)
 
 
 def eye_mask(size):
@@ -139,13 +139,11 @@
     return columns.astype(jnp.int32)
 
 
-def take_rows(split, source):
-    trials = split.shape[0]
-    samples = split.shape[1] // 2
+def take_rows(split, weight, source):
+    trials = weight.shape[1]
     lane = lax.broadcasted_iota(jnp.int32, (trials, trials), 1)
-    onehot = jnp.where(lane == source, 1.0, 0.0).astype(bf16)
-    y = jnp.dot(onehot, split, preferred_element_type=f32)
-    return y[:, :samples] + y[:, samples:]
+    picked = jnp.where(lane == source, weight, 0.0).astype(bf16)
+    return jnp.dot(jnp.concatenate([picked, picked], axis=1), split, preferred_element_type=f32)
 
 
 def delay_rows(x, delay):
@@ -159,40 +157,52 @@
     return jnp.concatenate([jnp.where(inside, first, 0.0), jnp.where(inside, second, first)], axis=1)
 
 
-def merge_unit(split_ref, table, level):
+def table_row(level):
+    return 3 * (len(KEEPS) - 1 - level)
+
+
+def table_rows(level):
+    return -(-(3 * (len(KEEPS) - level) + 2) // 8) * 8
+
+
+def merge_unit(split_ref, weight_ref, table, level):
     columns = columns_of(table)
-    lower = take_rows(split_ref[0], columns[:, 3 * level : 3 * level + 1])
-    upper = take_rows(split_ref[1], columns[:, 3 * level + 1 : 3 * level + 2])
-    return lower + delay_rows(upper, columns[:, 3 * level + 2 : 3 * level + 3])
-
-
-STEPS = 65534.0
+    row = table_row(level)
+    lower = take_rows(split_ref[0], weight_ref[0], columns[:, row : row + 1])
+    upper = take_rows(split_ref[1], weight_ref[1], columns[:, row + 1 : row + 2])
+    return lower + delay_rows(upper, columns[:, row + 2 : row + 3])
+
+
+def scale_of(code):
+    return jnp.exp2(code * (1.0 / 256.0)).astype(bf16).astype(f32)
 
 
 def put_message(out_ref, x, table):
     trials = x.shape[0]
+    rows = out_ref.shape[0] - trials
     peak = jnp.maximum(jnp.max(x, axis=1, keepdims=True), 1e-30)
-    code = jnp.floor(jnp.log2(peak) * 256.0) + 2.0
-    scale = jnp.exp2(code * (-1.0 / 256.0)) * STEPS
-    out_ref[:trials] = ((x * scale + 0.5).astype(jnp.int32) - int(STEPS) // 2).astype(jnp.int16)
+    code = jnp.floor(jnp.log2(peak) * 256.0) + 3.0
+    out_ref[:trials] = ((x * (65536.0 / scale_of(code)) + 0.5).astype(jnp.int32) - 32768).astype(jnp.int16)
     code_row = jnp.sum(jnp.where(eye_mask(trials), code, 0.0), axis=0, keepdims=True).astype(jnp.int32)
+    table = table[:rows].astype(jnp.int32)
     row = lax.broadcasted_iota(jnp.int32, table.shape, 0)
-    rows = jnp.where(row == 0, code_row >> 8, jnp.where(row == 1, code_row & 255, table.astype(jnp.int32)))
-    out_ref[trials:] = rows.astype(jnp.int16)
+    filled = jnp.where(row == rows - 2, code_row >> 8, jnp.where(row == rows - 1, code_row & 255, table))
+    out_ref[trials:] = filled.astype(jnp.int16)
 
 
 def take_message(in_ref, trials):
     table = in_ref[trials:].astype(jnp.int32).astype(f32)
-    columns = columns_of(table)
-    code = (columns[:, 0:1] * 256 + columns[:, 1:2]).astype(f32)
-    scale = jnp.exp2(code * (1.0 / 256.0)) * (1.0 / STEPS)
-    x = (in_ref[:trials].astype(jnp.int32) + int(STEPS) // 2).astype(f32) * scale
-    return x, table
-
-
-def dedisperse_kernel(arrived_ref, tables_ref, sent_ref, split_ref, table_ref, stack_ref):
+    rows = table.shape[0]
+    weight = scale_of(table[rows - 2 : rows - 1] * 256.0 + table[rows - 1 :]) * (1.0 / 65536.0)
+    x = in_ref[:trials].astype(jnp.int32) + 32768
+    split = jnp.concatenate([(x & 0xFF00).astype(f32).astype(bf16), (x & 0xFF).astype(f32).astype(bf16)], axis=0)
+    return split, weight, table
+
+
+def dedisperse_kernel(arrived_ref, tables_ref, sent_ref, split_ref, weight_ref, table_ref, stack_ref):
     sources, _, upchan, samples = arrived_ref.shape
-    trials = split_ref.shape[1]
+    trials = weight_ref.shape[2]
+    weight_ref[...] = jnp.ones(weight_ref.shape, f32)
     channels = sources * upchan
     for unit in range(2):
         x = arrived_ref[:, unit].reshape(channels, samples).astype(f32)
@@ -215,31 +225,34 @@
         split_ref[unit] = split_of(total)
         packed = tables_ref[unit, trials:].astype(f32)
         table_ref[unit] = jnp.concatenate([packed[:, :samples], packed[:, samples:]], axis=0)
-    put_sent(0, split_ref, table_ref, sent_ref)
-
-
-def put_sent(level, split_ref, table_ref, sent_ref):
+    put_sent(0, split_ref, weight_ref, table_ref, sent_ref)
+
+
+def put_sent(level, split_ref, weight_ref, table_ref, sent_ref):
     table = table_ref[1 - KEEPS[level](here())]
-    put_message(sent_ref, merge_unit(split_ref, table, level), table)
-
-
-def kept_kernel(level, split_in_ref, table_in_ref, split_ref, table_ref):
+    put_message(sent_ref, merge_unit(split_ref, weight_ref, table, level), table)
+
+
+def kept_kernel(level, split_in_ref, weight_in_ref, table_in_ref, split_ref, table_ref):
     table = table_in_ref[KEEPS[level](here())]
-    split_ref[...] = split_of(merge_unit(split_in_ref, table, level))
-    table_ref[...] = table
-
-
-def load_units(own, kept_split_ref, kept_table_ref, received_ref, split_ref, table_ref):
+    split_ref[...] = split_of(merge_unit(split_in_ref, weight_in_ref, table, level))
+    table_ref[...] = table[: table_ref.shape[0]]
+
+
+def load_units(own, kept_split_ref, kept_table_ref, received_ref, split_ref, weight_ref, table_ref):
     split_ref[own] = kept_split_ref[...]
+    weight_ref[own] = jnp.ones(weight_ref.shape[1:], f32)
     table_ref[own] = kept_table_ref[...]
-    x, table = take_message(received_ref, kept_split_ref.shape[0])
-    split_ref[1 - own] = split_of(x)
+    split, weight, table = take_message(received_ref, weight_ref.shape[2])
+    split_ref[1 - own] = split
+    weight_ref[1 - own] = weight
     table_ref[1 - own] = table
 
 
-def sent_kernel(level, kept_split_ref, kept_table_ref, received_ref, sent_ref, split_ref, table_ref):
-    load_units(bit(here(), level), kept_split_ref, kept_table_ref, received_ref, split_ref, table_ref)
-    put_sent(level, split_ref, table_ref, sent_ref)
+def sent_kernel(level, kept_split_ref, kept_table_ref, received_ref, sent_ref, split_ref, weight_ref, table_ref):
+    own = bit(here(), level)
+    load_units(own, kept_split_ref, kept_table_ref, received_ref, split_ref, weight_ref, table_ref)
+    put_sent(level, split_ref, weight_ref, table_ref, sent_ref)
 
 
 def unit_peaks(merged):
@@ -259,13 +272,14 @@
     return jnp.concatenate(peaks, axis=0)
 
 
-def sent_peaks_kernel(level, kept_split_ref, kept_table_ref, received_ref, peaks_ref, split_ref, table_ref):
-    load_units(bit(here(), level), kept_split_ref, kept_table_ref, received_ref, split_ref, table_ref)
-    peaks_ref[...] = unit_peaks(merge_unit(split_ref, table_ref[1 - KEEPS[level](here())], level))
-
-
-def kept_peaks_kernel(level, split_ref, table_ref, peaks_ref):
-    peaks_ref[...] = unit_peaks(merge_unit(split_ref, table_ref[KEEPS[level](here())], level))
+def sent_peaks_kernel(level, kept_split_ref, kept_table_ref, received_ref, peaks_ref, split_ref, weight_ref, table_ref):
+    own = bit(here(), level)
+    load_units(own, kept_split_ref, kept_table_ref, received_ref, split_ref, weight_ref, table_ref)
+    peaks_ref[...] = unit_peaks(merge_unit(split_ref, weight_ref, table_ref[1 - KEEPS[level](here())], level))
+
+
+def kept_peaks_kernel(level, split_ref, weight_ref, table_ref, peaks_ref):
+    peaks_ref[...] = unit_peaks(merge_unit(split_ref, weight_ref, table_ref[KEEPS[level](here())], level))
 
 
 def join_kernel(kept_ref, received_ref, out_ref):
@@ -318,33 +332,32 @@
     power = filter_power(voltages)
     arrived = lax.all_to_all(power, "freq", split_axis=0, concat_axis=0, tiled=True)
 
-    rows = -(-3 * levels // 16) * 16
-    table = jnp.pad(merge_tables.reshape(3 * levels, trials), ((0, rows - 3 * levels), (0, 0)))
+    rows = table_rows(0) // 16 * 16
+    table = jnp.pad(merge_tables[::-1].reshape(3 * levels, trials), ((0, rows - 3 * levels), (0, 0)))
     table = table.reshape(2, rows // 2, trials).transpose(1, 0, 2).reshape(rows // 2, 2 * trials)
     first, second = gather_units(jnp.concatenate([sub_delays, table], axis=0).astype(bf16))
     swapped = bit(here(), BEAM_BIT) == 1
     tables = jnp.stack([jnp.where(swapped, second, first), jnp.where(swapped, first, second)])
 
-    message = ((trials + rows, samples), jnp.int16)
-    splits, both_tables = ((2, trials, 2 * samples), bf16), ((2, rows, samples), f32)
-    split, table = ((trials, 2 * samples), bf16), ((rows, samples), f32)
+    def message(level):
+        return (trials + table_rows(level), samples), jnp.int16
+
+    def both_units(rows):
+        return ((2, 2 * trials, samples), bf16), ((2, 1, trials), f32), ((2, rows, samples), f32)
+
     stack = pltpu.VMEM((INNER * channels, samples), bf16)
-    sent, *both = call(
-        dedisperse_kernel, "dedisperse", (message, splits, both_tables), (arrived, tables), [stack], 24
-    )
-    for level in range(levels - 1):
-        received = swap(sent, PARTNERS[level])
-        kept = call(functools.partial(kept_kernel, level), "kept", (split, table), tuple(both))
-        if level < levels - 2:
-            sent, *both = call(
-                functools.partial(sent_kernel, level + 1), "sent", (message, splits, both_tables), (*kept, received)
-            )
-    peak = ((WIDTHS, trials), f32)
-    sent, *both = call(
-        functools.partial(sent_peaks_kernel, levels - 1), "sent_peaks", (peak, splits, both_tables), (*kept, received)
-    )
+    sent, *both = call(dedisperse_kernel, "dedisperse", (message(1), *both_units(rows)), (arrived, tables), [stack], 24)
+    for level in range(1, levels):
+        rows = table_rows(level)
+        received = swap(sent, PARTNERS[level - 1])
+        units = ((2 * trials, samples), bf16), ((rows, samples), f32)
+        kept = call(functools.partial(kept_kernel, level - 1), "kept", units, tuple(both))
+        last = level == levels - 1
+        kernel, name = (sent_peaks_kernel, "sent_peaks") if last else (sent_kernel, "sent")
+        out = ((WIDTHS, trials), f32) if last else message(level + 1)
+        sent, *both = call(functools.partial(kernel, level), name, (out, *both_units(rows)), (*kept, received))
     received = swap(sent, 1 << BEAM_BIT)
-    kept = call(functools.partial(kept_peaks_kernel, levels - 1), "kept_peaks", (peak,), tuple(both))
+    kept = call(functools.partial(kept_peaks_kernel, levels - 1), "kept_peaks", (out,), tuple(both))
     peaks = call(join_kernel, "join", (((2, WIDTHS, trials), f32),), (*kept, received))[0]
     return move(peaks, home)
 

time: 81.1 us -> 80.1 us (0.988)
  no operation moved by 1% of the time
where the time goes in v8:
time: 80.1 us; the launch traced here: 79.4 us
  waiting for transfers between devices  45.2 us (56%)
  starting transfers between devices  18 us (22%)
  Pallas kernels  15.1 us (19%)
    ppermute x7, waiting for transfers between devices, move(): lax.ppermute(x, 'freq', pairs)  29 us
    all_to_all x1, waiting for transfers between devices, local(): lax.all_to_all(power, 'freq', split_axis=0, concat_axis=0, tiled=True)  16.2 us
    all_to_all x1, starting transfers between devices, local(): lax.all_to_all(power, 'freq', split_axis=0, concat_axis=0, tiled=True)  12.7 us
    pallas_call x11, Pallas kernels, call(): pl.pallas_call(kernel, out_shape=tuple((jax.ShapeDtypeStruct(shape, dtype...  12.1 us
    ppermute x7, starting transfers between devices, move(): lax.ppermute(x, 'freq', pairs)  5.3 us
    pallas_call x1, Pallas kernels, filter_power(): pl.pallas_call(filter_kernel, out_shape=jax.ShapeDtypeStruct((coarse // 2...  3.07 us
  transfers between devices with their start and end apart: 8, of which 7 were waited for; matrix products, arithmetic and copies ran while one was open for 0% of the time, Pallas kernels for 4%

profile of v8, /device:TPU:1, one launch (start us, length us, event | category | flops | bytes accessed | tf_op | source)
XLA Modules:
  0.0 79.4 jit_solution(14637693785348002850)
XLA Ops:
  0.0 3.1 %filter_power.1 = bf16[32,2,16,256]{3,2,1,0:T(8,128)(2,1)} custom-call(bf16[64,128]{1,0:T(8,128)(2,1)} %constant.14.clone.matrix_hbm, bf16[2,2,32,16,256]{4,3,2,1,0:T(8,128)(2,1)} %volts_hbm.1), custom_call_target="tpu_custom_call" | custom-call | tf_op jit(solution)/shard_map/filter_power/pallas_call | solution.py:110
  3.1 0.0 copy-start.1
  3.1 0.0 copy-start
  3.1 12.7 %all-to-all-start = ((bf16[32,2,16,256]{3,2,1,0:T(8,128)(2,1)}), bf16[32,2,16,256]{3,2,1,0:T(8,128)(2,1)S(1)}, u32[]{:S(2)}, u32[]{:S(2)}) async-start(bf16[32,2,16,256]{3,2,1,0:T(8,128)(2,1)} %filter_power.1), calls=%async_computation | async-start | bytes 1048576 | tf_op jit(solution)/shard_map/all_to_all | solution.py:333
  16.0 0.3 collective-permute-start
  16.3 1.3 %collective-permute-done = bf16[264,512]{1,0:T(8,128)(2,1)S(1)} collective-permute-done((bf16[264,512]{1,0:T(8,128)(2,1)S(1)}, bf16[264,512]{1,0:T(8,128)(2,1)S(1)}, u32[]{:S(2)}, u32[]{:S(2)}) %collective-permute-start) | collective-permute-done | bytes 270368 | tf_op jit(solution)/shard_map/ppermute | solution.py:308
  17.6 0.1 select_bitcast_fusion.1
  17.7 0.1 pad_maximum_fusion.tables_ref
  17.8 16.2 %all-to-all-done.arrived_ref = bf16[32,2,16,256]{3,2,1,0:T(8,128)(2,1)S(1)} async-done(((bf16[32,2,16,256]{3,2,1,0:T(8,128)(2,1)}), bf16[32,2,16,256]{3,2,1,0:T(8,128)(2,1)S(1)}, u32[]{:S(2)}, u32[]{:S(2)}) %all-to-all-start) | async-done | bytes 524320 | tf_op jit(solution)/shard_map/all_to_all | solution.py:333
  34.0 5.1 %dedisperse.1 = (s16[272,256]{1,0:T(8,128)(2,1)S(1)}, bf16[2,512,256]{2,1,0:T(8,128)(2,1)S(1)}, f32[2,1,256]{2,1,0:T(1,128)S(1)}, f32[2,16,256]{2,1,0:T(8,128)S(1)}) custom-call(bf16[32,2,16,256]{3,2,1,0:T(8,128)(2,1)S(1)} %all-to-all-done.arrived_ref, bf16[2,264,512]{2,1,0:T(8,128)(2,1)S(1)} %pad_maximum_fusion.tables_ref), custom_call_target="tpu_custom_call" | custom-call | tf_op jit(solution)/shard_map/dedisperse/pallas_call | solution.py:295
  39.1 0.1 collective-permute-start.1
  39.2 0.6 kept.4
  39.9 4.4 %collective-permute-done.1.received_ref = s16[272,256]{1,0:T(8,128)(2,1)S(1)} collective-permute-done((s16[272,256]{1,0:T(8,128)(2,1)S(1)}, s16[272,256]{1,0:T(8,128)(2,1)S(1)}, u32[]{:S(2)}, u32[]{:S(2)}) %collective-permute-start.1) | collective-permute-done | bytes 139296 | tf_op jit(solution)/shard_map/ppermute | solution.py:308
  44.3 0.8 sent.3
  45.1 1.3 %collective-permute-start.2 = (s16[272,256]{1,0:T(8,128)(2,1)S(1)}, s16[272,256]{1,0:T(8,128)(2,1)S(1)}, u32[]{:S(2)}, u32[]{:S(2)}) collective-permute-start(s16[272,256]{1,0:T(8,128)(2,1)S(1)} %get-tuple-element.44), channel_id=1, source_target_pairs={{0,48},{8,56},{16,32},{24,40},{32,16},{40,24},{48,0},{56,8},{64,11... | collective-permute-start | bytes 417800 | tf_op jit(solution)/shard_map/ppermute | solution.py:308
  46.3 0.6 kept.5
  47.0 4.2 %collective-permute-done.2.received_ref = s16[272,256]{1,0:T(8,128)(2,1)S(1)} collective-permute-done((s16[272,256]{1,0:T(8,128)(2,1)S(1)}, s16[272,256]{1,0:T(8,128)(2,1)S(1)}, u32[]{:S(2)}, u32[]{:S(2)}) %collective-permute-start.2) | collective-permute-done | bytes 139296 | tf_op jit(solution)/shard_map/ppermute | solution.py:308
  51.2 0.8 sent.4
  52.0 0.6 collective-permute-start.3
  52.6 0.6 kept.6
  53.3 8.0 %collective-permute-done.3.received_ref = s16[264,256]{1,0:T(8,128)(2,1)S(1)} collective-permute-done((s16[264,256]{1,0:T(8,128)(2,1)S(1)}, s16[264,256]{1,0:T(8,128)(2,1)S(1)}, u32[]{:S(2)}, u32[]{:S(2)}) %collective-permute-start.3) | collective-permute-done | bytes 135200 | tf_op jit(solution)/shard_map/ppermute | solution.py:308
  61.3 0.8 sent.5
  62.1 0.1 collective-permute-start.4
  62.2 0.6 kept.7
  62.9 6.0 %collective-permute-done.4.received_ref = s16[264,256]{1,0:T(8,128)(2,1)S(1)} collective-permute-done((s16[264,256]{1,0:T(8,128)(2,1)S(1)}, s16[264,256]{1,0:T(8,128)(2,1)S(1)}, u32[]{:S(2)}, u32[]{:S(2)}) %collective-permute-start.4) | collective-permute-done | bytes 135200 | tf_op jit(solution)/shard_map/ppermute | solution.py:308
  68.8 1.0 %sent_peaks.1 = (f32[8,256]{1,0:T(8,128)S(1)}, bf16[2,512,256]{2,1,0:T(8,128)(2,1)S(1)}, f32[2,1,256]{2,1,0:T(1,128)S(1)}, f32[2,8,256]{2,1,0:T(8,128)S(1)}) custom-call(bf16[512,256]{1,0:T(8,128)(2,1)S(1)} %get-tuple-element.54.kept_split_ref, f32[8,256]{1,0:T(8,128)S(1)} %get-tuple-element.55.kept_table_ref, ...), custom_call_target="tpu_custom_call" | custom-call | tf_op jit(solution)/shard_map/sent_peaks/pallas_call | solution.py:295
  69.9 1.7 %collective-permute-start.5 = (f32[8,256]{1,0:T(8,128)S(1)}, f32[8,256]{1,0:T(8,128)S(1)}, u32[]{:S(2)}, u32[]{:S(2)}) collective-permute-start(f32[8,256]{1,0:T(8,128)S(1)} %get-tuple-element.60), channel_id=1, source_target_pairs={{0,8},{8,0},{16,24},{24,16},{32,40},{40,32},{48,56},{56,48},{64,72... | collective-permute-start | bytes 24584 | tf_op jit(solution)/shard_map/ppermute | solution.py:308
  71.5 1.0 %kept_peaks.1.kept_ref = f32[8,256]{1,0:T(8,128)S(1)} custom-call(bf16[2,512,256]{2,1,0:T(8,128)(2,1)S(1)} %get-tuple-element.57.split_ref, f32[2,1,256]{2,1,0:T(1,128)S(1)} %get-tuple-element.58.weight_ref, f32[2,8,256]{2,1,0:T(8,128)S(1)} %get-tuple-element.59.table_ref), custom_call_target="tpu_custom_call" | custom-call | tf_op jit(solution)/shard_map/kept_peaks/pallas_call | solution.py:295
  72.5 0.0 collective-permute-done.5.received_ref
  72.6 1.2 %collective-permute-start.6 = (f32[2,8,256]{2,1,0:T(8,128)S(1)}, f32[2,8,256]{2,1,0:T(8,128)S(1)}, u32[]{:S(2)}, u32[]{:S(2)}) collective-permute-start(f32[2,8,256]{2,1,0:T(8,128)S(1)} %join.1), channel_id=1, source_target_pairs={{0,80},{8,208},{16,72},{24,200},{32,88},{40,216},{48,64},{56,192},... | collective-permute-start | bytes 49160 | tf_op jit(solution)/shard_map/ppermute | solution.py:308
  73.8 5.0 %collective-permute-done.6 = f32[2,8,256]{2,1,0:T(8,128)S(1)} collective-permute-done((f32[2,8,256]{2,1,0:T(8,128)S(1)}, f32[2,8,256]{2,1,0:T(8,128)S(1)}, u32[]{:S(2)}, u32[]{:S(2)}) %collective-permute-start.6) | collective-permute-done | bytes 16416 | tf_op jit(solution)/shard_map/ppermute | solution.py:308
  78.8 0.6 copy.6
  (8 shorter events, 0.1 us)
Async XLA Ops:
  3.1 12.8 %copy-start.1 = (s32[5,3,256]{2,1,0:T(4,128)S(1)}, s32[5,3,256]{2,1,0:T(4,128)}, u32[]{:S(2)}) copy-start(s32[5,3,256]{2,1,0:T(4,128)} %param.6) | copy-start | bytes 46084
  3.1 12.8 %copy-start = (s32[256,512]{1,0:T(8,128)S(1)}, s32[256,512]{1,0:T(8,128)}, u32[]{:S(2)}) copy-start(s32[256,512]{1,0:T(8,128)} %param.5) | copy-start | bytes 1572868
  3.1 30.9 %all-to-all-start = ((bf16[32,2,16,256]{3,2,1,0:T(8,128)(2,1)}), bf16[32,2,16,256]{3,2,1,0:T(8,128)(2,1)S(1)}, u32[]{:S(2)}, u32[]{:S(2)}) async-start(bf16[32,2,16,256]{3,2,1,0:T(8,128)(2,1)} %filter_power.1), calls=%async_computation | async-start | bytes 1048576 | tf_op jit(solution)/shard_map/all_to_all | solution.py:333
  16.0 1.6 %collective-permute-start = (bf16[264,512]{1,0:T(8,128)(2,1)S(1)}, bf16[264,512]{1,0:T(8,128)(2,1)S(1)}, u32[]{:S(2)}, u32[]{:S(2)}) collective-permute-start(bf16[264,512]{1,0:T(8,128)(2,1)S(1)} %pad_maximum_fusion.1), channel_id=1, source_target_pairs={{0,8},{8,0},{16,24},{24,16},{32,40},{40,32},{48,56},{56,48},{64,72... | collective-permute-start | bytes 811016 | tf_op jit(solution)/shard_map/ppermute | solution.py:308
  39.1 5.2 %collective-permute-start.1 = (s16[272,256]{1,0:T(8,128)(2,1)S(1)}, s16[272,256]{1,0:T(8,128)(2,1)S(1)}, u32[]{:S(2)}, u32[]{:S(2)}) collective-permute-start(s16[272,256]{1,0:T(8,128)(2,1)S(1)} %get-tuple-element.38), channel_id=1, source_target_pairs={{0,16},{8,24},{16,0},{24,8},{32,48},{40,56},{48,32},{56,40},{64,80... | collective-permute-start | bytes 417800 | tf_op jit(solution)/shard_map/ppermute | solution.py:308
  45.1 6.1 %collective-permute-start.2 = (s16[272,256]{1,0:T(8,128)(2,1)S(1)}, s16[272,256]{1,0:T(8,128)(2,1)S(1)}, u32[]{:S(2)}, u32[]{:S(2)}) collective-permute-start(s16[272,256]{1,0:T(8,128)(2,1)S(1)} %get-tuple-element.44), channel_id=1, source_target_pairs={{0,48},{8,56},{16,32},{24,40},{32,16},{40,24},{48,0},{56,8},{64,11... | collective-permute-start | bytes 417800 | tf_op jit(solution)/shard_map/ppermute | solution.py:308
  52.0 9.3 %collective-permute-start.3 = (s16[264,256]{1,0:T(8,128)(2,1)S(1)}, s16[264,256]{1,0:T(8,128)(2,1)S(1)}, u32[]{:S(2)}, u32[]{:S(2)}) collective-permute-start(s16[264,256]{1,0:T(8,128)(2,1)S(1)} %get-tuple-element.50), channel_id=1, source_target_pairs={{0,64},{8,72},{16,80},{24,88},{32,96},{40,104},{48,112},{56,120},{... | collective-permute-start | bytes 405512 | tf_op jit(solution)/shard_map/ppermute | solution.py:308
  62.1 6.7 %collective-permute-start.4 = (s16[264,256]{1,0:T(8,128)(2,1)S(1)}, s16[264,256]{1,0:T(8,128)(2,1)S(1)}, u32[]{:S(2)}, u32[]{:S(2)}) collective-permute-start(s16[264,256]{1,0:T(8,128)(2,1)S(1)} %get-tuple-element.56), channel_id=1, source_target_pairs={{0,192},{8,200},{16,208},{24,216},{32,224},{40,232},{48,240},{56,2... | collective-permute-start | bytes 405512 | tf_op jit(solution)/shard_map/ppermute | solution.py:308
  69.9 2.7 %collective-permute-start.5 = (f32[8,256]{1,0:T(8,128)S(1)}, f32[8,256]{1,0:T(8,128)S(1)}, u32[]{:S(2)}, u32[]{:S(2)}) collective-permute-start(f32[8,256]{1,0:T(8,128)S(1)} %get-tuple-element.60), channel_id=1, source_target_pairs={{0,8},{8,0},{16,24},{24,16},{32,40},{40,32},{48,56},{56,48},{64,72... | collective-permute-start | bytes 24584 | tf_op jit(solution)/shard_map/ppermute | solution.py:308
  72.6 6.3 %collective-permute-start.6 = (f32[2,8,256]{2,1,0:T(8,128)S(1)}, f32[2,8,256]{2,1,0:T(8,128)S(1)}, u32[]{:S(2)}, u32[]{:S(2)}) collective-permute-start(f32[2,8,256]{2,1,0:T(8,128)S(1)} %join.1), channel_id=1, source_target_pairs={{0,80},{8,208},{16,72},{24,200},{32,88},{40,216},{48,64},{56,192},... | collective-permute-start | bytes 49160 | tf_op jit(solution)/shard_map/ppermute | solution.py:308
